TPU v7x, 32 devices: a whole 2x2x4 slice. The times are simulated.
32 devices in a mesh: region: 8 (over z, y), survey: 4 (over x, core).
Axes of the slice: x: 2, y: 2, z: 4, core: 2. Of those that a mesh axis runs over, the one named last changes fastest.
Arguments:
- sensitivity: bfloat16 [128, 512, 4096], P(('region', 'survey')), may hold values from -0.09375 to 0.09375
- observed: float32 [128, 8, 512], P(('region', 'survey')), may hold values from -6 to 6
- data_weight: float32 [128, 512], P(('region', 'survey')), may hold values from 0.5 to 2
- data_counts: int32 [128], P(('region', 'survey')), may hold values from 128 to 512
- tile_bricks: int32 [128, 32], P(('region', 'survey')), may hold values from 0 to 16383, as said below
- start_model: float32 [128, 128, 8, 128], P('region', 'survey'), may hold values from -6 to 6
- active_cells: int32 [128, 128, 128], P('region', 'survey'), may hold values from 0 to 1
- face_links: int32 [128, 128, 128], P('region', 'survey'), may hold values from 0 to 63
- reg_weight: float32 [8], replicated, may hold values from 0.3 to 3
Outputs:
- final_model: float32 [128, 128, 8, 128], P('region', 'survey')
- misfit: float32 [128, 8, 512], P(('region', 'survey'))
Inputs may be any that keep to these rules, and one draw needn't show every extreme that they name: `tile_bricks`: brick b lies on owning device b // 512 (region index times 4 plus survey index), at its slab's layer (b % 512) // 32 and row b % 32. The 128 entries of one device's tiles name bricks of at most 8 per owning device; one owning device, the same for all, is named exactly 8 times by every device's tiles. Entries may repeat.
All inputs are finite; a program needn't handle non-finite values.
Results may differ from a plain program's by a relative error of at most 0.0031.
Values may be sent and summed in bfloat16 or wider, within the bound.
No kernel may reach another device: no remote copies, remote signals or barrier semaphores. Data moves between devices by JAX's collectives and lax.ppermute only.
A program may use at most 128 MiB of HBM per device.

v0:
```python
import jax
import jax.numpy as jnp
from jax import lax
from jax.sharding import PartitionSpec as P

ITERS = 2


EPS_SQ = 0.09


def with_halo(shard, sides, width):
    for axis, dim in sides:
        count, length = (lax.axis_size(axis), shard.shape[dim])
        up = [(i, (i + 1) % count) for i in range(count - 1)]
        down = [(j, i) for i, j in up]
        last = lax.slice_in_dim(shard, length - width, length, axis=dim)
        first = lax.slice_in_dim(shard, 0, width, axis=dim)
        before = lax.ppermute(last, axis, up)
        after = lax.ppermute(first, axis, down)
        shard = jnp.concatenate([before, shard, after], axis=dim)
    return shard


def stencil_list(padded):
    centre = padded[1:-1, 1:-1]
    zero_rim = jnp.zeros_like(centre[..., :1])
    neighbours = [
        padded[:-2, 1:-1],
        padded[2:, 1:-1],
        padded[1:-1, :-2],
        padded[1:-1, 2:],
        jnp.concatenate([zero_rim, centre[..., :-1]], axis=3),
        jnp.concatenate([centre[..., 1:], zero_rim], axis=3),
    ]
    return (centre, neighbours)


def irls_weights(centre, neighbours, link_bits, depth_index, active, depth_count):
    smallness = (
        active * (1.0 + 2.0 * depth_index / depth_count) / jnp.sqrt(centre * centre + EPS_SQ)
    )
    offsets = [-1.0, 1.0, 0.0, 0.0, 0.0, 0.0]
    face_weights = []
    for number in range(6):
        depth_level = 1.0 + (2.0 * depth_index + offsets[number]) / depth_count
        difference = centre - neighbours[number]
        face_weights.append(
            link_bits[number] * depth_level / jnp.sqrt(difference * difference + EPS_SQ)
        )
    return (smallness, face_weights)


def reg_gradient(centre, neighbours, smallness, face_weights):
    running = smallness * centre
    for number in range(6):
        running = running + face_weights[number] * (centre - neighbours[number])
    return running


def reg_curvature(centre, neighbours, smallness, face_weights):
    running = smallness * centre * centre
    for number in range(6):
        difference = centre - neighbours[number]
        running = running + 0.5 * face_weights[number] * difference * difference
    return jnp.sum(running, axis=(0, 1, 3))


def widen(field):
    return with_halo(field, (("region", 0), ("survey", 1)), 1)


def fetch_bricks(field_low, asked_ids, slot_of):
    layers, strip_rows, samples, cells_x = field_low.shape
    brick_store = field_low.reshape(layers * strip_rows, samples, cells_x)
    replies = brick_store[asked_ids]
    arrived = lax.all_to_all(replies, ("region", "survey"), split_axis=0, concat_axis=0, tiled=True)
    return arrived.reshape(-1, samples, cells_x)[slot_of]


def return_grads(products, slot_of, asked_ids, layers, strip_rows):
    owners, capacity = asked_ids.shape
    samples, cells_x = (products.shape[1], products.shape[2])
    buffer = jnp.zeros((owners * capacity, samples, cells_x), jnp.float32).at[slot_of].set(products)
    buffer = buffer.reshape(owners, capacity, samples, cells_x)
    arrived = lax.all_to_all(buffer, ("region", "survey"), split_axis=0, concat_axis=0, tiled=True)
    summed = jnp.zeros((layers * strip_rows, samples, cells_x), jnp.float32)
    summed = summed.at[asked_ids.reshape(-1)].add(arrived.reshape(-1, samples, cells_x))
    return summed.reshape(layers, strip_rows, samples, cells_x)


def predict(sensor_view, bricks, tiles, tile_width):
    picked = bricks.reshape(tiles, tile_width, bricks.shape[1], bricks.shape[2])
    return jnp.einsum("tdbx,tbsx->tsd", sensor_view, picked, preferred_element_type=jnp.float32)


def shards(
    sensitivity,
    observed,
    data_weight,
    data_counts,
    tile_bricks,
    start_model,
    active_cells,
    face_links,
    reg_weight,
):
    layers, strip_rows, samples, cells_x = start_model.shape
    tiles, tile_width = tile_bricks.shape
    data_slots = sensitivity.shape[1]
    owners = lax.axis_size("region") * lax.axis_size("survey")
    per_owner = layers * strip_rows
    capacity = max(2, 2 * tiles * tile_width // owners)
    depth_count = layers * lax.axis_size("region")
    sensor_view = sensitivity.reshape(tiles, data_slots, tile_width, cells_x)
    requests = tile_bricks.reshape(-1)
    owner_of = requests // per_owner
    local_of = requests % per_owner
    owner_hits = (owner_of[:, None] == jnp.arange(owners, dtype=jnp.int32)[None, :]).astype(
        jnp.int32
    )
    before = jnp.cumsum(owner_hits, axis=0) - owner_hits
    rank_of = jnp.sum(before * owner_hits, axis=1)
    slot_of = owner_of * capacity + rank_of
    slot_hits = slot_of[:, None] == jnp.arange(owners * capacity, dtype=jnp.int32)[None, :]
    asking = jnp.sum(jnp.where(slot_hits, local_of[:, None], 0), axis=0).reshape(owners, capacity)
    asked_ids = lax.all_to_all(
        asking, ("region", "survey"), split_axis=0, concat_axis=0, tiled=True
    )
    active = active_cells.astype(jnp.float32)[:, :, None, :]
    link_bits = [
        (face_links // 2**number % 2).astype(jnp.float32)[:, :, None, :] for number in range(6)
    ]
    depth_index = (
        (lax.axis_index("region") * layers + jnp.arange(layers, dtype=jnp.int32))
        .astype(jnp.float32)
        .reshape(layers, 1, 1, 1)
    )
    row_mask = (
        jnp.arange(data_slots, dtype=jnp.int32)[None, None, :] < data_counts[:, None, None]
    ).astype(jnp.float32)
    weight_sq = row_mask * (data_weight * data_weight)[:, None, :]
    reg_scale = reg_weight[None, None, :, None]
    model_now = start_model * active
    predicted = predict(
        sensor_view,
        fetch_bricks(model_now.astype(jnp.bfloat16), asked_ids, slot_of),
        tiles,
        tile_width,
    )
    model_wide = widen(model_now)
    for iteration in range(ITERS):
        weighted = (weight_sq * (predicted - observed)).astype(jnp.bfloat16)
        products = jnp.einsum(
            "tsd,tdbx->tbsx", weighted, sensor_view, preferred_element_type=jnp.float32
        )
        data_grad = return_grads(
            products.reshape(-1, samples, cells_x), slot_of, asked_ids, layers, strip_rows
        )
        centre, neighbours = stencil_list(model_wide)
        smallness, face_weights = irls_weights(
            centre, neighbours, link_bits, depth_index, active, depth_count
        )
        gradient = active * data_grad + reg_scale * reg_gradient(
            centre, neighbours, smallness, face_weights
        )
        step_pred = predict(
            sensor_view,
            fetch_bricks(gradient.astype(jnp.bfloat16), asked_ids, slot_of),
            tiles,
            tile_width,
        )
        grad_wide = widen(gradient)
        grad_centre, grad_neighbours = stencil_list(grad_wide)
        reg_curv = reg_curvature(grad_centre, grad_neighbours, smallness, face_weights)
        grad_norm = jnp.sum(gradient * gradient, axis=(0, 1, 3))
        data_curv = jnp.sum(weight_sq * step_pred * step_pred, axis=(0, 2))
        grad_norm, data_curv, reg_curv = lax.psum(
            (grad_norm, data_curv, reg_curv), ("region", "survey")
        )
        step_length = grad_norm / (data_curv + reg_weight * reg_curv)
        model_now = model_now - step_length[None, None, :, None] * gradient
        model_wide = model_wide - step_length[None, None, :, None] * grad_wide
        predicted = predicted - step_length[None, :, None] * step_pred
    misfit = row_mask * data_weight[:, None, :] * (predicted - observed)
    return (model_now, misfit)


def solution(mesh):
    return jax.shard_map(
        shards,
        mesh=mesh,
        in_specs=(
            P(("region", "survey"), None, None),
            P(("region", "survey"), None, None),
            P(("region", "survey"), None),
            P(("region", "survey")),
            P(("region", "survey"), None),
            P("region", "survey", None, None),
            P("region", "survey", None),
            P("region", "survey", None),
            P(),
        ),
        out_specs=(P("region", "survey", None, None), P(("region", "survey"), None, None)),
        check_vma=False,
    )
```

profile of v0, /device:TPU:0, one launch (start us, length us, event | category | flops | bytes accessed | tf_op | source)
XLA Modules:
  0.0 419.1 jit_solution(4119584449608338521)
XLA Ops:
  2.7 7.3 %all-to-all-start = ((s32[32,1,8]{2,1,0:T(1,128)}), s32[32,1,8]{2,1,0:T(1,128)S(1)}, u32[]{:S(2)}, u32[]{:S(2)}) async-start(s32[32,1,8]{2,1,0:T(1,128)} %bitcast), calls=%async_computation | async-start | bytes 32768 | tf_op jit(solution)/shard_map/all_to_all | solution.py:127
  11.7 2.0 fusion.88
  13.8 3.4 all-to-all-done
  19.4 2.6 all-to-all-start.1
  22.8 14.8 %all-to-all-done.1 = bf16[32,8,8,128]{3,2,1,0:T(8,128)(2,1)S(1)} async-done(((bf16[32,8,8,128]{3,2,1,0:T(8,128)(2,1)}), bf16[32,8,8,128]{3,2,1,0:T(8,128)(2,1)S(1)}, u32[]{:S(2)}, u32[]{:S(2)}) %all-to-all-start.1) | async-done | bytes 524320 | tf_op jit(solution)/shard_map/all_to_all | solution.py:77
  38.3 8.1 %fusion.41 = f32[4,8,512]{2,1,0:T(8,128)S(1)} fusion(bf16[4,32,8,128]{3,2,1,0:T(8,128)(2,1)S(1)} %bitcast.109, bf16[4,512,4096]{2,1,0:T(8,128)(2,1)} %param.9), kind=kOutput, calls=%fused_computation.118 | convolution fusion | flops 134217728 | bytes 17104896 | tf_op jit(solution)/shard_map/tdbx,tbsx->tsd/dot_general | solution.py:94
  46.4 7.0 %fusion.6 = f32[4,8,32,128]{3,1,2,0:T(8,128)S(1)} fusion(f32[4,8,512]{2,1,0:T(8,128)S(1)} %fusion.41, f32[4,8,512]{2,1,0:T(8,128)S(1)} %copy-done.15, f32[4,512]{1,0:T(4,128)S(1)} %get-tuple-element.41, bf16[4,512,4096]{2,1,0:T(8,128)(2,1)} %param.9), kind=kOutput, calls=%fused_computation.16 | convolution fusion | flops 134266880 | bytes 17440768 | tf_op jit(solution)/shard_map/tsd,tdbx->tbsx/dot_general | solution.py:154
  54.5 12.4 %scatter_fusion = f32[256,8,128]{2,1,0:T(8,128)} fusion(f32[256,8,128]{2,1,0:T(8,128)} %broadcast.388.clone, s32[128]{0:T(128)S(1)} %fusion.86, f32[128,8,128]{2,1,0:T(8,128)S(1)} %bitcast.102), kind=kCustom, calls=%fused_computation.6 | custom fusion | bytes 1573376 | tf_op jit(solution)/shard_map/scatter | solution.py:84
  66.8 3.4 all-to-all-start.2
  71.0 3.5 collective-permute-start
  75.8 2.7 fusion.94
  78.5 2.0 fusion.58
  83.2 1.9 collective-permute-done.1
  86.4 1.9 collective-permute-start.2
  89.6 7.3 %all-to-all-done.2 = f32[32,8,8,128]{3,2,1,0:T(8,128)} async-done(((f32[32,8,8,128]{3,2,1,0:T(8,128)}), f32[32,8,8,128]{3,2,1,0:T(8,128)}, u32[]{:S(2)}, u32[]{:S(2)}) %all-to-all-start.2) | async-done | bytes 1048608 | tf_op jit(solution)/shard_map/all_to_all | solution.py:86
  98.5 28.1 %scatter_fusion.1 = f32[512,8,128]{2,1,0:T(8,128)} fusion(f32[512,8,128]{2,1,0:T(8,128)} %broadcast.382.clone, s32[256]{0:T(256)S(1)} %bitcast.111, f32[256,8,128]{2,1,0:T(8,128)} %bitcast.16), kind=kCustom, calls=%fused_computation.7 | custom fusion | flops 262144 | bytes 3146752 | tf_op jit(solution)/shard_map/scatter-add | solution.py:88
  126.6 6.9 %multiply_reduce_fusion.1 = (f32[8]{0:T(128)}, f32[16,32,8,128]{3,2,1,0:T(8,128)S(1)}) fusion(f32[16,32,8,128]{3,2,1,0:T(8,128)S(1)} %get-tuple-element.13, f32[16,32,8,127]{3,2,1,0:T(8,128)} %get-tuple-element.31, f32[16,32,128]{2,1,0:T(8,128)S(1)} %get-tuple-element.37, f32[16,32,8,127]{3,2,1,0:T(8,128)} %get-tuple-element.30, ...), kind=kLoop, calls=%fused_computation.107 | loop fusion | flops 27787256 | bytes 12959808 | tf_op jit(solution)/shard_map/reduce_sum | solution.py:176
  133.5 2.4 collective-permute-start.4
  137.2 2.0 collective-permute-done.4
  139.2 5.0 %collective-permute-done.5 = f32[1,32,8,128]{3,2,1,0:T(8,128)S(1)} collective-permute-done((f32[1,32,8,128]{3,2,1,0:T(8,128)S(1)}, f32[1,32,8,128]{3,2,1,0:T(8,128)S(1)}, u32[]{:S(2)}, u32[]{:S(2)}) %collective-permute-start.5) | collective-permute-done | bytes 131104 | tf_op jit(solution)/shard_map/ppermute | solution.py:20
  144.9 3.8 collective-permute-start.6
  150.0 2.8 fusion.92
  153.9 2.8 gather_fusion.2
  156.7 14.2 %all-to-all-start.3 = ((bf16[32,8,8,128]{3,2,1,0:T(8,128)(2,1)}), bf16[32,8,8,128]{3,2,1,0:T(8,128)(2,1)}, u32[]{:S(2)}, u32[]{:S(2)}) async-start(bf16[32,8,8,128]{3,2,1,0:T(8,128)(2,1)} %bitcast.104), calls=%async_computation.3 | async-start | bytes 1048576 | tf_op jit(solution)/shard_map/all_to_all | solution.py:77
  171.0 11.0 %fusion.21 = f32[8]{0:T(128)S(1)} fusion(f32[16,32,8,128]{3,2,1,0:T(8,128)} %copy-done.2, f32[18,1,8,128]{3,2,1,0:T(8,128)} %collective-permute-done.7, f32[1,32,8,128]{3,2,1,0:T(8,128)} %copy-done.8, f32[1,32,8,128]{3,2,1,0:T(8,128)} %copy-done.7, f32[18,1,8,128]{3,2,1,0:T(8,128)} %collective-permute-done.6, f32[16,32,8,127]{3,2,1,0:T(8,128)} %get-tuple-element.27, ...), kind=kLoop, calls=%fused_computation.47 | loop fusion | flops 39845880 | bytes 15171616 | tf_op jit(solution)/shard_map/reduce_sum | solution.py:66
  182.0 4.4 %all-to-all-done.3 = bf16[32,8,8,128]{3,2,1,0:T(8,128)(2,1)} async-done(((bf16[32,8,8,128]{3,2,1,0:T(8,128)(2,1)}), bf16[32,8,8,128]{3,2,1,0:T(8,128)(2,1)}, u32[]{:S(2)}, u32[]{:S(2)}) %all-to-all-start.3) | async-done | bytes 524320 | tf_op jit(solution)/shard_map/all_to_all | solution.py:77
  186.4 1.8 gather_fusion.3
  188.3 8.2 %fusion.76 = (f32[8]{0:T(128)S(1)}, f32[4,8,512]{2,1,0:T(8,128)S(1)}) fusion(f32[4,512]{1,0:T(4,128)S(1)} %copy-done.24, bf16[4,32,8,128]{3,2,1,0:T(8,128)(2,1)S(1)} %bitcast.108, bf16[4,512,4096]{2,1,0:T(8,128)(2,1)} %param.9), kind=kOutput, calls=%fused_computation.195 | convolution fusion | flops 134266880 | bytes 17113120 | tf_op jit(solution)/shard_map/tdbx,tbsx->tsd/dot_general | solution.py:94
  196.5 38.9 %all-reduce.9 = (f32[8]{0:T(128)S(1)}, f32[8]{0:T(128)S(1)}, f32[8]{0:T(128)S(1)}) all-reduce(f32[8]{0:T(128)S(1)} %copy-done.38, f32[8]{0:T(128)S(1)} %get-tuple-element.45, f32[8]{0:T(128)S(1)} %fusion.21), channel_id=1, replica_groups=mesh['region'=8,'survey'=4] {'region','survey'}, use_global_device_ids=true, to_apply=%region_6.7 | all-reduce | flops 24 | bytes 192 | tf_op jit(solution)/shard_map/psum | solution.py:178
  235.4 7.0 %fusion.2 = f32[4,8,32,128]{3,1,2,0:T(8,128)S(1)} fusion(f32[4,8,512]{2,1,0:T(8,128)S(1)} %copy-done.16, f32[4,512]{1,0:T(4,128)S(1)} %copy-done.24, f32[4,8,512]{2,1,0:T(8,128)S(1)} %copy-done.10, f32[4,8,512]{2,1,0:T(8,128)S(1)} %get-tuple-element.46, f32[8]{0:T(128)S(1)} %add_divide_fusion.1, bf16[4,512,4096]{2,1,0:T(8,128)(2,1)} %param.9), kind=kOutput, calls=%fused_computation.12 | convolution fusion | flops 134299648 | bytes 17506336 | tf_op jit(solution)/shard_map/tsd,tdbx->tbsx/dot_general | solution.py:154
  243.5 12.3 %scatter_fusion.2 = f32[256,8,128]{2,1,0:T(8,128)} fusion(f32[256,8,128]{2,1,0:T(8,128)} %broadcast.388, s32[128]{0:T(128)S(1)} %copy-done.37, f32[128,8,128]{2,1,0:T(8,128)S(1)} %bitcast.101), kind=kCustom, calls=%fused_computation.8 | custom fusion | bytes 1573376 | tf_op jit(solution)/shard_map/scatter | solution.py:84
  255.9 3.9 all-to-all-start.4
  259.8 2.8 maximum_subtract_fusion
  262.6 2.7 fusion.89
  265.3 20.7 %all-to-all-done.4 = f32[32,8,8,128]{3,2,1,0:T(8,128)} async-done(((f32[32,8,8,128]{3,2,1,0:T(8,128)}), f32[32,8,8,128]{3,2,1,0:T(8,128)}, u32[]{:S(2)}, u32[]{:S(2)}) %all-to-all-start.4) | async-done | bytes 1048608 | tf_op jit(solution)/shard_map/all_to_all | solution.py:86
  287.4 28.5 %scatter_fusion.3 = f32[512,8,128]{2,1,0:T(8,128)} fusion(f32[512,8,128]{2,1,0:T(8,128)} %broadcast.382, s32[256]{0:T(256)} %bitcast.112, f32[256,8,128]{2,1,0:T(8,128)} %bitcast.29), kind=kCustom, calls=%fused_computation.9 | custom fusion | flops 262144 | bytes 3146752 | tf_op jit(solution)/shard_map/scatter-add | solution.py:88
  316.0 7.0 %fusion.87 = (bf16[16,32,8,128]{3,2,1,0:T(8,128)(2,1)}, f32[16,32,8,128]{3,2,1,0:T(8,128)S(1)}) fusion(f32[16,32,8,127]{3,2,1,0:T(8,128)} %get-tuple-element.15, f32[16,32,128]{2,1,0:T(8,128)S(1)} %get-tuple-element.37, f32[16,32,8,127]{3,2,1,0:T(8,128)} %get-tuple-element.14, f32[16,32,128]{2,1,0:T(8,128)S(1)} %get-tuple-element.35, ...), kind=kLoop, calls=%fused_computation.235 | loop fusion | flops 23068672 | bytes 21987360 | tf_op jit(solution)/shard_map/convert_element_type | solution.py:169
  322.9 2.7 collective-permute-start.8
  326.9 2.8 fusion.90
  329.7 3.7 collective-permute-done.9
  334.1 2.1 collective-permute-start.10
  338.7 2.9 gather_fusion.4
  341.6 8.1 %all-to-all-start.5 = ((bf16[32,8,8,128]{3,2,1,0:T(8,128)(2,1)}), bf16[32,8,8,128]{3,2,1,0:T(8,128)(2,1)}, u32[]{:S(2)}, u32[]{:S(2)}) async-start(bf16[32,8,8,128]{3,2,1,0:T(8,128)(2,1)} %bitcast.103), calls=%async_computation.5 | async-start | bytes 1048576 | tf_op jit(solution)/shard_map/all_to_all | solution.py:77
  349.7 11.6 %fusion.28 = f32[8]{0:T(128)} fusion(f32[16,32,8,128]{3,2,1,0:T(8,128)} %copy-done.3, f32[18,1,8,128]{3,2,1,0:T(8,128)} %collective-permute-done.11, f32[1,32,8,128]{3,2,1,0:T(8,128)} %copy-done.21, f32[1,32,8,128]{3,2,1,0:T(8,128)} %copy-done.20, f32[18,1,8,128]{3,2,1,0:T(8,128)} %collective-permute-done.10, f32[16,32,8,127]{3,2,1,0:T(8,128)} %get-tuple-element.23, ...), kind=kLoop, calls=%fused_computation.54 | loop fusion | flops 35651576 | bytes 23150624 | tf_op jit(solution)/shard_map/reduce_sum | solution.py:66
  361.3 3.7 all-to-all-done.5
  367.0 8.3 %fusion.77 = (f32[8]{0:T(128)S(1)}, f32[4,8,512]{2,1,0:T(8,128)S(1)}) fusion(f32[4,512]{1,0:T(4,128)} %copy-done.23, bf16[4,32,8,128]{3,2,1,0:T(8,128)(2,1)S(1)} %bitcast.107, bf16[4,512,4096]{2,1,0:T(8,128)(2,1)} %param.9), kind=kOutput, calls=%fused_computation.196 | convolution fusion | flops 134266880 | bytes 17113120 | tf_op jit(solution)/shard_map/tdbx,tbsx->tsd/dot_general | solution.py:94
  375.3 38.9 %all-reduce.8 = (f32[8]{0:T(128)S(1)}, f32[8]{0:T(128)S(1)}, f32[8]{0:T(128)S(1)}) all-reduce(f32[8]{0:T(128)S(1)} %copy-done.39, f32[8]{0:T(128)S(1)} %get-tuple-element.47, f32[8]{0:T(128)S(1)} %copy-done.40), channel_id=1, replica_groups=mesh['region'=8,'survey'=4] {'region','survey'}, use_global_device_ids=true, to_apply=%region_14.15 | all-reduce | flops 24 | bytes 192 | tf_op jit(solution)/shard_map/psum | solution.py:178
  414.3 4.0 multiply_subtract_fusion
  (138 shorter events, 31.5 us)
Async XLA Ops:
  2.7 14.4 %all-to-all-start = ((s32[32,1,8]{2,1,0:T(1,128)}), s32[32,1,8]{2,1,0:T(1,128)S(1)}, u32[]{:S(2)}, u32[]{:S(2)}) async-start(s32[32,1,8]{2,1,0:T(1,128)} %bitcast), calls=%async_computation | async-start | bytes 32768 | tf_op jit(solution)/shard_map/all_to_all | solution.py:127
  13.7 157.3 %copy-start = (f32[16,32,8,128]{3,2,1,0:T(8,128)}, f32[16,32,8,128]{3,2,1,0:T(8,128)S(1)}, u32[]{:S(2)}) copy-start(f32[16,32,8,128]{3,2,1,0:T(8,128)S(1)} %get-tuple-element.13) | copy-start | bytes 6291460
  13.7 8.3 %copy-start.34 = (s32[4,32]{1,0:T(4,128)S(1)}, s32[4,32]{1,0:T(4,128)}, u32[]{:S(2)}) copy-start(s32[4,32]{1,0:T(4,128)} %param.13) | copy-start | bytes 1540
  13.7 8.4 %copy-start.33 = (f32[4,512]{1,0:T(4,128)S(1)}, f32[4,512]{1,0:T(4,128)}, u32[]{:S(2)}) copy-start(f32[4,512]{1,0:T(4,128)} %param.11) | copy-start | bytes 24580
  13.7 8.4 %copy-start.41 = (s32[4]{0:T(128)S(1)}, s32[4]{0:T(128)}, u32[]{:S(2)}) copy-start(s32[4]{0:T(128)} %param.12) | copy-start | bytes 52
  17.8 28.6 %copy-start.13 = (s32[1024]{0:T(1024)}, s32[1024]{0:T(1024)S(1)}, u32[]{:S(2)}) copy-start(s32[1024]{0:T(1024)S(1)} %pad_clamp_fusion.1) | copy-start | bytes 12292
  19.4 18.2 %all-to-all-start.1 = ((bf16[32,8,8,128]{3,2,1,0:T(8,128)(2,1)}), bf16[32,8,8,128]{3,2,1,0:T(8,128)(2,1)S(1)}, u32[]{:S(2)}, u32[]{:S(2)}) async-start(bf16[32,8,8,128]{3,2,1,0:T(8,128)(2,1)} %bitcast.105), calls=%async_computation.1 | async-start | bytes 1048576 | tf_op jit(solution)/shard_map/all_to_all | solution.py:77
  22.1 32.4 %copy-start.36 = (s32[128]{0:T(128)}, s32[128]{0:T(128)S(1)}, u32[]{:S(2)}) copy-start(s32[128]{0:T(128)S(1)} %fusion.86) | copy-start | bytes 1540
  22.2 24.2 %copy-start.35 = (s32[1024]{0:T(1024)}, s32[1024]{0:T(1024)S(1)}, u32[]{:S(2)}) copy-start(s32[1024]{0:T(1024)S(1)} %pad_clamp_fusion) | copy-start | bytes 12292
  22.8 23.6 %copy-start.23 = (f32[4,512]{1,0:T(4,128)}, f32[4,512]{1,0:T(4,128)S(1)}, u32[]{:S(2)}) copy-start(f32[4,512]{1,0:T(4,128)S(1)} %get-tuple-element.41) | copy-start | bytes 24580
  38.3 8.1 %copy-start.15 = (f32[4,8,512]{2,1,0:T(8,128)S(1)}, f32[4,8,512]{2,1,0:T(8,128)}, u32[]{:S(2)}) copy-start(f32[4,8,512]{2,1,0:T(8,128)} %param.10) | copy-start | bytes 196612
  46.4 7.0 %copy-start.9 = (f32[4,8,512]{2,1,0:T(8,128)}, f32[4,8,512]{2,1,0:T(8,128)S(1)}, u32[]{:S(2)}) copy-start(f32[4,8,512]{2,1,0:T(8,128)S(1)} %fusion.41) | copy-start | bytes 196612
  66.8 30.1 %all-to-all-start.2 = ((f32[32,8,8,128]{3,2,1,0:T(8,128)}), f32[32,8,8,128]{3,2,1,0:T(8,128)}, u32[]{:S(2)}, u32[]{:S(2)}) async-start(f32[32,8,8,128]{3,2,1,0:T(8,128)} %bitcast.15), calls=%async_computation.2 | async-start | bytes 2097152 | tf_op jit(solution)/shard_map/all_to_all | solution.py:86
  71.0 12.2 %collective-permute-start = (f32[1,32,8,128]{3,2,1,0:T(8,128)}, f32[1,32,8,128]{3,2,1,0:T(8,128)S(1)}, u32[]{:S(2)}, u32[]{:S(2)}) collective-permute-start(f32[1,32,8,128]{3,2,1,0:T(8,128)} %get-tuple-element.32), channel_id=1, source_target_pairs={{0,4},{4,8},{8,12},{12,16},{16,20},{20,24},{24,28},{1,5},{5,9},{9,... | collective-permute-start | bytes 393224 | tf_op jit(solution)/shard_map/ppermute | solution.py:19
  74.4 10.6 %collective-permute-start.1 = (f32[1,32,8,128]{3,2,1,0:T(8,128)}, f32[1,32,8,128]{3,2,1,0:T(8,128)}, u32[]{:S(2)}, u32[]{:S(2)}) collective-permute-start(f32[1,32,8,128]{3,2,1,0:T(8,128)} %get-tuple-element.33), channel_id=1, source_target_pairs={{4,0},{8,4},{12,8},{16,12},{20,16},{24,20},{28,24},{5,1},{9,5},{13... | collective-permute-start | bytes 393224 | tf_op jit(solution)/shard_map/ppermute | solution.py:20
  80.6 90.4 %copy-start.4 = (f32[16,32,128]{2,1,0:T(8,128)}, f32[16,32,128]{2,1,0:T(8,128)S(1)}, u32[]{:S(2)}) copy-start(f32[16,32,128]{2,1,0:T(8,128)S(1)} %get-tuple-element.38) | copy-start | bytes 786436
  83.2 87.8 %copy-start.6 = (f32[1,32,8,128]{3,2,1,0:T(8,128)}, f32[1,32,8,128]{3,2,1,0:T(8,128)S(1)}, u32[]{:S(2)}) copy-start(f32[1,32,8,128]{3,2,1,0:T(8,128)S(1)} %collective-permute-done) | copy-start | bytes 393220
  86.4 40.2 %collective-permute-start.2 = (f32[18,1,8,128]{3,2,1,0:T(8,128)}, f32[18,1,8,128]{3,2,1,0:T(8,128)}, u32[]{:S(2)}, u32[]{:S(2)}) collective-permute-start(f32[18,1,8,128]{3,2,1,0:T(8,128)} %get-tuple-element.20), channel_id=1, source_target_pairs={{0,1},{1,2},{2,3},{4,5},{5,6},{6,7},{8,9},{9,10},{10,11},{12,13},{... | collective-permute-start | bytes 221192 | tf_op jit(solution)/shard_map/ppermute | solution.py:19
  88.3 38.3 %collective-permute-start.3 = (f32[18,1,8,128]{3,2,1,0:T(8,128)}, f32[18,1,8,128]{3,2,1,0:T(8,128)}, u32[]{:S(2)}, u32[]{:S(2)}) collective-permute-start(f32[18,1,8,128]{3,2,1,0:T(8,128)} %get-tuple-element.21), channel_id=1, source_target_pairs={{1,0},{2,1},{3,2},{5,4},{6,5},{7,6},{9,8},{10,9},{11,10},{13,12},{... | collective-permute-start | bytes 221192 | tf_op jit(solution)/shard_map/ppermute | solution.py:20
  89.6 37.0 %copy-start.30 = (s32[256,1]{0,1:T(1,128)}, s32[256,1]{0,1:T(1,128)S(1)}, u32[]{:S(2)}) copy-start(s32[256,1]{0,1:T(1,128)S(1)} %compare_select_fusion.1) | copy-start | bytes 3076
  98.5 28.1 %copy-start.31 = (f32[8]{0:T(128)S(1)}, f32[8]{0:T(128)}, u32[]{:S(2)}) copy-start(f32[8]{0:T(128)} %param.17) | copy-start | bytes 100
  133.5 20.4 %copy-start.2 = (f32[16,32,8,128]{3,2,1,0:T(8,128)}, f32[16,32,8,128]{3,2,1,0:T(8,128)S(1)}, u32[]{:S(2)}) copy-start(f32[16,32,8,128]{3,2,1,0:T(8,128)S(1)} %get-tuple-element.11) | copy-start | bytes 6291460
  133.5 5.7 %collective-permute-start.4 = (f32[1,32,8,128]{3,2,1,0:T(8,128)S(1)}, f32[1,32,8,128]{3,2,1,0:T(8,128)S(1)}, u32[]{:S(2)}, u32[]{:S(2)}) collective-permute-start(f32[1,32,8,128]{3,2,1,0:T(8,128)S(1)} %get-tuple-element.28), channel_id=1, source_target_pairs={{0,4},{4,8},{8,12},{12,16},{16,20},{20,24},{24,28},{1,5},{5,9},{9,... | collective-permute-start | bytes 393224 | tf_op jit(solution)/shard_map/ppermute | solution.py:19
  135.9 8.2 %collective-permute-start.5 = (f32[1,32,8,128]{3,2,1,0:T(8,128)S(1)}, f32[1,32,8,128]{3,2,1,0:T(8,128)S(1)}, u32[]{:S(2)}, u32[]{:S(2)}) collective-permute-start(f32[1,32,8,128]{3,2,1,0:T(8,128)S(1)} %get-tuple-element.29), channel_id=1, source_target_pairs={{4,0},{8,4},{12,8},{16,12},{20,16},{24,20},{28,24},{5,1},{9,5},{13... | collective-permute-start | bytes 393224 | tf_op jit(solution)/shard_map/ppermute | solution.py:20
  144.9 26.1 %collective-permute-start.6 = (f32[18,1,8,128]{3,2,1,0:T(8,128)}, f32[18,1,8,128]{3,2,1,0:T(8,128)}, u32[]{:S(2)}, u32[]{:S(2)}) collective-permute-start(f32[18,1,8,128]{3,2,1,0:T(8,128)} %get-tuple-element.18), channel_id=1, source_target_pairs={{0,1},{1,2},{2,3},{4,5},{5,6},{6,7},{8,9},{9,10},{10,11},{12,13},{... | collective-permute-start | bytes 221192 | tf_op jit(solution)/shard_map/ppermute | solution.py:19
  148.7 22.3 %collective-permute-start.7 = (f32[18,1,8,128]{3,2,1,0:T(8,128)}, f32[18,1,8,128]{3,2,1,0:T(8,128)}, u32[]{:S(2)}, u32[]{:S(2)}) collective-permute-start(f32[18,1,8,128]{3,2,1,0:T(8,128)} %get-tuple-element.19), channel_id=1, source_target_pairs={{1,0},{2,1},{3,2},{5,4},{6,5},{7,6},{9,8},{10,9},{11,10},{13,12},{... | collective-permute-start | bytes 221192 | tf_op jit(solution)/shard_map/ppermute | solution.py:20
  156.7 29.6 %all-to-all-start.3 = ((bf16[32,8,8,128]{3,2,1,0:T(8,128)(2,1)}), bf16[32,8,8,128]{3,2,1,0:T(8,128)(2,1)}, u32[]{:S(2)}, u32[]{:S(2)}) async-start(bf16[32,8,8,128]{3,2,1,0:T(8,128)(2,1)} %bitcast.104), calls=%async_computation.3 | async-start | bytes 1048576 | tf_op jit(solution)/shard_map/all_to_all | solution.py:77
  171.0 17.2 %copy-start.24 = (f32[4,512]{1,0:T(4,128)S(1)}, f32[4,512]{1,0:T(4,128)}, u32[]{:S(2)}) copy-start(f32[4,512]{1,0:T(4,128)} %copy-done.23) | copy-start | bytes 24580
  188.2 8.2 %copy-start.38 = (f32[8]{0:T(128)S(1)}, f32[8]{0:T(128)}, u32[]{:S(2)}) copy-start(f32[8]{0:T(128)} %get-tuple-element.10) | copy-start | bytes 100
  188.2 47.2 %copy-start.10 = (f32[4,8,512]{2,1,0:T(8,128)S(1)}, f32[4,8,512]{2,1,0:T(8,128)}, u32[]{:S(2)}) copy-start(f32[4,8,512]{2,1,0:T(8,128)} %copy-done.9) | copy-start | bytes 196612
  188.2 47.2 %copy-start.16 = (f32[4,8,512]{2,1,0:T(8,128)S(1)}, f32[4,8,512]{2,1,0:T(8,128)}, u32[]{:S(2)}) copy-start(f32[4,8,512]{2,1,0:T(8,128)} %param.10) | copy-start | bytes 196612
  196.5 46.0 %copy-start.18 = (f32[4,8,512]{2,1,0:T(8,128)}, f32[4,8,512]{2,1,0:T(8,128)S(1)}, u32[]{:S(2)}) copy-start(f32[4,8,512]{2,1,0:T(8,128)S(1)} %get-tuple-element.46) | copy-start | bytes 196612
  235.4 7.1 %copy-start.28 = (f32[8]{0:T(128)}, f32[8]{0:T(128)S(1)}, u32[]{:S(2)}) copy-start(f32[8]{0:T(128)S(1)} %add_divide_fusion.1) | copy-start | bytes 100
  235.4 8.1 %copy-start.37 = (s32[128]{0:T(128)S(1)}, s32[128]{0:T(128)}, u32[]{:S(2)}) copy-start(s32[128]{0:T(128)} %copy-done.36) | copy-start | bytes 1540
  255.9 30.1 %all-to-all-start.4 = ((f32[32,8,8,128]{3,2,1,0:T(8,128)}), f32[32,8,8,128]{3,2,1,0:T(8,128)}, u32[]{:S(2)}, u32[]{:S(2)}) async-start(f32[32,8,8,128]{3,2,1,0:T(8,128)} %bitcast.28), calls=%async_computation.4 | async-start | bytes 2097152 | tf_op jit(solution)/shard_map/all_to_all | solution.py:86
  322.9 15.7 %copy-start.3 = (f32[16,32,8,128]{3,2,1,0:T(8,128)}, f32[16,32,8,128]{3,2,1,0:T(8,128)S(1)}, u32[]{:S(2)}) copy-start(f32[16,32,8,128]{3,2,1,0:T(8,128)S(1)} %get-tuple-element.9) | copy-start | bytes 6291460
  322.9 6.8 %collective-permute-start.8 = (f32[1,32,8,128]{3,2,1,0:T(8,128)S(1)}, f32[1,32,8,128]{3,2,1,0:T(8,128)S(1)}, u32[]{:S(2)}, u32[]{:S(2)}) collective-permute-start(f32[1,32,8,128]{3,2,1,0:T(8,128)S(1)} %get-tuple-element.24), channel_id=1, source_target_pairs={{0,4},{4,8},{8,12},{12,16},{16,20},{20,24},{24,28},{1,5},{5,9},{9,... | collective-permute-start | bytes 393224 | tf_op jit(solution)/shard_map/ppermute | solution.py:19
  325.6 7.8 %collective-permute-start.9 = (f32[1,32,8,128]{3,2,1,0:T(8,128)S(1)}, f32[1,32,8,128]{3,2,1,0:T(8,128)S(1)}, u32[]{:S(2)}, u32[]{:S(2)}) collective-permute-start(f32[1,32,8,128]{3,2,1,0:T(8,128)S(1)} %get-tuple-element.25), channel_id=1, source_target_pairs={{4,0},{8,4},{12,8},{16,12},{20,16},{24,20},{28,24},{5,1},{9,5},{13... | collective-permute-start | bytes 393224 | tf_op jit(solution)/shard_map/ppermute | solution.py:20
  329.7 8.9 %copy-start.20 = (f32[1,32,8,128]{3,2,1,0:T(8,128)}, f32[1,32,8,128]{3,2,1,0:T(8,128)S(1)}, u32[]{:S(2)}) copy-start(f32[1,32,8,128]{3,2,1,0:T(8,128)S(1)} %collective-permute-done.8) | copy-start | bytes 393220
  333.4 5.3 %copy-start.21 = (f32[1,32,8,128]{3,2,1,0:T(8,128)}, f32[1,32,8,128]{3,2,1,0:T(8,128)S(1)}, u32[]{:S(2)}) copy-start(f32[1,32,8,128]{3,2,1,0:T(8,128)S(1)} %collective-permute-done.9) | copy-start | bytes 393220
  334.1 15.6 %collective-permute-start.10 = (f32[18,1,8,128]{3,2,1,0:T(8,128)}, f32[18,1,8,128]{3,2,1,0:T(8,128)}, u32[]{:S(2)}, u32[]{:S(2)}) collective-permute-start(f32[18,1,8,128]{3,2,1,0:T(8,128)} %get-tuple-element.16), channel_id=1, source_target_pairs={{0,1},{1,2},{2,3},{4,5},{5,6},{6,7},{8,9},{9,10},{10,11},{12,13},{... | collective-permute-start | bytes 221192 | tf_op jit(solution)/shard_map/ppermute | solution.py:19
  336.2 13.5 %collective-permute-start.11 = (f32[18,1,8,128]{3,2,1,0:T(8,128)}, f32[18,1,8,128]{3,2,1,0:T(8,128)}, u32[]{:S(2)}, u32[]{:S(2)}) collective-permute-start(f32[18,1,8,128]{3,2,1,0:T(8,128)} %get-tuple-element.17), channel_id=1, source_target_pairs={{1,0},{2,1},{3,2},{5,4},{6,5},{7,6},{9,8},{10,9},{11,10},{13,12},{... | collective-permute-start | bytes 221192 | tf_op jit(solution)/shard_map/ppermute | solution.py:20
  341.6 23.5 %all-to-all-start.5 = ((bf16[32,8,8,128]{3,2,1,0:T(8,128)(2,1)}), bf16[32,8,8,128]{3,2,1,0:T(8,128)(2,1)}, u32[]{:S(2)}, u32[]{:S(2)}) async-start(bf16[32,8,8,128]{3,2,1,0:T(8,128)(2,1)} %bitcast.103), calls=%async_computation.5 | async-start | bytes 1048576 | tf_op jit(solution)/shard_map/all_to_all | solution.py:77
  366.9 8.4 %copy-start.39 = (f32[8]{0:T(128)S(1)}, f32[8]{0:T(128)}, u32[]{:S(2)}) copy-start(f32[8]{0:T(128)} %multiply_reduce_fusion) | copy-start | bytes 100
  366.9 8.4 %copy-start.40 = (f32[8]{0:T(128)S(1)}, f32[8]{0:T(128)}, u32[]{:S(2)}) copy-start(f32[8]{0:T(128)} %fusion.28) | copy-start | bytes 100
  366.9 47.3 %copy-start.32 = (f32[8]{0:T(128)S(1)}, f32[8]{0:T(128)}, u32[]{:S(2)}) copy-start(f32[8]{0:T(128)} %param.17) | copy-start | bytes 100
  366.9 47.3 %copy-start.1 = (f32[16,32,8,128]{3,2,1,0:T(8,128)S(1)}, f32[16,32,8,128]{3,2,1,0:T(8,128)}, u32[]{:S(2)}) copy-start(f32[16,32,8,128]{3,2,1,0:T(8,128)} %copy-done) | copy-start | bytes 6291460
  366.9 47.3 %copy-start.29 = (f32[8]{0:T(128)S(1)}, f32[8]{0:T(128)}, u32[]{:S(2)}) copy-start(f32[8]{0:T(128)} %copy-done.28) | copy-start | bytes 100
  (12 other events, 32.5 us)
where the time goes:
time: 422 us; the launch traced here: 419 us
  other arithmetic  113 us (27%)
  blocking collectives  77.9 us (18%)
  waiting for transfers between devices  66.7 us (16%)
  starting transfers between devices  63.5 us (15%)
  local copies, waits for them, and re-layouts  57.7 us (14%)
  matrix products  38.6 us (9%)
    psum x2, blocking collectives, shards(): lax.psum((grad_norm, data_curv, reg_curv), ('region', 'survey'))  77.9 us
    scatter-add x2, other arithmetic, return_grads(): summed.at[asked_ids.reshape(-1)].add(arrived.reshape(-1, samples, cells_x))  56.7 us
    all_to_all x2, waiting for transfers between devices, return_grads(): lax.all_to_all(buffer, ('region', 'survey'), split_axis=0, concat_axis=0,...  28 us
    all_to_all x3, starting transfers between devices, fetch_bricks(): lax.all_to_all(replies, ('region', 'survey'), split_axis=0, concat_axis=0...  24.9 us
    scatter x2, local copies, waits for them, and re-layouts, return_grads(): jnp.zeros((owners * capacity, samples, cells_x), jnp.float32).at[slot_of]  24.7 us
    dot_general x3, matrix products, predict(): jnp.einsum('tdbx,tbsx->tsd', sensor_view, picked, preferred_element_type=...  24.6 us
    all_to_all x3, waiting for transfers between devices, fetch_bricks(): lax.all_to_all(replies, ('region', 'survey'), split_axis=0, concat_axis=0...  22.9 us
    reduce_sum x2, other arithmetic, reg_curvature(): return jnp.sum(running, axis=(0, 1, 3))  22.6 us
  transfers between devices with their start and end apart: 18, of which 10 were waited for; matrix products, arithmetic and copies ran while one was open for 20% of the time, Pallas kernels for 0%

commit v1 on v0

v1 whole, which is shorter than its diff:
```python
import functools

import jax
import jax.numpy as jnp
from jax import lax
from jax.experimental import pallas as pl
from jax.experimental.pallas import tpu as pltpu
from jax.sharding import PartitionSpec as P

AXES = ("region", "survey")
EPS_SQ = 0.09
VMEM_LIMIT = 32 * 1024 * 1024


def swap(field):
    return lax.all_to_all(field, AXES, split_axis=0, concat_axis=0, tiled=True)


def edges(field):
    rims = []
    for axis, dim in (("region", 0), ("survey", 1)):
        count, length = (lax.axis_size(axis), field.shape[dim])
        up = [(i, i + 1) for i in range(count - 1)]
        down = [(i + 1, i) for i in range(count - 1)]
        last = lax.slice_in_dim(field, length - 1, length, axis=dim)
        first = lax.slice_in_dim(field, 0, 1, axis=dim)
        rims.append(lax.ppermute(last, axis, up))
        rims.append(lax.ppermute(first, axis, down))
    return rims


def neighbour_list(centre, rims):
    above, below, left, right = rims
    zero_rim = jnp.zeros_like(centre[..., :1])
    return [
        jnp.concatenate([above, centre[:-1]], axis=0),
        jnp.concatenate([centre[1:], below], axis=0),
        jnp.concatenate([left, centre[:, :-1]], axis=1),
        jnp.concatenate([centre[:, 1:], right], axis=1),
        jnp.concatenate([zero_rim, centre[..., :-1]], axis=3),
        jnp.concatenate([centre[..., 1:], zero_rim], axis=3),
    ]


def irls_weights(centre, neighbours, link_bits, depth_index, active, depth_count):
    smallness = (
        active * (1.0 + 2.0 * depth_index / depth_count) * lax.rsqrt(centre * centre + EPS_SQ)
    )
    offsets = [-1.0, 1.0, 0.0, 0.0, 0.0, 0.0]
    face_weights = []
    for number in range(6):
        depth_level = 1.0 + (2.0 * depth_index + offsets[number]) / depth_count
        difference = centre - neighbours[number]
        face_weights.append(
            link_bits[number] * depth_level * lax.rsqrt(difference * difference + EPS_SQ)
        )
    return (smallness, face_weights)


def reg_gradient(centre, neighbours, smallness, face_weights):
    running = smallness * centre
    for number in range(6):
        running = running + face_weights[number] * (centre - neighbours[number])
    return running


def reg_curvature(centre, neighbours, smallness, face_weights):
    running = smallness * centre * centre
    for number in range(6):
        difference = centre - neighbours[number]
        running = running + 0.5 * face_weights[number] * difference * difference
    return jnp.sum(running, axis=(0, 1, 3))


def gather_rows(tile, width, slot_ref, arrived_ref, rows_ref):
    cells = arrived_ref.shape[2]
    for entry in range(width):
        slot = slot_ref[tile * width + entry]
        rows_ref[:, entry * cells : (entry + 1) * cells] = arrived_ref[slot]


def scatter_rows(tile, width, slot_ref, blocks, buffer_ref):
    cells = buffer_ref.shape[2]
    for entry in range(width):
        slot = slot_ref[tile * width + entry]
        block = blocks[:, entry * cells : (entry + 1) * cells]
        buffer_ref[slot] = block.astype(buffer_ref.dtype)


def project(rows, sensor):
    return lax.dot_general(
        rows, sensor, (((1,), (1,)), ((), ())), preferred_element_type=jnp.float32
    )


def residual_kernel(
    slot_ref, arrived_ref, sensor_ref, observed_ref, weight_ref, pred_ref, buffer_ref, rows_ref
):
    tile = pl.program_id(0)
    width = slot_ref.shape[0] // pl.num_programs(0)

    @pl.when(tile == 0)
    def _():
        buffer_ref[...] = jnp.zeros_like(buffer_ref)

    gather_rows(tile, width, slot_ref, arrived_ref, rows_ref)
    pred = project(rows_ref[...], sensor_ref[0])
    pred_ref[0] = pred
    weighted = (weight_ref[0] * (pred - observed_ref[0])).astype(jnp.bfloat16)
    blocks = jnp.dot(weighted, sensor_ref[0], preferred_element_type=jnp.float32)
    scatter_rows(tile, width, slot_ref, blocks, buffer_ref)


def forward_kernel(slot_ref, arrived_ref, sensor_ref, weight_ref, pred_ref, curv_ref, rows_ref):
    tile = pl.program_id(0)
    width = slot_ref.shape[0] // pl.num_programs(0)

    @pl.when(tile == 0)
    def _():
        curv_ref[...] = jnp.zeros_like(curv_ref)

    gather_rows(tile, width, slot_ref, arrived_ref, rows_ref)
    pred = project(rows_ref[...], sensor_ref[0])
    pred_ref[0] = pred
    curv_ref[...] += weight_ref[0] * pred * pred


def backward_kernel(slot_ref, sensor_ref, pred_ref, weight_ref, buffer_ref):
    tile = pl.program_id(0)
    width = slot_ref.shape[0] // pl.num_programs(0)
    samples = pred_ref.shape[1]

    @pl.when(tile == 0)
    def _():
        buffer_ref[...] = jnp.zeros_like(buffer_ref)

    weighted = weight_ref[0] * pred_ref[0]
    upper = weighted.astype(jnp.bfloat16).astype(jnp.float32)
    both = jnp.concatenate([upper, weighted - upper], axis=0).astype(jnp.bfloat16)
    blocks = jnp.dot(both, sensor_ref[0], preferred_element_type=jnp.float32)
    scatter_rows(tile, width, slot_ref, blocks[:samples] + blocks[samples:], buffer_ref)


def tile_call(kernel, name, ids, operands, outs, scratch, fixed):
    tiles = outs[0].shape[0] if "pred" in name else operands[0].shape[0]

    def spec(array, whole):
        if whole:
            return pl.BlockSpec(array.shape, lambda t, *_: (0,) * len(array.shape))
        block = (1,) + tuple(array.shape[1:])
        return pl.BlockSpec(block, lambda t, *_: (t,) + (0,) * (len(block) - 1))

    return pl.pallas_call(
        kernel,
        name=name,
        out_shape=outs,
        grid_spec=pltpu.PrefetchScalarGridSpec(
            num_scalar_prefetch=1,
            grid=(tiles,),
            in_specs=[spec(a, f) for a, f in zip(operands, fixed[0])],
            out_specs=[spec(a, f) for a, f in zip(outs, fixed[1])],
            scratch_shapes=scratch,
        ),
        compiler_params=pltpu.CompilerParams(
            dimension_semantics=("arbitrary",), vmem_limit_bytes=VMEM_LIMIT
        ),
    )(ids, *operands)


def sum_kernel(
    first, ids_ref, arrived_ref, reg_ref, active_ref, *refs
):
    if first:
        total_ref, grad_ref, reply_ref, norm_ref = refs
    else:
        base_ref, step_ref, grad_ref, reply_ref, norm_ref, total_ref = refs
        step = step_ref[...]
    count = ids_ref.shape[0]
    bricks = grad_ref.shape[0]
    group = 8
    total_ref[...] = jnp.zeros_like(total_ref)

    def add(i, carry):
        for k in range(group):
            j = i * group + k
            row = ids_ref[j]
            total_ref[row] += arrived_ref[j].astype(jnp.float32)
        return carry

    lax.fori_loop(0, count // group, add, 0)

    def combine(i, norm):
        live = active_ref[pl.ds(pl.multiple_of(i * group, group), group), :]
        for k in range(group):
            j = i * group + k
            data = total_ref[j]
            if not first:
                data = base_ref[j] - step * data
            grad = live[k : k + 1] * data + reg_ref[j]
            grad_ref[j] = grad
            norm = norm + grad * grad
        return norm

    norm = lax.fori_loop(0, bricks // group, combine, jnp.zeros(norm_ref.shape, jnp.float32))
    norm_ref[...] = norm

    def reply(i, carry):
        for k in range(group):
            j = i * group + k
            reply_ref[j] = grad_ref[ids_ref[j]].astype(reply_ref.dtype)
        return carry

    lax.fori_loop(0, count // group, reply, 0)


def sum_call(first, ids, arrived, reg, active, *more):
    bricks, samples, cells = reg.shape
    field = jax.ShapeDtypeStruct((bricks, samples, cells), jnp.float32)
    outs = [
        field,
        jax.ShapeDtypeStruct(arrived.shape, jnp.bfloat16),
        jax.ShapeDtypeStruct((samples, cells), jnp.float32),
    ]
    scratch = []
    if first:
        outs = [field] + outs
    else:
        scratch = [pltpu.VMEM(field.shape, jnp.float32)]
    whole = pl.BlockSpec(memory_space=pltpu.VMEM)
    operands = (arrived, reg, active) + more
    return pl.pallas_call(
        functools.partial(sum_kernel, first),
        name="sum_first" if first else "sum_next",
        out_shape=outs,
        grid_spec=pltpu.PrefetchScalarGridSpec(
            num_scalar_prefetch=1,
            grid=(),
            in_specs=[whole] * len(operands),
            out_specs=[whole] * len(outs),
            scratch_shapes=scratch,
        ),
        compiler_params=pltpu.CompilerParams(vmem_limit_bytes=VMEM_LIMIT),
    )(ids, *operands)


def total_sums(owners, samples, *sums):
    packed = jnp.concatenate(sums)
    packed = jnp.pad(packed, (0, -packed.shape[0] % 128))
    sent = jnp.broadcast_to(packed[None, None, :], (owners, 1, packed.shape[0]))
    got = jnp.sum(swap(sent), axis=(0, 1))
    return [got[i * samples : (i + 1) * samples] for i in range(len(sums))]


def shards(
    sensitivity,
    observed,
    data_weight,
    data_counts,
    tile_bricks,
    start_model,
    active_cells,
    face_links,
    reg_weight,
):
    layers, strip_rows, samples, cells_x = start_model.shape
    tiles, tile_width = tile_bricks.shape
    data_slots = sensitivity.shape[1]
    owners = lax.axis_size("region") * lax.axis_size("survey")
    per_owner = layers * strip_rows
    capacity = max(2, 2 * tiles * tile_width // owners)
    slots = owners * capacity
    depth_count = layers * lax.axis_size("region")
    requests = tile_bricks.reshape(-1)
    owner_of = requests // per_owner
    local_of = requests % per_owner
    owner_hits = (owner_of[:, None] == jnp.arange(owners, dtype=jnp.int32)[None, :]).astype(
        jnp.int32
    )
    before = jnp.cumsum(owner_hits, axis=0) - owner_hits
    rank_of = jnp.sum(before * owner_hits, axis=1)
    slot_of = owner_of * capacity + rank_of
    slot_hits = slot_of[:, None] == jnp.arange(slots, dtype=jnp.int32)[None, :]
    asking = jnp.sum(jnp.where(slot_hits, local_of[:, None], 0), axis=0).reshape(owners, capacity)
    asked_ids = swap(asking).reshape(-1)

    active_rows = active_cells.astype(jnp.float32)
    active = active_rows[:, :, None, :]
    active_flat = active_rows.reshape(per_owner, cells_x)
    link_bits = [
        (face_links // 2**number % 2).astype(jnp.float32)[:, :, None, :] for number in range(6)
    ]
    depth_index = (
        (lax.axis_index("region") * layers + jnp.arange(layers, dtype=jnp.int32))
        .astype(jnp.float32)
        .reshape(layers, 1, 1, 1)
    )
    row_mask = (
        jnp.arange(data_slots, dtype=jnp.int32)[None, None, :] < data_counts[:, None, None]
    ).astype(jnp.float32)
    weight_sq = row_mask * (data_weight * data_weight)[:, None, :]
    reg_scale = reg_weight[None, None, :, None]

    model = start_model * active
    model_rims = edges(model)

    bricks = model.astype(jnp.bfloat16).reshape(per_owner, samples, cells_x)
    replies = bricks[asked_ids]
    f32 = functools.partial(jax.ShapeDtypeStruct, dtype=jnp.float32)
    pred_shape = f32((tiles, samples, data_slots))
    buffer_shape = jax.ShapeDtypeStruct((slots, samples, cells_x), jnp.bfloat16)
    rows = pltpu.VMEM((samples, tile_width * cells_x), jnp.bfloat16)

    def exchange(blocks):
        return swap(blocks.reshape(owners, capacity, samples, cells_x)).reshape(
            slots, samples, cells_x
        )

    def weights_of(field, rims):
        neighbours = neighbour_list(field, rims)
        smallness, faces = irls_weights(
            field, neighbours, link_bits, depth_index, active, depth_count
        )
        return smallness, faces, reg_scale * reg_gradient(field, neighbours, smallness, faces)

    predicted, buffer = tile_call(
        residual_kernel,
        "residual_pred",
        slot_of,
        (exchange(replies), sensitivity, observed, weight_sq),
        [pred_shape, buffer_shape],
        [rows],
        ((True, False, False, False), (False, True)),
    )

    def forward(replies):
        return tile_call(
            forward_kernel,
            "forward_pred",
            slot_of,
            (exchange(replies), sensitivity, weight_sq),
            [pred_shape, f32((samples, data_slots))],
            [rows],
            ((True, False, False), (False, True)),
        )

    def curvature(grad, rims, smallness, faces):
        return reg_curvature(grad, neighbour_list(grad, rims), smallness, faces)

    def step_of(norm, data_curv, reg_curv):
        norm, data_curv, reg_curv = total_sums(
            owners, samples, jnp.sum(norm, axis=1), jnp.sum(data_curv, axis=1), reg_curv
        )
        return norm / (data_curv + reg_weight * reg_curv)

    smallness, faces, reg = weights_of(model, model_rims)
    data_sum, grad, replies, norm = sum_call(
        True, asked_ids, exchange(buffer), reg.reshape(per_owner, samples, cells_x), active_flat
    )
    grad = grad.reshape(start_model.shape)
    grad_rims = edges(grad)
    step_pred, data_curv = forward(replies)
    reg_curv = curvature(grad, grad_rims, smallness, faces)
    step = step_of(norm, data_curv, reg_curv)
    (buffer,) = tile_call(
        backward_kernel,
        "backward",
        slot_of,
        (sensitivity, step_pred, weight_sq),
        [buffer_shape],
        [],
        ((False, False, False), (True,)),
    )
    arrived = exchange(buffer)
    step_field = step[None, None, :, None]
    model = model - step_field * grad
    model_rims = [a - step_field * b for a, b in zip(model_rims, grad_rims)]
    predicted = predicted - step[None, :, None] * step_pred

    smallness, faces, reg = weights_of(model, model_rims)
    grad, replies, norm = sum_call(
        False,
        asked_ids,
        arrived,
        reg.reshape(per_owner, samples, cells_x),
        active_flat,
        data_sum,
        jnp.broadcast_to(step[:, None], (samples, cells_x)),
    )
    grad = grad.reshape(start_model.shape)
    grad_rims = edges(grad)
    step_pred, data_curv = forward(replies)
    reg_curv = curvature(grad, grad_rims, smallness, faces)
    step = step_of(norm, data_curv, reg_curv)
    model = model - step[None, None, :, None] * grad
    predicted = predicted - step[None, :, None] * step_pred
    misfit = row_mask * data_weight[:, None, :] * (predicted - observed)
    return (model, misfit)


def solution(mesh):
    return jax.shard_map(
        shards,
        mesh=mesh,
        in_specs=(
            P(("region", "survey"), None, None),
            P(("region", "survey"), None, None),
            P(("region", "survey"), None),
            P(("region", "survey")),
            P(("region", "survey"), None),
            P("region", "survey", None, None),
            P("region", "survey", None),
            P("region", "survey", None),
            P(),
        ),
        out_specs=(P("region", "survey", None, None), P(("region", "survey"), None, None)),
        check_vma=False,
    )
```

time: 422 us -> 254 us (0.60)
  blocking collectives: 77.9 us -> 10.8 us
  waiting for transfers between devices: 66.7 us -> 9.03 us
  other arithmetic: 113 us -> 61.7 us
  matrix products: 38.6 us -> 0 us
  Pallas kernels: 0 us -> 31.5 us
  local copies, waits for them, and re-layouts: 57.7 us -> 69.3 us
  starting transfers between devices: 63.5 us -> 69.3 us
    psum x2 -> x0, blocking collectives: 77.9 us -> none  [shards(): lax.psum((grad_norm, data_curv, reg_curv), ('region', 'survey'))]
    scatter-add x2 -> x0, other arithmetic: 56.7 us -> none  [return_grads(): summed.at[asked_ids.reshape(-1)].add(arrived.reshape(-1, samples, cells_x))]
    all_to_all x6 -> x7, waiting for transfers between devices: 54.2 us -> 9 us  [swap(): return lax.all_to_all(field, AXES, split_axis=0, concat_axis=0, tiled=True)]
    dot_general x5 -> x0, matrix products: 38.6 us -> none  [the longest x3 24.6 us: predict(): jnp.einsum('tdbx,tbsx->tsd', sensor_view, picked, preferred_element_type=...]
    pallas_call x0 -> x6, Pallas kernels: none -> 31.5 us  [the longest x4 23.5 us: tile_call(): pl.pallas_call(kernel, name=name, out_shape=outs, grid_spec=pltpu.Prefetc...]
    unnamed x84 -> x70, local copies, waits for them, and re-layouts: 1.49 us -> 29.1 us
    scatter x2 -> x0, local copies, waits for them, and re-layouts: 24.7 us -> none  [return_grads(): jnp.zeros((owners * capacity, samples, cells_x), jnp.float32).at[slot_of]]
    slice x7 -> x18, local copies, waits for them, and re-layouts: 11.8 us -> 35.7 us  [the longest x2 5.73 us: neighbour_list(): centre[..., 1:]]
  transfers between devices with their start and end apart: 18 -> 19, of which waited for: 10 -> 5; matrix products, arithmetic and copies ran while one was open for 20% -> 32% of each run, Pallas kernels for 0% -> 5%
where the time goes in v1:
time: 254 us; the launch traced here: 253 us
  local copies, waits for them, and re-layouts  69.3 us (27%)
  starting transfers between devices  69.3 us (27%)
  other arithmetic  61.7 us (24%)
  Pallas kernels  31.5 us (12%)
  blocking collectives  10.8 us (4%)
  waiting for transfers between devices  9.03 us (4%)
    all_to_all x7, starting transfers between devices, swap(): return lax.all_to_all(field, AXES, split_axis=0, concat_axis=0, tiled=True)  38.1 us
    unnamed x70, local copies, waits for them, and re-layouts  29.1 us
    reduce_sum x2, other arithmetic, reg_curvature(): return jnp.sum(running, axis=(0, 1, 3))  26.6 us
    pallas_call x4, Pallas kernels, tile_call(): pl.pallas_call(kernel, name=name, out_shape=outs, grid_spec=pltpu.Prefetc...  23.5 us
    ppermute x6, starting transfers between devices, edges(): rims.append(lax.ppermute(last, axis, up))  23.5 us
    mul x2, other arithmetic, weights_of(): reg_scale * reg_gradient(field, neighbours, smallness, faces)  15 us
    all_to_all x1, blocking collectives, swap(): return lax.all_to_all(field, AXES, split_axis=0, concat_axis=0, tiled=True)  10.8 us
    all_to_all x7, waiting for transfers between devices, swap(): return lax.all_to_all(field, AXES, split_axis=0, concat_axis=0, tiled=True)  9 us
  transfers between devices with their start and end apart: 19, of which 5 were waited for; matrix products, arithmetic and copies ran while one was open for 32% of the time, Pallas kernels for 5%

profile of v1, /device:TPU:0, one launch (start us, length us, event | category | flops | bytes accessed | tf_op | source)
XLA Modules:
  0.0 252.9 jit_solution(7505219349319361899)
XLA Ops:
  2.7 7.3 %all-to-all-start = ((s32[32,1,8]{2,1,0:T(1,128)}), s32[32,1,8]{2,1,0:T(1,128)S(1)}, u32[]{:S(2)}, u32[]{:S(2)}) async-start(s32[32,1,8]{2,1,0:T(1,128)} %bitcast), calls=%async_computation | async-start | bytes 32768 | tf_op jit(solution)/shard_map/all_to_all | solution.py:16
  11.0 3.3 %fusion.42 = (bf16[16,32,8,128]{3,2,1,0:T(8,128)(2,1)S(1)}, f32[16,32,8,128]{3,2,1,0:T(8,128)}) fusion(f32[16,32,8,128]{3,2,1,0:T(8,128)} %param.14, f32[16,32,128]{2,1,0:T(8,128)S(1)} %convert_element_type.44), kind=kLoop, calls=%fused_computation.164 | loop fusion | flops 1048576 | bytes 5505024 | tf_op jit(solution)/shard_map/convert_element_type | solution.py:306
  15.8 2.1 collective-permute-start.2
  19.3 1.7 fusion.54
  21.0 3.5 %collective-permute-start = (f32[1,32,8,128]{3,2,1,0:T(8,128)}, f32[1,32,8,128]{3,2,1,0:T(8,128)S(1)}, u32[]{:S(2)}, u32[]{:S(2)}) collective-permute-start(f32[1,32,8,128]{3,2,1,0:T(8,128)} %get-tuple-element.56), channel_id=1, source_target_pairs={{0,4},{4,8},{8,12},{12,16},{16,20},{20,24},{24,28},{1,5},{5,9},{9,... | collective-permute-start | bytes 393224 | tf_op jit(solution)/shard_map/ppermute | solution.py:27
  27.6 9.6 %all-to-all-start.1 = ((bf16[32,8,8,128]{3,2,1,0:T(8,128)(2,1)}), bf16[32,8,8,128]{3,2,1,0:T(8,128)(2,1)S(1)}, u32[]{:S(2)}, u32[]{:S(2)}) async-start(bf16[32,8,8,128]{3,2,1,0:T(8,128)(2,1)} %bitcast.3), calls=%async_computation.1 | async-start | bytes 1048576 | tf_op jit(solution)/shard_map/all_to_all | solution.py:16
  37.2 4.5 %fusion.55 = (f32[15,32,8,128]{3,2,1,0:T(8,128)}, f32[15,32,8,128]{3,2,1,0:T(8,128)}) fusion(f32[16,32,8,128]{3,2,1,0:T(8,128)} %get-tuple-element.29), kind=kLoop, calls=%fused_computation.177 | loop fusion | bytes 7864320 | tf_op jit(solution)/shard_map/slice | solution.py:36
  41.7 4.5 %fusion.57 = (f32[16,31,8,128]{3,2,1,0:T(8,128)}, f32[16,31,8,128]{3,2,1,0:T(8,128)}) fusion(f32[16,32,8,128]{3,2,1,0:T(8,128)} %get-tuple-element.29), kind=kLoop, calls=%fused_computation.179 | loop fusion | bytes 8126464 | tf_op jit(solution)/shard_map/slice | solution.py:38
  46.2 5.0 %fusion.58 = (f32[16,32,8,127]{3,2,1,0:T(8,128)}, f32[16,32,8,127]{3,2,1,0:T(8,128)}) fusion(f32[16,32,8,128]{3,2,1,0:T(8,128)} %get-tuple-element.29), kind=kLoop, calls=%fused_computation.180 | loop fusion | bytes 8323072 | tf_op jit(solution)/shard_map/slice | solution.py:41
  51.2 1.7 all-to-all-done.1
  52.8 5.8 %copy-done = bf16[4,512,4096]{2,1,0:T(8,128)(2,1)S(1)} copy-done((bf16[4,512,4096]{2,1,0:T(8,128)(2,1)S(1)}, bf16[4,512,4096]{2,1,0:T(8,128)(2,1)}, u32[]{:S(2)}) %copy-start) | copy-done | bytes 16777240
  58.6 8.8 %residual_pred.1 = (f32[4,8,512]{2,1,0:T(8,128)S(1)}, bf16[256,8,128]{2,1,0:T(8,128)(2,1)}) custom-call(s32[128]{0:T(128)S(1)} %multiply_add_fusion.3.slot_ref, bf16[256,8,128]{2,1,0:T(8,128)(2,1)S(1)} %bitcast.54, bf16[4,512,4096]{2,1,0:T(8,128)(2,1)S(1)} %copy-done, f32[4,8,512]{2,1,0:T(8,128)S(1)} %copy-done.9, f32[4,1,512]{2,1,0:T(1,128)S(1)} %mul.540.weight_ref), custom_call_target="tpu_custom_call" | custom-call | tf_op jit(solution)/shard_map/residual_pred/pallas_call | solution.py:153
  67.4 4.2 %all-to-all-start.2 = ((bf16[32,8,8,128]{3,2,1,0:T(8,128)(2,1)}), bf16[32,8,8,128]{3,2,1,0:T(8,128)(2,1)S(1)}, u32[]{:S(2)}, u32[]{:S(2)}) async-start(bf16[32,8,8,128]{3,2,1,0:T(8,128)(2,1)} %bitcast.5), calls=%async_computation.2 | async-start | bytes 1048576 | tf_op jit(solution)/shard_map/all_to_all | solution.py:16
  71.5 3.3 %fusion.22 = (f32[16,32,128]{2,1,0:T(8,128)S(1)}, f32[16,32,128]{2,1,0:T(8,128)}, f32[16,32,128]{2,1,0:T(8,128)}, f32[16,32,128]{2,1,0:T(8,128)}, f32[16,32,128]...) fusion(s32[16,32,128]{2,1,0:T(8,128)} %param.16, f32[16]{0:T(128)S(1)} %multiply_add_fusion.2, ...), kind=kLoop, calls=%fused_computation.108 | loop fusion | flops 8388608 | bytes 2359488 | tf_op jit(solution)/shard_map/mul | solution.py:55
  76.3 8.7 %add_multiply_fusion.1 = f32[16,32,8,128]{3,2,1,0:T(8,128)} fusion(f32[16,32,8,128]{3,2,1,0:T(8,128)} %get-tuple-element.29, f32[16,32,128]{2,1,0:T(8,128)} %get-tuple-element.69, f32[16,32,128]{2,1,0:T(8,128)} %get-tuple-element.67, f32[16,32,128]{2,1,0:T(8,128)} %get-tuple-element.68, f32[16,32,128]{2,1,0:T(8,128)S(1)} %get-tuple-element.66, ...), kind=kLoop, calls=%fused_computation.57 | loop fusion | flops 23592960 | bytes 18579488 | tf_op jit(solution)/shard_map/mul | solution.py:323
  85.0 2.2 all-to-all-done.2
  87.1 1.6 copy-done.6
  88.7 4.0 %sum_first.1 = (f32[512,8,128]{2,1,0:T(8,128)S(1)}, f32[512,8,128]{2,1,0:T(8,128)S(1)}, bf16[256,8,128]{2,1,0:T(8,128)(2,1)}, f32[8,128]{1,0:T(8,128)S(1)}) custom-call(s32[256]{0:T(256)S(1)} %reshape.235.ids_ref, bf16[256,8,128]{2,1,0:T(8,128)(2,1)S(1)} %bitcast.55, f32[512,8,128]{2,1,0:T(8,128)S(1)} %bitcast.48, f32[512,128]{1,0:T(8,128)S(1)} %bitcast.49), custom_call_target="tpu_custom_call" | custom-call | tf_op jit(solution)/shard_map/sum_first/pallas_call | solution.py:231
  94.1 2.2 fusion.51
  96.3 2.7 %fusion.50 = (f32[16,32,8,127]{3,2,1,0:T(8,128)}, f32[16,32,8,127]{3,2,1,0:T(8,128)}) fusion(f32[16,32,8,128]{3,2,1,0:T(8,128)S(1)} %bitcast.41), kind=kLoop, calls=%fused_computation.172 | loop fusion | bytes 8323072 | tf_op jit(solution)/shard_map/slice | solution.py:40
  100.3 3.7 %collective-permute-start.6 = (f32[16,1,8,128]{3,2,1,0:T(8,128)}, f32[16,1,8,128]{3,2,1,0:T(8,128)}, u32[]{:S(2)}, u32[]{:S(2)}) collective-permute-start(f32[16,1,8,128]{3,2,1,0:T(8,128)} %get-tuple-element.51), channel_id=1, source_target_pairs={{0,1},{1,2},{2,3},{4,5},{5,6},{6,7},{8,9},{9,10},{10,11},{12,13},{... | collective-permute-start | bytes 196616 | tf_op jit(solution)/shard_map/ppermute | solution.py:27
  105.3 5.2 %collective-permute-start.4 = (f32[1,32,8,128]{3,2,1,0:T(8,128)}, f32[1,32,8,128]{3,2,1,0:T(8,128)}, u32[]{:S(2)}, u32[]{:S(2)}) collective-permute-start(f32[1,32,8,128]{3,2,1,0:T(8,128)} %get-tuple-element.55), channel_id=1, source_target_pairs={{0,4},{4,8},{8,12},{12,16},{16,20},{20,24},{24,28},{1,5},{5,9},{9,... | collective-permute-start | bytes 393224 | tf_op jit(solution)/shard_map/ppermute | solution.py:27
  110.5 2.1 fusion.53
  112.6 3.1 %all-to-all-start.3 = ((bf16[32,8,8,128]{3,2,1,0:T(8,128)(2,1)}), bf16[32,8,8,128]{3,2,1,0:T(8,128)(2,1)S(1)}, u32[]{:S(2)}, u32[]{:S(2)}) async-start(bf16[32,8,8,128]{3,2,1,0:T(8,128)(2,1)} %bitcast.9), calls=%async_computation.3 | async-start | bytes 1048576 | tf_op jit(solution)/shard_map/all_to_all | solution.py:16
  115.9 13.1 %fusion.6 = f32[8]{0:T(128)S(1)} fusion(f32[16,32,8,128]{3,2,1,0:T(8,128)S(1)} %bitcast.42, f32[15,32,8,128]{3,2,1,0:T(8,128)} %bitcast.59, f32[1,32,8,128]{3,2,1,0:T(8,128)} %collective-permute-done.4, f32[1,32,8,128]{3,2,1,0:T(8,128)} %collective-permute-done.5, f32[15,32,8,128]{3,2,1,0:T(8,128)} %bitcast.58, f32[16,31,8,128]{3,2,1,0:T(8,128)} %get-tuple-element.49, ...), kind=kLoop, calls=%fused_computation.21 | loop fusion | flops 35651576 | bytes 31129632 | tf_op jit(solution)/shard_map/reduce_sum | solution.py:72
  129.0 2.4 all-to-all-done.3
  131.4 5.8 %copy-done.1 = bf16[4,512,4096]{2,1,0:T(8,128)(2,1)S(1)} copy-done((bf16[4,512,4096]{2,1,0:T(8,128)(2,1)S(1)}, bf16[4,512,4096]{2,1,0:T(8,128)(2,1)}, u32[]{:S(2)}) %copy-start.1) | copy-done | bytes 16777240
  137.2 5.3 %forward_pred.2 = (f32[4,8,512]{2,1,0:T(8,128)S(1)}, f32[8,512]{1,0:T(8,128)S(1)}) custom-call(s32[128]{0:T(128)S(1)} %multiply_add_fusion.3.slot_ref, bf16[256,8,128]{2,1,0:T(8,128)(2,1)S(1)} %bitcast.53, bf16[4,512,4096]{2,1,0:T(8,128)(2,1)S(1)} %copy-done.1, f32[4,1,512]{2,1,0:T(1,128)S(1)} %mul.540.weight_ref), custom_call_target="tpu_custom_call" | custom-call | tf_op jit(solution)/shard_map/forward_pred/pallas_call | solution.py:153
  143.3 3.4 %all-to-all-start.4 = ((f32[32,1,128]{2,1,0:T(1,128)}), f32[32,1,128]{2,1,0:T(1,128)S(1)}, u32[]{:S(2)}, u32[]{:S(2)}) async-start(f32[32,1,128]{2,1,0:T(1,128)} %broadcast_in_dim.20), calls=%async_computation.4 | async-start | bytes 32768 | tf_op jit(solution)/shard_map/all_to_all | solution.py:16
  146.8 5.8 %copy-done.2 = bf16[4,512,4096]{2,1,0:T(8,128)(2,1)S(1)} copy-done((bf16[4,512,4096]{2,1,0:T(8,128)(2,1)S(1)}, bf16[4,512,4096]{2,1,0:T(8,128)(2,1)}, u32[]{:S(2)}) %copy-start.2) | copy-done | bytes 16777240
  152.6 4.1 %backward.1 = bf16[256,8,128]{2,1,0:T(8,128)(2,1)} custom-call(s32[128]{0:T(128)S(1)} %multiply_add_fusion.3.slot_ref, bf16[4,512,4096]{2,1,0:T(8,128)(2,1)S(1)} %copy-done.2, f32[4,8,512]{2,1,0:T(8,128)S(1)} %get-tuple-element.20.pred_ref, f32[4,1,512]{2,1,0:T(1,128)S(1)} %mul.540.weight_ref), custom_call_target="tpu_custom_call" | custom-call | tf_op jit(solution)/shard_map/backward/pallas_call | solution.py:153
  156.6 5.8 %all-to-all-start.5 = ((bf16[32,8,8,128]{3,2,1,0:T(8,128)(2,1)}), bf16[32,8,8,128]{3,2,1,0:T(8,128)(2,1)S(1)}, u32[]{:S(2)}, u32[]{:S(2)}) async-start(bf16[32,8,8,128]{3,2,1,0:T(8,128)(2,1)} %bitcast.17), calls=%async_computation.5 | async-start | bytes 1048576 | tf_op jit(solution)/shard_map/all_to_all | solution.py:16
  162.6 1.9 multiply_subtract_fusion.1
  166.7 2.4 multiply_subtract_fusion.3
  171.0 6.3 %add_multiply_fusion = f32[16,32,8,128]{3,2,1,0:T(8,128)} fusion(f32[16,32,128]{2,1,0:T(8,128)S(1)} %copy-done.21, f32[16,32,128]{2,1,0:T(8,128)S(1)} %copy-done.18, f32[16,32,128]{2,1,0:T(8,128)S(1)} %copy-done.20, f32[16,32,128]{2,1,0:T(8,128)S(1)} %get-tuple-element.66, f32[16,32,128]{2,1,0:T(8,128)S(1)} %copy-done.23, f32[16,32,128]{2,1,0:T(8,128)S(1)} %copy-done.22, ...), kind=kLoop, calls=%fused_computation.46 | loop fusion | flops 24641536 | bytes 20676672 | tf_op jit(solution)/shard_map/mul | solution.py:323
  181.4 4.0 %sum_next.1 = (f32[512,8,128]{2,1,0:T(8,128)S(1)}, bf16[256,8,128]{2,1,0:T(8,128)(2,1)}, f32[8,128]{1,0:T(8,128)S(1)}) custom-call(s32[256]{0:T(256)S(1)} %reshape.235.ids_ref, bf16[256,8,128]{2,1,0:T(8,128)(2,1)S(1)} %bitcast.52, f32[512,8,128]{2,1,0:T(8,128)S(1)} %bitcast.47, f32[512,128]{1,0:T(8,128)S(1)} %bitcast.50, f32[512,8,128]{2,1,0:T(8,128)S(1)} %copy-done.8, ...), custom_call_target="tpu_custom_call" | custom-call | tf_op jit(solution)/shard_map/sum_next/pallas_call | solution.py:231
  186.8 2.3 fusion.44
  189.1 2.7 %fusion.43 = (f32[16,32,8,127]{3,2,1,0:T(8,128)}, f32[16,32,8,127]{3,2,1,0:T(8,128)}) fusion(f32[16,32,8,128]{3,2,1,0:T(8,128)S(1)} %bitcast.45), kind=kLoop, calls=%fused_computation.165 | loop fusion | bytes 8323072 | tf_op jit(solution)/shard_map/slice | solution.py:40
  193.1 3.7 %collective-permute-start.10 = (f32[16,1,8,128]{3,2,1,0:T(8,128)}, f32[16,1,8,128]{3,2,1,0:T(8,128)}, u32[]{:S(2)}, u32[]{:S(2)}) collective-permute-start(f32[16,1,8,128]{3,2,1,0:T(8,128)} %get-tuple-element.35), channel_id=1, source_target_pairs={{0,1},{1,2},{2,3},{4,5},{5,6},{6,7},{8,9},{9,10},{10,11},{12,13},{... | collective-permute-start | bytes 196616 | tf_op jit(solution)/shard_map/ppermute | solution.py:27
  198.1 5.3 %collective-permute-start.8 = (f32[1,32,8,128]{3,2,1,0:T(8,128)}, f32[1,32,8,128]{3,2,1,0:T(8,128)}, u32[]{:S(2)}, u32[]{:S(2)}) collective-permute-start(f32[1,32,8,128]{3,2,1,0:T(8,128)} %get-tuple-element.39), channel_id=1, source_target_pairs={{0,4},{4,8},{8,12},{12,16},{16,20},{20,24},{24,28},{1,5},{5,9},{9,... | collective-permute-start | bytes 393224 | tf_op jit(solution)/shard_map/ppermute | solution.py:27
  203.4 2.2 fusion.46
  205.7 4.6 %all-to-all-start.6 = ((bf16[32,8,8,128]{3,2,1,0:T(8,128)(2,1)}), bf16[32,8,8,128]{3,2,1,0:T(8,128)(2,1)S(1)}, u32[]{:S(2)}, u32[]{:S(2)}) async-start(bf16[32,8,8,128]{3,2,1,0:T(8,128)(2,1)} %bitcast.20), calls=%async_computation.6 | async-start | bytes 1048576 | tf_op jit(solution)/shard_map/all_to_all | solution.py:16
  210.4 13.5 %fusion.13 = f32[8]{0:T(128)S(1)} fusion(f32[16,32,8,128]{3,2,1,0:T(8,128)} %bitcast.46, f32[15,32,8,128]{3,2,1,0:T(8,128)} %bitcast.57, f32[1,32,8,128]{3,2,1,0:T(8,128)} %collective-permute-done.8, f32[1,32,8,128]{3,2,1,0:T(8,128)} %collective-permute-done.9, f32[15,32,8,128]{3,2,1,0:T(8,128)} %bitcast.56, f32[16,31,8,128]{3,2,1,0:T(8,128)} %get-tuple-element.33, ...), kind=kLoop, calls=%fused_computation.28 | loop fusion | flops 35651576 | bytes 31129632 | tf_op jit(solution)/shard_map/reduce_sum | solution.py:72
  223.9 2.0 all-to-all-done.6
  225.9 5.8 %copy-done.3 = bf16[4,512,4096]{2,1,0:T(8,128)(2,1)S(1)} copy-done((bf16[4,512,4096]{2,1,0:T(8,128)(2,1)S(1)}, bf16[4,512,4096]{2,1,0:T(8,128)(2,1)}, u32[]{:S(2)}) %copy-start.3) | copy-done | bytes 16777240
  231.7 5.3 %forward_pred.3 = (f32[4,8,512]{2,1,0:T(8,128)S(1)}, f32[8,512]{1,0:T(8,128)S(1)}) custom-call(s32[128]{0:T(128)S(1)} %multiply_add_fusion.3.slot_ref, bf16[256,8,128]{2,1,0:T(8,128)(2,1)S(1)} %bitcast.51, bf16[4,512,4096]{2,1,0:T(8,128)(2,1)S(1)} %copy-done.3, f32[4,1,512]{2,1,0:T(1,128)S(1)} %mul.540.weight_ref), custom_call_target="tpu_custom_call" | custom-call | tf_op jit(solution)/shard_map/forward_pred/pallas_call | solution.py:153
  237.3 10.8 %all_to_all.44 = f32[32,1,128]{2,1,0:T(1,128)S(1)} all-to-all(f32[32,1,128]{2,1,0:T(1,128)S(1)} %broadcast_in_dim.22), channel_id=1, replica_groups=mesh['region'=8,'survey'=4] {'region','survey'}, dimensions={0} | all-to-all | bytes 32768 | tf_op jit(solution)/shard_map/all_to_all | solution.py:16
  248.2 4.0 %multiply_subtract_fusion = f32[16,32,8,128]{3,2,1,0:T(8,128)} fusion(f32[8]{0:T(128)S(1)} %add_divide_fusion, f32[512,8,128]{2,1,0:T(8,128)} %copy-done.4, f32[16,32,8,128]{3,2,1,0:T(8,128)} %get-tuple-element.29, f32[512,8,128]{2,1,0:T(8,128)S(1)} %get-tuple-element.19, f32[8]{0:T(128)S(1)} %add_divide_fusion.1), kind=kLoop, calls=%fused_computation.45 | loop fusion | flops 2097152 | bytes 8388672 | tf_op jit(solution)/shard_map/sub | solution.py:394
  (129 shorter events, 28.4 us)
Async XLA Ops:
  2.7 23.3 %all-to-all-start = ((s32[32,1,8]{2,1,0:T(1,128)}), s32[32,1,8]{2,1,0:T(1,128)S(1)}, u32[]{:S(2)}, u32[]{:S(2)}) async-start(s32[32,1,8]{2,1,0:T(1,128)} %bitcast), calls=%async_computation | async-start | bytes 32768 | tf_op jit(solution)/shard_map/all_to_all | solution.py:16
  11.0 14.8 %copy-start.33 = (f32[4,512]{1,0:T(4,128)S(1)}, f32[4,512]{1,0:T(4,128)}, u32[]{:S(2)}) copy-start(f32[4,512]{1,0:T(4,128)} %param.11) | copy-start | bytes 24580
  11.0 14.8 %copy-start.34 = (s32[4]{0:T(128)S(1)}, s32[4]{0:T(128)}, u32[]{:S(2)}) copy-start(s32[4]{0:T(128)} %param.12) | copy-start | bytes 52
  15.8 60.4 %collective-permute-start.2 = (f32[16,1,8,128]{3,2,1,0:T(8,128)}, f32[16,1,8,128]{3,2,1,0:T(8,128)S(1)}, u32[]{:S(2)}, u32[]{:S(2)}) collective-permute-start(f32[16,1,8,128]{3,2,1,0:T(8,128)} %get-tuple-element.60), channel_id=1, source_target_pairs={{0,1},{1,2},{2,3},{4,5},{5,6},{6,7},{8,9},{9,10},{10,11},{12,13},{... | collective-permute-start | bytes 196616 | tf_op jit(solution)/shard_map/ppermute | solution.py:27
  18.0 58.2 %collective-permute-start.3 = (f32[16,1,8,128]{3,2,1,0:T(8,128)}, f32[16,1,8,128]{3,2,1,0:T(8,128)}, u32[]{:S(2)}, u32[]{:S(2)}) collective-permute-start(f32[16,1,8,128]{3,2,1,0:T(8,128)} %get-tuple-element.61), channel_id=1, source_target_pairs={{1,0},{2,1},{3,2},{5,4},{6,5},{7,6},{9,8},{10,9},{11,10},{13,12},{... | collective-permute-start | bytes 196616 | tf_op jit(solution)/shard_map/ppermute | solution.py:28
  21.0 55.3 %collective-permute-start = (f32[1,32,8,128]{3,2,1,0:T(8,128)}, f32[1,32,8,128]{3,2,1,0:T(8,128)S(1)}, u32[]{:S(2)}, u32[]{:S(2)}) collective-permute-start(f32[1,32,8,128]{3,2,1,0:T(8,128)} %get-tuple-element.56), channel_id=1, source_target_pairs={{0,4},{4,8},{8,12},{12,16},{16,20},{20,24},{24,28},{1,5},{5,9},{9,... | collective-permute-start | bytes 393224 | tf_op jit(solution)/shard_map/ppermute | solution.py:27
  24.5 51.7 %collective-permute-start.1 = (f32[1,32,8,128]{3,2,1,0:T(8,128)}, f32[1,32,8,128]{3,2,1,0:T(8,128)}, u32[]{:S(2)}, u32[]{:S(2)}) collective-permute-start(f32[1,32,8,128]{3,2,1,0:T(8,128)} %get-tuple-element.57), channel_id=1, source_target_pairs={{4,0},{8,4},{12,8},{16,12},{20,16},{24,20},{28,24},{5,1},{9,5},{13... | collective-permute-start | bytes 393224 | tf_op jit(solution)/shard_map/ppermute | solution.py:28
  27.6 25.2 %all-to-all-start.1 = ((bf16[32,8,8,128]{3,2,1,0:T(8,128)(2,1)}), bf16[32,8,8,128]{3,2,1,0:T(8,128)(2,1)S(1)}, u32[]{:S(2)}, u32[]{:S(2)}) async-start(bf16[32,8,8,128]{3,2,1,0:T(8,128)(2,1)} %bitcast.3), calls=%async_computation.1 | async-start | bytes 1048576 | tf_op jit(solution)/shard_map/all_to_all | solution.py:16
  46.2 6.7 %copy-start.9 = (f32[4,8,512]{2,1,0:T(8,128)S(1)}, f32[4,8,512]{2,1,0:T(8,128)}, u32[]{:S(2)}) copy-start(f32[4,8,512]{2,1,0:T(8,128)} %observed_ref.1) | copy-start | bytes 196612
  52.8 5.8 %copy-start = (bf16[4,512,4096]{2,1,0:T(8,128)(2,1)S(1)}, bf16[4,512,4096]{2,1,0:T(8,128)(2,1)}, u32[]{:S(2)}) copy-start(bf16[4,512,4096]{2,1,0:T(8,128)(2,1)} %sensor_ref.7) | copy-start | bytes 50331652
  67.4 8.9 %copy-start.11 = (f32[16,32,8,127]{3,2,1,0:T(8,128)S(1)}, f32[16,32,8,127]{3,2,1,0:T(8,128)}, u32[]{:S(2)}) copy-start(f32[16,32,8,127]{3,2,1,0:T(8,128)} %get-tuple-element.64) | copy-start | bytes 6242308
  67.4 8.9 %copy-start.32 = (f32[8]{0:T(128)S(1)}, f32[8]{0:T(128)}, u32[]{:S(2)}) copy-start(f32[8]{0:T(128)} %param.17) | copy-start | bytes 100
  67.4 19.8 %all-to-all-start.2 = ((bf16[32,8,8,128]{3,2,1,0:T(8,128)(2,1)}), bf16[32,8,8,128]{3,2,1,0:T(8,128)(2,1)S(1)}, u32[]{:S(2)}, u32[]{:S(2)}) async-start(bf16[32,8,8,128]{3,2,1,0:T(8,128)(2,1)} %bitcast.5), calls=%async_computation.2 | async-start | bytes 1048576 | tf_op jit(solution)/shard_map/all_to_all | solution.py:16
  76.2 39.7 %copy-start.28 = (f32[16,1,8,128]{3,2,1,0:T(8,128)}, f32[16,1,8,128]{3,2,1,0:T(8,128)S(1)}, u32[]{:S(2)}) copy-start(f32[16,1,8,128]{3,2,1,0:T(8,128)S(1)} %collective-permute-done.2) | copy-start | bytes 196612
  87.1 1.6 copy-start.6
  92.7 3.6 %copy-start.7 = (f32[512,8,128]{2,1,0:T(8,128)}, f32[512,8,128]{2,1,0:T(8,128)S(1)}, u32[]{:S(2)}) copy-start(f32[512,8,128]{2,1,0:T(8,128)S(1)} %get-tuple-element.21.refs_0_) | copy-start | bytes 6291460
  99.1 16.8 %collective-permute-start.7 = (f32[16,1,8,128]{3,2,1,0:T(8,128)}, f32[16,1,8,128]{3,2,1,0:T(8,128)}, u32[]{:S(2)}, u32[]{:S(2)}) collective-permute-start(f32[16,1,8,128]{3,2,1,0:T(8,128)} %get-tuple-element.50), channel_id=1, source_target_pairs={{1,0},{2,1},{3,2},{5,4},{6,5},{7,6},{9,8},{10,9},{11,10},{13,12},{... | collective-permute-start | bytes 196616 | tf_op jit(solution)/shard_map/ppermute | solution.py:28
  100.3 15.6 %collective-permute-start.6 = (f32[16,1,8,128]{3,2,1,0:T(8,128)}, f32[16,1,8,128]{3,2,1,0:T(8,128)}, u32[]{:S(2)}, u32[]{:S(2)}) collective-permute-start(f32[16,1,8,128]{3,2,1,0:T(8,128)} %get-tuple-element.51), channel_id=1, source_target_pairs={{0,1},{1,2},{2,3},{4,5},{5,6},{6,7},{8,9},{9,10},{10,11},{12,13},{... | collective-permute-start | bytes 196616 | tf_op jit(solution)/shard_map/ppermute | solution.py:27
  104.0 11.9 %collective-permute-start.5 = (f32[1,32,8,128]{3,2,1,0:T(8,128)}, f32[1,32,8,128]{3,2,1,0:T(8,128)}, u32[]{:S(2)}, u32[]{:S(2)}) collective-permute-start(f32[1,32,8,128]{3,2,1,0:T(8,128)} %get-tuple-element.54), channel_id=1, source_target_pairs={{4,0},{8,4},{12,8},{16,12},{20,16},{24,20},{28,24},{5,1},{9,5},{13... | collective-permute-start | bytes 393224 | tf_op jit(solution)/shard_map/ppermute | solution.py:28
  105.3 10.6 %collective-permute-start.4 = (f32[1,32,8,128]{3,2,1,0:T(8,128)}, f32[1,32,8,128]{3,2,1,0:T(8,128)}, u32[]{:S(2)}, u32[]{:S(2)}) collective-permute-start(f32[1,32,8,128]{3,2,1,0:T(8,128)} %get-tuple-element.55), channel_id=1, source_target_pairs={{0,4},{4,8},{8,12},{12,16},{16,20},{20,24},{24,28},{1,5},{5,9},{9,... | collective-permute-start | bytes 393224 | tf_op jit(solution)/shard_map/ppermute | solution.py:27
  112.6 18.8 %all-to-all-start.3 = ((bf16[32,8,8,128]{3,2,1,0:T(8,128)(2,1)}), bf16[32,8,8,128]{3,2,1,0:T(8,128)(2,1)S(1)}, u32[]{:S(2)}, u32[]{:S(2)}) async-start(bf16[32,8,8,128]{3,2,1,0:T(8,128)(2,1)} %bitcast.9), calls=%async_computation.3 | async-start | bytes 1048576 | tf_op jit(solution)/shard_map/all_to_all | solution.py:16
  131.4 5.8 %copy-start.1 = (bf16[4,512,4096]{2,1,0:T(8,128)(2,1)S(1)}, bf16[4,512,4096]{2,1,0:T(8,128)(2,1)}, u32[]{:S(2)}) copy-start(bf16[4,512,4096]{2,1,0:T(8,128)(2,1)} %sensor_ref.7) | copy-start | bytes 50331652
  143.3 13.3 %all-to-all-start.4 = ((f32[32,1,128]{2,1,0:T(1,128)}), f32[32,1,128]{2,1,0:T(1,128)S(1)}, u32[]{:S(2)}, u32[]{:S(2)}) async-start(f32[32,1,128]{2,1,0:T(1,128)} %broadcast_in_dim.20), calls=%async_computation.4 | async-start | bytes 32768 | tf_op jit(solution)/shard_map/all_to_all | solution.py:16
  146.8 5.8 %copy-start.2 = (bf16[4,512,4096]{2,1,0:T(8,128)(2,1)S(1)}, bf16[4,512,4096]{2,1,0:T(8,128)(2,1)}, u32[]{:S(2)}) copy-start(bf16[4,512,4096]{2,1,0:T(8,128)(2,1)} %sensor_ref.7) | copy-start | bytes 50331652
  156.6 21.5 %all-to-all-start.5 = ((bf16[32,8,8,128]{3,2,1,0:T(8,128)(2,1)}), bf16[32,8,8,128]{3,2,1,0:T(8,128)(2,1)S(1)}, u32[]{:S(2)}, u32[]{:S(2)}) async-start(bf16[32,8,8,128]{3,2,1,0:T(8,128)(2,1)} %bitcast.17), calls=%async_computation.5 | async-start | bytes 1048576 | tf_op jit(solution)/shard_map/all_to_all | solution.py:16
  164.9 5.4 %copy-start.16 = (f32[15,32,8,128]{3,2,1,0:T(8,128)}, f32[15,32,8,128]{3,2,1,0:T(8,128)S(1)}, u32[]{:S(2)}) copy-start(f32[15,32,8,128]{3,2,1,0:T(8,128)S(1)} %get-tuple-element.40) | copy-start | bytes 5898244
  164.9 5.4 %copy-start.17 = (f32[15,32,8,128]{3,2,1,0:T(8,128)}, f32[15,32,8,128]{3,2,1,0:T(8,128)S(1)}, u32[]{:S(2)}) copy-start(f32[15,32,8,128]{3,2,1,0:T(8,128)S(1)} %get-tuple-element.41) | copy-start | bytes 5898244
  165.8 4.6 %copy-start.14 = (f32[16,31,8,128]{3,2,1,0:T(8,128)}, f32[16,31,8,128]{3,2,1,0:T(8,128)S(1)}, u32[]{:S(2)}) copy-start(f32[16,31,8,128]{3,2,1,0:T(8,128)S(1)} %get-tuple-element.42) | copy-start | bytes 6094852
  165.8 4.6 %copy-start.15 = (f32[16,31,8,128]{3,2,1,0:T(8,128)}, f32[16,31,8,128]{3,2,1,0:T(8,128)S(1)}, u32[]{:S(2)}) copy-start(f32[16,31,8,128]{3,2,1,0:T(8,128)S(1)} %get-tuple-element.43) | copy-start | bytes 6094852
  165.8 3.3 %copy-start.29 = (f32[16,1,8,128]{3,2,1,0:T(8,128)S(1)}, f32[16,1,8,128]{3,2,1,0:T(8,128)}, u32[]{:S(2)}) copy-start(f32[16,1,8,128]{3,2,1,0:T(8,128)} %copy-done.28) | copy-start | bytes 196612
  165.8 5.2 %copy-start.18 = (f32[16,32,128]{2,1,0:T(8,128)S(1)}, f32[16,32,128]{2,1,0:T(8,128)}, u32[]{:S(2)}) copy-start(f32[16,32,128]{2,1,0:T(8,128)} %get-tuple-element.67) | copy-start | bytes 786436
  165.8 5.2 %copy-start.20 = (f32[16,32,128]{2,1,0:T(8,128)S(1)}, f32[16,32,128]{2,1,0:T(8,128)}, u32[]{:S(2)}) copy-start(f32[16,32,128]{2,1,0:T(8,128)} %get-tuple-element.68) | copy-start | bytes 786436
  165.9 5.2 %copy-start.21 = (f32[16,32,128]{2,1,0:T(8,128)S(1)}, f32[16,32,128]{2,1,0:T(8,128)}, u32[]{:S(2)}) copy-start(f32[16,32,128]{2,1,0:T(8,128)} %get-tuple-element.69) | copy-start | bytes 786436
  165.9 5.2 %copy-start.22 = (f32[16,32,128]{2,1,0:T(8,128)S(1)}, f32[16,32,128]{2,1,0:T(8,128)}, u32[]{:S(2)}) copy-start(f32[16,32,128]{2,1,0:T(8,128)} %get-tuple-element.70) | copy-start | bytes 786436
  165.9 5.1 %copy-start.23 = (f32[16,32,128]{2,1,0:T(8,128)S(1)}, f32[16,32,128]{2,1,0:T(8,128)}, u32[]{:S(2)}) copy-start(f32[16,32,128]{2,1,0:T(8,128)} %get-tuple-element.71) | copy-start | bytes 786436
  165.9 5.1 %copy-start.24 = (f32[16,32,128]{2,1,0:T(8,128)S(1)}, f32[16,32,128]{2,1,0:T(8,128)}, u32[]{:S(2)}) copy-start(f32[16,32,128]{2,1,0:T(8,128)} %get-tuple-element.74) | copy-start | bytes 786436
  166.7 3.8 %copy-start.12 = (f32[16,32,8,127]{3,2,1,0:T(8,128)}, f32[16,32,8,127]{3,2,1,0:T(8,128)S(1)}, u32[]{:S(2)}) copy-start(f32[16,32,8,127]{3,2,1,0:T(8,128)S(1)} %get-tuple-element.44) | copy-start | bytes 6242308
  166.7 3.8 %copy-start.13 = (f32[16,32,8,127]{3,2,1,0:T(8,128)}, f32[16,32,8,127]{3,2,1,0:T(8,128)S(1)}, u32[]{:S(2)}) copy-start(f32[16,32,8,127]{3,2,1,0:T(8,128)S(1)} %get-tuple-element.45) | copy-start | bytes 6242308
  178.2 1.6 copy-start.5
  185.4 18.0 %copy-start.4 = (f32[512,8,128]{2,1,0:T(8,128)}, f32[512,8,128]{2,1,0:T(8,128)S(1)}, u32[]{:S(2)}) copy-start(f32[512,8,128]{2,1,0:T(8,128)S(1)} %get-tuple-element.25) | copy-start | bytes 6291460
  191.8 18.5 %collective-permute-start.11 = (f32[16,1,8,128]{3,2,1,0:T(8,128)}, f32[16,1,8,128]{3,2,1,0:T(8,128)}, u32[]{:S(2)}, u32[]{:S(2)}) collective-permute-start(f32[16,1,8,128]{3,2,1,0:T(8,128)} %get-tuple-element.34), channel_id=1, source_target_pairs={{1,0},{2,1},{3,2},{5,4},{6,5},{7,6},{9,8},{10,9},{11,10},{13,12},{... | collective-permute-start | bytes 196616 | tf_op jit(solution)/shard_map/ppermute | solution.py:28
  193.1 17.2 %collective-permute-start.10 = (f32[16,1,8,128]{3,2,1,0:T(8,128)}, f32[16,1,8,128]{3,2,1,0:T(8,128)}, u32[]{:S(2)}, u32[]{:S(2)}) collective-permute-start(f32[16,1,8,128]{3,2,1,0:T(8,128)} %get-tuple-element.35), channel_id=1, source_target_pairs={{0,1},{1,2},{2,3},{4,5},{5,6},{6,7},{8,9},{9,10},{10,11},{12,13},{... | collective-permute-start | bytes 196616 | tf_op jit(solution)/shard_map/ppermute | solution.py:27
  196.8 13.6 %collective-permute-start.9 = (f32[1,32,8,128]{3,2,1,0:T(8,128)}, f32[1,32,8,128]{3,2,1,0:T(8,128)}, u32[]{:S(2)}, u32[]{:S(2)}) collective-permute-start(f32[1,32,8,128]{3,2,1,0:T(8,128)} %get-tuple-element.38), channel_id=1, source_target_pairs={{4,0},{8,4},{12,8},{16,12},{20,16},{24,20},{28,24},{5,1},{9,5},{13... | collective-permute-start | bytes 393224 | tf_op jit(solution)/shard_map/ppermute | solution.py:28
  198.0 12.3 %copy-start.19 = (f32[16,32,128]{2,1,0:T(8,128)S(1)}, f32[16,32,128]{2,1,0:T(8,128)}, u32[]{:S(2)}) copy-start(f32[16,32,128]{2,1,0:T(8,128)} %get-tuple-element.67) | copy-start | bytes 786436
  198.0 12.3 %copy-start.26 = (f32[1,32,8,128]{3,2,1,0:T(8,128)S(1)}, f32[1,32,8,128]{3,2,1,0:T(8,128)}, u32[]{:S(2)}) copy-start(f32[1,32,8,128]{3,2,1,0:T(8,128)} %copy-done.25) | copy-start | bytes 393220
  198.1 12.3 %collective-permute-start.8 = (f32[1,32,8,128]{3,2,1,0:T(8,128)}, f32[1,32,8,128]{3,2,1,0:T(8,128)}, u32[]{:S(2)}, u32[]{:S(2)}) collective-permute-start(f32[1,32,8,128]{3,2,1,0:T(8,128)} %get-tuple-element.39), channel_id=1, source_target_pairs={{0,4},{4,8},{8,12},{12,16},{16,20},{20,24},{24,28},{1,5},{5,9},{9,... | collective-permute-start | bytes 393224 | tf_op jit(solution)/shard_map/ppermute | solution.py:27
  205.7 20.3 %all-to-all-start.6 = ((bf16[32,8,8,128]{3,2,1,0:T(8,128)(2,1)}), bf16[32,8,8,128]{3,2,1,0:T(8,128)(2,1)S(1)}, u32[]{:S(2)}, u32[]{:S(2)}) async-start(bf16[32,8,8,128]{3,2,1,0:T(8,128)(2,1)} %bitcast.20), calls=%async_computation.6 | async-start | bytes 1048576 | tf_op jit(solution)/shard_map/all_to_all | solution.py:16
  225.9 5.8 %copy-start.3 = (bf16[4,512,4096]{2,1,0:T(8,128)(2,1)S(1)}, bf16[4,512,4096]{2,1,0:T(8,128)(2,1)}, u32[]{:S(2)}) copy-start(bf16[4,512,4096]{2,1,0:T(8,128)(2,1)} %sensor_ref.7) | copy-start | bytes 50331652
  (6 other events, 6.8 us)

commit v2 on v1

v2 whole, which is shorter than its diff:
```python
import functools

import jax
import jax.numpy as jnp
from jax import lax
from jax.experimental import pallas as pl
from jax.experimental.pallas import tpu as pltpu
from jax.sharding import PartitionSpec as P


AXES = ("region", "survey")
EPS_SQ = 0.09
KERNEL_VMEM = 32 * 1024 * 1024
PART = 256


def swap(field):
    return lax.all_to_all(field, AXES, split_axis=0, concat_axis=0, tiled=True)


def outer(field):
    return [field[0], field[-1], field[:, 0], field[:, -1]]


def edges(parts, both=True):
    rims = [[], []]
    for axis, (first, last) in (("region", parts[:2]), ("survey", parts[2:])):
        count = lax.axis_size(axis)
        rims[0].append(lax.ppermute(first, axis, [(i + 1, i) for i in range(count - 1)]))
        if both:
            rims[1].append(lax.ppermute(last, axis, [(i, i + 1) for i in range(count - 1)]))
    return rims[0] + rims[1]


def start_pads(field_ref, pad, next_refs, sem):
    layers, rows = field_ref.shape[:2]
    copy = pltpu.make_async_copy(field_ref, pad.at[pl.ds(0, layers), pl.ds(0, rows)], sem)
    copy.start()
    pad[layers, pl.ds(0, rows)] = next_refs[0][...].astype(pad.dtype)
    for layer in range(layers):
        pad[layer, rows] = next_refs[1][layer].astype(pad.dtype)
    return copy


def face(here, there, link):
    difference = here - there
    return difference, link * lax.rsqrt(difference * difference + EPS_SQ)


def levels(base, layer, depth_count):
    depth = (base + layer).astype(jnp.float32)
    return [1.0 + (2.0 * depth + offset) / depth_count for offset in (-1.0, 0.0, 1.0)]


def link_of(codes, number, level):
    return (lax.shift_right_logical(codes, number) & 1).astype(jnp.float32) * level


def next_lane(value):
    return pltpu.roll(value, value.shape[-1] - 1, value.ndim - 1)


def reg_kernel(first, depth_count, base_ref, links_ref, active_ref, scale_ref, field_ref, *refs):
    if first:
        below, right, above, left, reg_ref, out, pad, flow, sems = refs
    else:
        below, right, above, left, step_ref, grad_ref, *refs = refs
        gbelow, gright, gabove, gleft, reg_ref, new_ref, nbelow, nright, *refs = refs
        out, pad, flow, sems, gpad = refs
        step = step_ref[...]
    layers, rows = field_ref.shape[:2]
    group = 8
    base = base_ref[0]
    scale = scale_ref[...]
    copies = [start_pads(field_ref, pad, (below, right), sems.at[0])]
    if not first:
        copies.append(start_pads(grad_ref, gpad, (gbelow, gright), sems.at[1]))
    for copy in copies:
        copy.wait()
    if not first:

        def move(layer, carry):
            for row in range(rows + 1):
                pad[layer, row] = pad[layer, row] - step * gpad[layer, row]
            return carry

        lax.fori_loop(0, layers, move, 0)
        for row in range(rows):
            pad[layers, row] = pad[layers, row] - step * gpad[layers, row]
        nbelow[...] = pad[layers, pl.ds(0, rows)]
        for layer in range(layers):
            nright[layer] = pad[layer, rows]
        store = pltpu.make_async_copy(
            pad.at[pl.ds(0, layers), pl.ds(0, rows)], new_ref, sems.at[2]
        )
        store.start()
    lane = lax.broadcasted_iota(jnp.int32, (group, pad.shape[-1]), 1)
    inner = (lane < pad.shape[-1] - 1).astype(jnp.float32)

    def prior(ref, gref, index):
        value = ref[index]
        if first:
            return value
        return value - step * gref[index].astype(jnp.float32)

    for start in range(0, rows, group):
        codes = links_ref[pl.ds(start, group), :]
        link = link_of(codes, 0, levels(base, 0, depth_count)[0])
        for k in range(group):
            row = start + k
            came = prior(above, None if first else gabove, row)
            difference, weight = face(came, pad[0, row], link[k : k + 1])
            flow[row] = weight * difference

    def one(layer, carry):
        _, level, level_below = levels(base, layer, depth_count)
        flow_y = None
        for start in range(0, rows, group):
            place = pl.ds(pl.multiple_of(layer * rows + start, group), group)
            codes = links_ref[place, :]
            link_z = link_of(codes, 1, level_below)
            link_y = link_of(codes, 3, level)
            link_x = link_of(codes, 5, level) * inner
            live = active_ref[place, :] * level
            if start == 0:
                came = prior(left, None if first else gleft, layer)
                link = link_of(codes, 2, level)
                difference, weight = face(came, pad[layer, 0], link[:1])
                flow_y = weight * difference
            for k in range(group):
                row = start + k
                one_row = slice(k, k + 1)
                here = pad[layer, row]
                total = live[one_row] * lax.rsqrt(here * here + EPS_SQ) * here
                difference, weight = face(here, next_lane(here), link_x[one_row])
                flow_x = weight * difference
                total = total + flow_x - pltpu.roll(flow_x, 1, 1)
                difference, weight = face(here, pad[layer, row + 1], link_y[one_row])
                out_y = weight * difference
                total = total + out_y - flow_y
                flow_y = out_y
                difference, weight = face(here, pad[layer + 1, row], link_z[one_row])
                out_z = weight * difference
                total = total + out_z - flow[row]
                flow[row] = out_z
                out[layer, row] = scale * total
        return carry

    lax.fori_loop(0, layers, one, 0)
    final = pltpu.make_async_copy(out, reg_ref, sems.at[3])
    final.start()
    final.wait()
    if not first:
        store.wait()


def curvature_kernel(
    depth_count, base_ref, links_ref, active_ref, field_ref, below, right, grad_ref, gbelow,
    gright, curv_ref, pad, gpad, sems
):
    layers, rows = field_ref.shape[:2]
    group = 8
    base = base_ref[0]
    copies = [
        start_pads(field_ref, pad, (below, right), sems.at[0]),
        start_pads(grad_ref, gpad, (gbelow, gright), sems.at[1]),
    ]
    for copy in copies:
        copy.wait()
    lane = lax.broadcasted_iota(jnp.int32, (group, pad.shape[-1]), 1)
    inner = (lane < pad.shape[-1] - 1).astype(jnp.float32)

    def one(layer, total):
        _, level, level_below = levels(base, layer, depth_count)
        for start in range(0, rows, group):
            place = pl.ds(pl.multiple_of(layer * rows + start, group), group)
            codes = links_ref[place, :]
            link_z = link_of(codes, 1, level_below)
            link_y = link_of(codes, 3, level)
            link_x = link_of(codes, 5, level) * inner
            live = active_ref[place, :] * level
            for k in range(group):
                row = start + k
                one_row = slice(k, k + 1)
                here = pad[layer, row]
                slope = gpad[layer, row]
                part = live[one_row] * lax.rsqrt(here * here + EPS_SQ) * slope * slope
                for there, gthere, link in (
                    (next_lane(here), next_lane(slope), link_x),
                    (pad[layer, row + 1], gpad[layer, row + 1], link_y),
                    (pad[layer + 1, row], gpad[layer + 1, row], link_z),
                ):
                    _, weight = face(here, there, link[one_row])
                    change = slope - gthere
                    part = part + weight * change * change
                total = total + part
        return total

    curv_ref[...] = lax.fori_loop(0, layers, one, jnp.zeros(curv_ref.shape, jnp.float32))


def grid_call(kernel, base, operands, apart, outs, outs_apart, scratch):
    whole = pl.BlockSpec(memory_space=pltpu.VMEM)
    far = pl.BlockSpec(memory_space=pltpu.HBM)
    return pl.pallas_call(
        kernel,
        out_shape=outs,
        grid_spec=pltpu.PrefetchScalarGridSpec(
            num_scalar_prefetch=1,
            grid=(),
            in_specs=[far if i in apart else whole for i in range(len(operands))],
            out_specs=[far if i in outs_apart else whole for i in range(len(outs))],
            scratch_shapes=scratch,
        ),
        compiler_params=pltpu.CompilerParams(vmem_limit_bytes=KERNEL_VMEM),
    )(base, *operands)


def shape_f32(*shape):
    return jax.ShapeDtypeStruct(shape, jnp.float32)


def reg_call(depth_count, base, links, active, scale, field, rims, moved=()):
    layers, rows, samples, cells = field.shape
    pad = pltpu.VMEM((layers + 1, rows + 1, samples, cells), jnp.float32)
    scratch = [
        pltpu.VMEM(field.shape, jnp.float32),
        pad,
        pltpu.VMEM((rows, samples, cells), jnp.float32),
        pltpu.SemaphoreType.DMA((4,)),
    ]
    operands = [links, active, scale, field, *rims]
    outs = [shape_f32(*field.shape)]
    apart = [3]
    if moved:
        step, grad, grad_rims = moved
        operands += [step, grad, *grad_rims]
        apart.append(9)
        scratch.append(pad)
        outs += [outs[0], shape_f32(rows, samples, cells), shape_f32(layers, samples, cells)]
    return grid_call(
        functools.partial(reg_kernel, not moved, depth_count),
        base,
        operands,
        apart,
        outs,
        [0, 1],
        scratch,
    )


def curvature_call(depth_count, base, links, active, field, rims, grad, grad_rims):
    layers, rows, samples, cells = field.shape
    pad = pltpu.VMEM((layers + 1, rows + 1, samples, cells), jnp.float32)
    (curv,) = grid_call(
        functools.partial(curvature_kernel, depth_count),
        base,
        [links, active, field, *rims[:2], grad, *grad_rims[:2]],
        [2, 5],
        [shape_f32(samples, cells)],
        [],
        [pad, pad, pltpu.SemaphoreType.DMA((2,))],
    )
    return jnp.sum(curv, axis=1)


def load_sensors(sensor_ref, held_ref, sems, parts):
    height = held_ref.shape[1]
    copies = []
    for chunk in range(held_ref.shape[0]):
        rows = pl.ds(chunk % parts * height, height)
        copies.append(
            pltpu.make_async_copy(
                sensor_ref.at[chunk // parts, rows], held_ref.at[chunk], sems.at[chunk]
            )
        )
        copies[-1].start()


def wait_part(sensor_ref, held_ref, sems, tile, part, parts):
    height = held_ref.shape[1]
    chunk = tile * parts + part
    rows = pl.ds(part * height, height)
    pltpu.make_async_copy(
        sensor_ref.at[tile, rows], held_ref.at[chunk], sems.at[chunk]
    ).wait()


def gather_rows(width, slot_ref, arrived_ref, rows_ref):
    cells = arrived_ref.shape[2]

    def one(tile, carry):
        for entry in range(width):
            slot = slot_ref[tile * width + entry]
            rows_ref[tile, :, entry * cells : (entry + 1) * cells] = arrived_ref[slot]
        return carry

    lax.fori_loop(0, rows_ref.shape[0], one, 0)


def scatter_rows(tile, width, slot_ref, blocks, buffer_ref):
    cells = buffer_ref.shape[2]
    for entry in range(width):
        slot = slot_ref[tile * width + entry]
        block = blocks[:, entry * cells : (entry + 1) * cells]
        buffer_ref[slot] = block.astype(buffer_ref.dtype)


def project(rows, sensor):
    return lax.dot_general(
        rows, sensor, (((1,), (1,)), ((), ())), preferred_element_type=jnp.float32
    )


def tile_kernel(mode, slot_ref, arrived_ref, sensor_ref, weight_ref, *refs):
    if mode == "residual":
        observed_ref, pred_ref, buffer_ref, rows_ref, held_ref, sems = refs
    else:
        pred_ref, curv_ref, rows_ref, held_ref, sems = refs
    tiles, _ = pred_ref.shape[:2]
    height = held_ref.shape[1]
    parts = held_ref.shape[0] // tiles
    width = slot_ref.shape[0] // tiles
    load_sensors(sensor_ref, held_ref, sems, parts)
    if mode == "residual":
        buffer_ref[...] = jnp.zeros_like(buffer_ref)
    else:
        curv_ref[...] = jnp.zeros_like(curv_ref)
    gather_rows(width, slot_ref, arrived_ref, rows_ref)

    def one(tile, carry):
        sent = []
        for part in range(parts):
            span = slice(part * height, (part + 1) * height)
            wait_part(sensor_ref, held_ref, sems, tile, part, parts)
            pred = project(rows_ref[tile], held_ref[tile * parts + part])
            pred_ref[tile, :, span] = pred
            weight = weight_ref[tile, :, span]
            if mode == "residual":
                weighted = weight * (pred - observed_ref[tile, :, span])
                sent.append(weighted.astype(jnp.bfloat16))
                continue
            curv_ref[:, span] += weight * pred * pred
        if mode == "residual":
            blocks = 0.0
            for part in range(parts):
                blocks += jnp.dot(
                    sent[part],
                    held_ref[tile * parts + part],
                    preferred_element_type=jnp.float32,
                )
            scatter_rows(tile, width, slot_ref, blocks, buffer_ref)
        return carry

    lax.fori_loop(0, tiles, one, 0)


def back_kernel(slot_ref, sensor_ref, weight_ref, pred_ref, buffer_ref, held_ref, sems):
    tiles, samples = pred_ref.shape[:2]
    height = held_ref.shape[1]
    parts = held_ref.shape[0] // tiles
    width = slot_ref.shape[0] // tiles
    load_sensors(sensor_ref, held_ref, sems, parts)
    buffer_ref[...] = jnp.zeros_like(buffer_ref)

    def one(tile, carry):
        weighted = weight_ref[tile] * pred_ref[tile]
        upper = weighted.astype(jnp.bfloat16).astype(jnp.float32)
        both = jnp.concatenate([upper, weighted - upper], axis=0).astype(jnp.bfloat16)
        blocks = 0.0
        for part in range(parts):
            wait_part(sensor_ref, held_ref, sems, tile, part, parts)
            blocks += jnp.dot(
                both[:, part * height : (part + 1) * height],
                held_ref[tile * parts + part],
                preferred_element_type=jnp.float32,
            )
        scatter_rows(tile, width, slot_ref, blocks[:samples] + blocks[samples:], buffer_ref)
        return carry

    lax.fori_loop(0, tiles, one, 0)


def back_call(slot_of, slots, cells, sensor, weight, pred):
    tiles, data_slots, length = sensor.shape
    height = PART if data_slots % PART == 0 else data_slots
    chunks = tiles * data_slots // height
    whole = pl.BlockSpec(memory_space=pltpu.VMEM)
    return pl.pallas_call(
        back_kernel,
        name="backward",
        out_shape=jax.ShapeDtypeStruct((slots, pred.shape[1], cells), jnp.bfloat16),
        grid_spec=pltpu.PrefetchScalarGridSpec(
            num_scalar_prefetch=1,
            grid=(),
            in_specs=[pl.BlockSpec(memory_space=pltpu.HBM), whole, whole],
            out_specs=whole,
            scratch_shapes=[
                pltpu.VMEM((chunks, height, length), jnp.bfloat16),
                pltpu.SemaphoreType.DMA((chunks,)),
            ],
        ),
        compiler_params=pltpu.CompilerParams(vmem_limit_bytes=KERNEL_VMEM),
    )(slot_of, sensor, weight, pred)


def tile_call(mode, slot_of, arrived, sensor, weight, *observed):
    tiles, data_slots, length = sensor.shape
    _, samples, _ = arrived.shape
    height = PART if data_slots % PART == 0 else data_slots
    parts = data_slots // height
    outs = [jax.ShapeDtypeStruct((tiles, samples, data_slots), jnp.float32)]
    if mode == "forward":
        outs.append(jax.ShapeDtypeStruct((samples, data_slots), jnp.float32))
    else:
        outs.append(jax.ShapeDtypeStruct(arrived.shape, jnp.bfloat16))
    whole = pl.BlockSpec(memory_space=pltpu.VMEM)
    return pl.pallas_call(
        functools.partial(tile_kernel, mode),
        out_shape=outs,
        grid_spec=pltpu.PrefetchScalarGridSpec(
            num_scalar_prefetch=1,
            grid=(),
            in_specs=[whole, pl.BlockSpec(memory_space=pltpu.HBM), whole]
            + [whole] * len(observed),
            out_specs=[whole] * len(outs),
            scratch_shapes=[
                pltpu.VMEM((tiles, samples, length), jnp.bfloat16),
                pltpu.VMEM((tiles * parts, height, length), jnp.bfloat16),
                pltpu.SemaphoreType.DMA((tiles * parts,)),
            ],
        ),
        compiler_params=pltpu.CompilerParams(vmem_limit_bytes=KERNEL_VMEM),
    )(slot_of, arrived, sensor, weight, *observed)


def sum_kernel(first, layers, ids_ref, arrived_ref, active_ref, reg_ref, *refs):
    if first:
        data_ref, grad_ref, reply_ref, norm_ref, *refs = refs
        rims, (total, reg, grad, sems) = (refs[:4], refs[4:])
    else:
        base_ref, step_ref, grad_ref, reply_ref, norm_ref, *refs = refs
        rims, (total, reg, grad, sems, base) = (refs[:4], refs[4:])
        step = step_ref[...]
    count = ids_ref.shape[0]
    bricks = grad.shape[0]
    rows = bricks // layers
    group = 8
    loads = [pltpu.make_async_copy(reg_ref, reg, sems.at[0])]
    if not first:
        loads.append(pltpu.make_async_copy(base_ref, base, sems.at[1]))
    for load in loads:
        load.start()
    total[...] = jnp.zeros_like(total)

    def add(i, carry):
        for k in range(group):
            j = i * group + k
            row = ids_ref[j]
            total[row] += arrived_ref[j].astype(jnp.float32)
        return carry

    lax.fori_loop(0, count // group, add, 0)
    for load in loads:
        load.wait()

    def combine(i, norm):
        live = active_ref[pl.ds(pl.multiple_of(i * group, group), group), :]
        for k in range(group):
            j = i * group + k
            data = total[j]
            if not first:
                data = base[j] - step * data
            value = live[k : k + 1] * data + reg[j]
            grad[j] = value
            norm = norm + value * value
        return norm

    norm = lax.fori_loop(0, bricks // group, combine, jnp.zeros(norm_ref.shape, jnp.float32))
    norm_ref[...] = norm
    stores = [pltpu.make_async_copy(grad, grad_ref, sems.at[2])]
    if first:
        stores.append(pltpu.make_async_copy(total, data_ref, sems.at[3]))
    for store in stores:
        store.start()

    def reply(i, carry):
        for k in range(group):
            j = i * group + k
            reply_ref[j] = grad[ids_ref[j]].astype(reply_ref.dtype)
        return carry

    lax.fori_loop(0, count // group, reply, 0)
    top, bottom, left, right = rims
    top[...] = grad[pl.ds(0, rows)].astype(top.dtype)
    bottom[...] = grad[pl.ds(bricks - rows, rows)].astype(bottom.dtype)
    for layer in range(layers):
        left[layer] = grad[layer * rows].astype(left.dtype)
        right[layer] = grad[layer * rows + rows - 1].astype(right.dtype)
    for store in stores:
        store.wait()


def sum_call(first, layers, ids, arrived, active, reg, *more):
    bricks, samples, cells = reg.shape
    field = jax.ShapeDtypeStruct((bricks, samples, cells), jnp.float32)
    whole = pl.BlockSpec(memory_space=pltpu.VMEM)
    apart = pl.BlockSpec(memory_space=pltpu.HBM)
    outs = [
        field,
        jax.ShapeDtypeStruct(arrived.shape, jnp.bfloat16),
        jax.ShapeDtypeStruct((samples, cells), jnp.float32),
    ]
    for length in (bricks // layers, bricks // layers, layers, layers):
        outs.append(jax.ShapeDtypeStruct((length, samples, cells), jnp.bfloat16))
    out_specs = [apart] + [whole] * (len(outs) - 1)
    in_specs = [whole, whole, apart]
    scratch = [pltpu.VMEM(field.shape, jnp.float32)] * 3 + [pltpu.SemaphoreType.DMA((4,))]
    if first:
        outs = [field] + outs
        out_specs = [apart] + out_specs
    else:
        scratch.append(pltpu.VMEM(field.shape, jnp.float32))
        in_specs = in_specs + [apart, whole]
    return pl.pallas_call(
        functools.partial(sum_kernel, first, layers),
        name="sum_first" if first else "sum_next",
        out_shape=outs,
        grid_spec=pltpu.PrefetchScalarGridSpec(
            num_scalar_prefetch=1,
            grid=(),
            in_specs=in_specs,
            out_specs=out_specs,
            scratch_shapes=scratch,
        ),
        compiler_params=pltpu.CompilerParams(vmem_limit_bytes=KERNEL_VMEM),
    )(ids, arrived, active, reg, *more)


def total_sums(owners, samples, *sums):
    packed = jnp.concatenate(sums)
    packed = jnp.pad(packed, (0, -packed.shape[0] % 128))
    sent = jnp.broadcast_to(packed[None, None, :], (owners, 1, packed.shape[0]))
    got = jnp.sum(swap(sent), axis=(0, 1))
    return [got[i * samples : (i + 1) * samples] for i in range(len(sums))]


def shards(
    sensitivity,
    observed,
    data_weight,
    data_counts,
    tile_bricks,
    start_model,
    active_cells,
    face_links,
    reg_weight,
):
    layers, strip_rows, samples, cells_x = start_model.shape
    tiles, tile_width = tile_bricks.shape
    data_slots = sensitivity.shape[1]
    owners = lax.axis_size("region") * lax.axis_size("survey")
    per_owner = layers * strip_rows
    capacity = max(2, 2 * tiles * tile_width // owners)
    slots = owners * capacity
    depth_count = layers * lax.axis_size("region")
    requests = tile_bricks.reshape(-1)
    owner_of = requests // per_owner
    local_of = requests % per_owner
    owner_hits = (owner_of[:, None] == jnp.arange(owners, dtype=jnp.int32)[None, :]).astype(
        jnp.int32
    )
    before = jnp.cumsum(owner_hits, axis=0) - owner_hits
    rank_of = jnp.sum(before * owner_hits, axis=1)
    slot_of = owner_of * capacity + rank_of
    slot_hits = slot_of[:, None] == jnp.arange(slots, dtype=jnp.int32)[None, :]
    asking = jnp.sum(jnp.where(slot_hits, local_of[:, None], 0), axis=0).reshape(owners, capacity)
    asked_ids = swap(asking).reshape(-1)

    active_rows = active_cells.astype(jnp.float32)
    active_flat = active_rows.reshape(per_owner, cells_x)
    links = face_links.reshape(per_owner, cells_x)
    base = (lax.axis_index("region") * layers).astype(jnp.int32).reshape(1)
    row_mask = (
        jnp.arange(data_slots, dtype=jnp.int32)[None, None, :] < data_counts[:, None, None]
    ).astype(jnp.float32)
    weight_sq = row_mask * (data_weight * data_weight)[:, None, :]
    reg_rows = jnp.broadcast_to(reg_weight[:, None], (samples, cells_x))

    model = start_model * active_rows[:, :, None, :]
    bricks = model.astype(jnp.bfloat16).reshape(per_owner, samples, cells_x)
    replies = bricks[asked_ids]

    def exchange(blocks):
        return swap(blocks.reshape(owners, capacity, samples, cells_x)).reshape(
            slots, samples, cells_x
        )

    def flat(field):
        return field.reshape(per_owner, samples, cells_x)

    def step_of(norm, data_curv, reg_curv):
        norm, data_curv, reg_curv = total_sums(
            owners, samples, jnp.sum(norm, axis=1), jnp.sum(data_curv, axis=1), reg_curv
        )
        return norm / (data_curv + reg_weight * reg_curv)

    grid = (depth_count, base, links, active_flat)
    arrived = exchange(replies)
    model_rims = edges(outer(model))
    predicted, buffer = tile_call("residual", slot_of, arrived, sensitivity, weight_sq, observed)

    arrived = exchange(buffer)
    (reg,) = reg_call(*grid, reg_rows, model, model_rims)
    data_sum, grad, replies, norm, *rims = sum_call(
        True, layers, asked_ids, arrived, active_flat, flat(reg)
    )
    arrived = exchange(replies)
    grad_rims = edges(rims)
    grad = grad.reshape(start_model.shape)
    reg_curv = curvature_call(*grid, model, model_rims, grad, grad_rims)
    step_pred, data_curv = tile_call("forward", slot_of, arrived, sensitivity, weight_sq)
    step = step_of(norm, data_curv, reg_curv)
    buffer = back_call(slot_of, slots, cells_x, sensitivity, weight_sq, step_pred)
    arrived = exchange(buffer)
    predicted = predicted - step[None, :, None] * step_pred

    step_rows = jnp.broadcast_to(step[:, None], (samples, cells_x))
    reg, model, *model_rims = reg_call(
        *grid, reg_rows, model, model_rims, (step_rows, grad, grad_rims)
    )
    grad, replies, norm, *rims = sum_call(
        False, layers, asked_ids, arrived, active_flat, flat(reg), data_sum, step_rows
    )
    arrived = exchange(replies)
    grad_rims = edges(rims, both=False)
    grad = grad.reshape(start_model.shape)
    reg_curv = curvature_call(*grid, model, model_rims, grad, grad_rims)
    step_pred, data_curv = tile_call("forward", slot_of, arrived, sensitivity, weight_sq)
    step = step_of(norm, data_curv, reg_curv)
    model = model - step[None, None, :, None] * grad
    predicted = predicted - step[None, :, None] * step_pred
    misfit = row_mask * data_weight[:, None, :] * (predicted - observed)
    return (model, misfit)


def solution(mesh):
    return jax.shard_map(
        shards,
        mesh=mesh,
        in_specs=(
            P(("region", "survey"), None, None),
            P(("region", "survey"), None, None),
            P(("region", "survey"), None),
            P(("region", "survey")),
            P(("region", "survey"), None),
            P("region", "survey", None, None),
            P("region", "survey", None),
            P("region", "survey", None),
            P(),
        ),
        out_specs=(P("region", "survey", None, None), P(("region", "survey"), None, None)),
        check_vma=False,
    )
```

time: 254 us -> 268 us (1.055)
  other arithmetic: 61.7 us -> 16.9 us
  Pallas kernels: 31.5 us -> 67 us
  waiting for transfers between devices: 9.03 us -> 30.5 us
  blocking collectives: 10.8 us -> 16.4 us
  local copies, waits for them, and re-layouts: 69.3 us -> 64.8 us
    slice x18 -> x0, local copies, waits for them, and re-layouts: 35.7 us -> none  [the longest x2 5.73 us: neighbour_list(): centre[..., 1:]]
    pallas_call x6 -> x10, Pallas kernels: 31.5 us -> 67 us  [the longest x3 37.8 us: tile_call(): pl.pallas_call(functools.partial(tile_kernel, mode), out_shape=outs, grid...]
    reduce_sum x2, other arithmetic: 26.6 us -> 0.8 us  [curvature_call(): return jnp.sum(curv, axis=1)]
    unnamed x70 -> x108, local copies, waits for them, and re-layouts: 29.1 us -> 53.4 us
    mul x3 -> x0, other arithmetic: 18.3 us -> none  [the longest x2 15 us: weights_of(): reg_scale * reg_gradient(field, neighbours, smallness, faces)]
    ppermute x12 -> x10, starting transfers between devices: 31.2 us -> 20.1 us  [the longest x4 12.3 us: edges(): lax.ppermute(last, axis, [(i, i + 1) for i in range(count - 1)])]
    all_to_all x7, waiting for transfers between devices: 9 us -> 20 us  [swap(): return lax.all_to_all(field, AXES, split_axis=0, concat_axis=0, tiled=True)]
    all_to_all x7, starting transfers between devices: 38.1 us -> 49 us  [swap(): return lax.all_to_all(field, AXES, split_axis=0, concat_axis=0, tiled=True)]
  transfers between devices with their start and end apart: 19 -> 17, of which waited for: 5 -> 9; matrix products, arithmetic and copies ran while one was open for 32% -> 7% of each run, Pallas kernels for 5% -> 8%
where the time goes in v2:
time: 268 us; the launch traced here: 266 us
  starting transfers between devices  69.1 us (26%)
  Pallas kernels  67 us (25%)
  local copies, waits for them, and re-layouts  64.8 us (24%)
  waiting for transfers between devices  30.5 us (11%)
  other arithmetic  16.9 us (6%)
  blocking collectives  16.4 us (6%)
    unnamed x108, local copies, waits for them, and re-layouts  53.4 us
    all_to_all x7, starting transfers between devices, swap(): return lax.all_to_all(field, AXES, split_axis=0, concat_axis=0, tiled=True)  49 us
    pallas_call x3, Pallas kernels, tile_call(): pl.pallas_call(functools.partial(tile_kernel, mode), out_shape=outs, grid...  37.8 us
    all_to_all x7, waiting for transfers between devices, swap(): return lax.all_to_all(field, AXES, split_axis=0, concat_axis=0, tiled=True)  20 us
    pallas_call x4, Pallas kernels, grid_call(): pl.pallas_call(kernel, out_shape=outs, grid_spec=pltpu.PrefetchScalarGrid...  16.4 us
    all_to_all x1, blocking collectives, swap(): return lax.all_to_all(field, AXES, split_axis=0, concat_axis=0, tiled=True)  16.4 us
    ppermute x4, starting transfers between devices, edges(): lax.ppermute(last, axis, [(i, i + 1) for i in range(count - 1)])  12.3 us
    ppermute x6, waiting for transfers between devices, edges(): lax.ppermute(first, axis, [(i + 1, i) for i in range(count - 1)])  9.72 us
  transfers between devices with their start and end apart: 17, of which 9 were waited for; matrix products, arithmetic and copies ran while one was open for 7% of the time, Pallas kernels for 8%

profile of v2, /device:TPU:0, one launch (start us, length us, event | category | flops | bytes accessed | tf_op | source)
XLA Modules:
  0.0 265.8 jit_solution(18182007020766765226)
XLA Ops:
  2.7 7.3 %all-to-all-start = ((s32[32,1,8]{2,1,0:T(1,128)}), s32[32,1,8]{2,1,0:T(1,128)S(1)}, u32[]{:S(2)}, u32[]{:S(2)}) async-start(s32[32,1,8]{2,1,0:T(1,128)} %bitcast.7), calls=%async_computation | async-start | bytes 32768 | tf_op jit(solution)/shard_map/all_to_all | solution.py:18
  11.2 3.3 %fusion.2 = (bf16[16,32,8,128]{3,2,0,1:T(8,128)(2,1)S(1)}, f32[16,32,8,128]{3,2,0,1:T(8,128)}) fusion(f32[16,32,128]{2,0,1:T(8,128)S(1)} %copy.36, f32[16,32,8,128]{3,2,1,0:T(8,128)} %param.14), kind=kLoop, calls=%fused_computation.30 | loop fusion | flops 1048576 | bytes 5505024 | tf_op jit(solution)/shard_map/convert_element_type | solution.py:591
  14.8 2.4 all-to-all-done
  17.2 1.6 gather_fusion
  18.8 3.5 %all-to-all-start.1 = ((bf16[32,8,8,128]{3,2,1,0:T(8,128)(2,1)}), bf16[32,8,8,128]{3,2,1,0:T(8,128)(2,1)S(1)}, u32[]{:S(2)}, u32[]{:S(2)}) async-start(bf16[32,8,8,128]{3,2,1,0:T(8,128)(2,1)} %bitcast.10), calls=%async_computation.1 | async-start | bytes 1048576 | tf_op jit(solution)/shard_map/all_to_all | solution.py:18
  23.0 14.9 %all-to-all-done.1 = bf16[32,8,8,128]{3,2,1,0:T(8,128)(2,1)S(1)} async-done(((bf16[32,8,8,128]{3,2,1,0:T(8,128)(2,1)}), bf16[32,8,8,128]{3,2,1,0:T(8,128)(2,1)S(1)}, u32[]{:S(2)}, u32[]{:S(2)}) %all-to-all-start.1) | async-done | bytes 524320 | tf_op jit(solution)/shard_map/all_to_all | solution.py:18
  37.9 5.8 %copy-done = bf16[4,512,4096]{2,1,0:T(8,128)(2,1)S(1)} copy-done((bf16[4,512,4096]{2,1,0:T(8,128)(2,1)S(1)}, bf16[4,512,4096]{2,1,0:T(8,128)(2,1)}, u32[]{:S(2)}) %copy-start) | copy-done | bytes 16777240
  43.7 14.8 %shard_map.104 = (f32[4,8,512]{2,1,0:T(8,128)S(1)}, bf16[256,8,128]{2,1,0:T(8,128)(2,1)}) custom-call(s32[128]{0:T(128)S(1)} %multiply_add_fusion.slot_ref, bf16[256,8,128]{2,1,0:T(8,128)(2,1)S(1)} %bitcast.50, bf16[4,512,4096]{2,1,0:T(8,128)(2,1)S(1)} %copy-done, f32[4,1,512]{2,1,0:T(1,128)S(1)} %mul.81.weight_ref, f32[4,8,512]{2,1,0:T(8,128)S(1)} %copy-done.21), custom_call_target="tpu_custom_call" | custom-call | tf_op jit(solution)/shard_map/pallas_call | solution.py:418
  58.5 3.0 %all-to-all-start.2 = ((bf16[32,8,8,128]{3,2,1,0:T(8,128)(2,1)}), bf16[32,8,8,128]{3,2,1,0:T(8,128)(2,1)S(1)}, u32[]{:S(2)}, u32[]{:S(2)}) async-start(bf16[32,8,8,128]{3,2,1,0:T(8,128)(2,1)} %bitcast.12), calls=%async_computation.2 | async-start | bytes 1048576 | tf_op jit(solution)/shard_map/all_to_all | solution.py:18
  61.5 1.7 slice_bitcast_fusion
  63.2 3.7 %collective-permute-start.2 = (f32[32,8,128]{2,1,0:T(8,128)}, f32[32,8,128]{2,1,0:T(8,128)S(1)}, u32[]{:S(2)}, u32[]{:S(2)}) collective-permute-start(f32[32,8,128]{2,1,0:T(8,128)} %get-tuple-element.52), channel_id=1, source_target_pairs={{0,4},{4,8},{8,12},{12,16},{16,20},{20,24},{24,28},{1,5},{5,9},{9,... | collective-permute-start | bytes 393224 | tf_op jit(solution)/shard_map/ppermute | solution.py:31
  68.2 1.5 slice_bitcast_fusion.2
  69.7 1.7 collective-permute-start.3
  72.8 1.8 copy.43.field_ref
  75.1 1.9 reduce.5
  78.6 3.8 %shard_map.105 = f32[16,32,8,128]{3,2,1,0:T(8,128)S(1)} custom-call(s32[1]{0:T(128)} %bitcast.base_ref, s32[512,128]{1,0:T(8,128)S(1)} %bitcast.42, f32[512,128]{1,0:T(8,128)S(1)} %bitcast.31, f32[8,128]{1,0:T(8,128)S(1)} %broadcast_in_dim.20.scale_ref, f32[16,32,8,128]{3,2,1,0:T(8,128)S(1)} %copy.43.field_ref, ...), custom_call_target="tpu_custom_call" | custom-call | tf_op jit(solution)/shard_map/pallas_call | solution.py:205
  83.7 1.6 copy-done.12
  85.3 3.5 %sum_first.1 = (f32[512,8,128]{2,1,0:T(8,128)S(1)}, f32[512,8,128]{2,1,0:T(8,128)S(1)}, bf16[256,8,128]{2,1,0:T(8,128)(2,1)S(1)}, f32[8,128]{1,0:T(8,128)S(1)}, ...) custom-call(s32[256]{0:T(256)S(1)} %reshape.186.ids_ref, ...), custom_call_target="tpu_custom_call" | custom-call | tf_op jit(solution)/shard_map/sum_first/pallas_call | solution.py:525
  90.2 1.3 copy-done.15
  95.4 9.4 %all-to-all-start.3 = ((bf16[32,8,8,128]{3,2,1,0:T(8,128)(2,1)}), bf16[32,8,8,128]{3,2,1,0:T(8,128)(2,1)S(1)}, u32[]{:S(2)}, u32[]{:S(2)}) async-start(bf16[32,8,8,128]{3,2,1,0:T(8,128)(2,1)} %bitcast.54), calls=%async_computation.3 | async-start | bytes 1048576 | tf_op jit(solution)/shard_map/all_to_all | solution.py:18
  109.5 3.5 %collective-permute-done.4.gbelow.refs_6_ = bf16[32,8,128]{2,1,0:T(8,128)(2,1)} collective-permute-done((bf16[32,8,128]{2,1,0:T(8,128)(2,1)}, bf16[32,8,128]{2,1,0:T(8,128)(2,1)}, u32[]{:S(2)}, u32[]{:S(2)}) %collective-permute-start.4) | collective-permute-done | bytes 65568 | tf_op jit(solution)/shard_map/ppermute | solution.py:29
  113.0 1.6 copy-done.9
  114.6 4.1 %shard_map.107 = f32[8,128]{1,0:T(8,128)S(1)} custom-call(s32[1]{0:T(128)} %bitcast.base_ref, s32[512,128]{1,0:T(8,128)S(1)} %bitcast.43, f32[512,128]{1,0:T(8,128)S(1)} %bitcast.33, f32[16,32,8,128]{3,2,1,0:T(8,128)S(1)} %copy.43.field_ref, f32[32,8,128]{2,1,0:T(8,128)S(1)} %collective-permute-done.refs_0_.below, ...), custom_call_target="tpu_custom_call" | custom-call | tf_op jit(solution)/shard_map/pallas_call | solution.py:205
  120.4 5.8 %copy-done.1 = bf16[4,512,4096]{2,1,0:T(8,128)(2,1)S(1)} copy-done((bf16[4,512,4096]{2,1,0:T(8,128)(2,1)S(1)}, bf16[4,512,4096]{2,1,0:T(8,128)(2,1)}, u32[]{:S(2)}) %copy-start.1) | copy-done | bytes 16777240
  126.9 11.5 %shard_map.106 = (f32[4,8,512]{2,1,0:T(8,128)S(1)}, f32[8,512]{1,0:T(8,128)S(1)}) custom-call(s32[128]{0:T(128)S(1)} %copy-done.34, bf16[256,8,128]{2,1,0:T(8,128)(2,1)S(1)} %bitcast.49, bf16[4,512,4096]{2,1,0:T(8,128)(2,1)S(1)} %copy-done.1, f32[4,1,512]{2,1,0:T(1,128)S(1)} %mul.81.weight_ref), custom_call_target="tpu_custom_call" | custom-call | tf_op jit(solution)/shard_map/pallas_call | solution.py:418
  141.8 10.0 %all-to-all-start.4 = ((f32[32,1,128]{2,1,0:T(1,128)}), f32[32,1,128]{2,1,0:T(1,128)S(1)}, u32[]{:S(2)}, u32[]{:S(2)}) async-start(f32[32,1,128]{2,1,0:T(1,128)} %broadcast_in_dim.23), calls=%async_computation.4 | async-start | bytes 32768 | tf_op jit(solution)/shard_map/all_to_all | solution.py:18
  151.8 5.8 %copy-done.2 = bf16[4,512,4096]{2,1,0:T(8,128)(2,1)S(1)} copy-done((bf16[4,512,4096]{2,1,0:T(8,128)(2,1)S(1)}, bf16[4,512,4096]{2,1,0:T(8,128)(2,1)}, u32[]{:S(2)}) %copy-start.2) | copy-done | bytes 16777240
  158.4 5.0 %backward.1 = bf16[256,8,128]{2,1,0:T(8,128)(2,1)S(1)} custom-call(s32[128]{0:T(128)S(1)} %copy-done.35, bf16[4,512,4096]{2,1,0:T(8,128)(2,1)S(1)} %copy-done.2, f32[4,1,512]{2,1,0:T(1,128)S(1)} %mul.81.weight_ref, f32[4,8,512]{2,1,0:T(8,128)S(1)} %copy-done.24), custom_call_target="tpu_custom_call" | custom-call | tf_op jit(solution)/shard_map/backward/pallas_call | solution.py:389
  164.8 5.8 %all-to-all-start.5 = ((bf16[32,8,8,128]{3,2,1,0:T(8,128)(2,1)}), bf16[32,8,8,128]{3,2,1,0:T(8,128)(2,1)S(1)}, u32[]{:S(2)}, u32[]{:S(2)}) async-start(bf16[32,8,8,128]{3,2,1,0:T(8,128)(2,1)} %bitcast.47), calls=%async_computation.5 | async-start | bytes 1048576 | tf_op jit(solution)/shard_map/all_to_all | solution.py:18
  170.6 2.8 %collective-permute-start.7 = (bf16[16,8,128]{2,1,0:T(8,128)(2,1)}, bf16[16,8,128]{2,1,0:T(8,128)(2,1)}, u32[]{:S(2)}, u32[]{:S(2)}) collective-permute-start(bf16[16,8,128]{2,1,0:T(8,128)(2,1)} %copy-done.43), channel_id=1, source_target_pairs={{0,1},{1,2},{2,3},{4,5},{5,6},{6,7},{8,9},{9,10},{10,11},{12,13},{... | collective-permute-start | bytes 98312 | tf_op jit(solution)/shard_map/ppermute | solution.py:31
  173.4 4.1 %collective-permute-start.6 = (bf16[32,8,128]{2,1,0:T(8,128)(2,1)}, bf16[32,8,128]{2,1,0:T(8,128)(2,1)}, u32[]{:S(2)}, u32[]{:S(2)}) collective-permute-start(bf16[32,8,128]{2,1,0:T(8,128)(2,1)} %copy-done.40), channel_id=1, source_target_pairs={{0,4},{4,8},{8,12},{12,16},{16,20},{20,24},{24,28},{1,5},{5,9},{9,... | collective-permute-start | bytes 196616 | tf_op jit(solution)/shard_map/ppermute | solution.py:31
  179.9 1.6 copy-done.10
  181.5 5.3 %shard_map.108 = (f32[16,32,8,128]{3,2,1,0:T(8,128)S(1)}, f32[16,32,8,128]{3,2,1,0:T(8,128)S(1)}, f32[32,8,128]{2,1,0:T(8,128)S(1)}, f32[16,8,128]{2,1,0:T(8,128)S(1)}) custom-call(s32[1]{0:T(128)} %bitcast.base_ref, s32[512,128]{1,0:T(8,128)S(1)} %bitcast.44, f32[512,128]{1,0:T(8,128)S(1)} %bitcast.34, f32[8,128]{1,0:T(8,128)S(1)} %broadcast_in_dim.20.scale_ref, ...), custom_call_target="tpu_custom_call" | custom-call | tf_op jit(solution)/shard_map/pallas_call | solution.py:205
  188.2 1.3 copy-done.17
  190.8 1.6 copy-done.16
  192.4 1.6 copy-done.18
  194.7 4.3 %sum_next.1 = (f32[512,8,128]{2,1,0:T(8,128)S(1)}, bf16[256,8,128]{2,1,0:T(8,128)(2,1)S(1)}, f32[8,128]{1,0:T(8,128)S(1)}, bf16[32,8,128]{2,1,0:T(8,128)(2,1)S(1...) custom-call(s32[256]{0:T(256)S(1)} %copy-done.38, ...), custom_call_target="tpu_custom_call" | custom-call | tf_op jit(solution)/shard_map/sum_next/pallas_call | solution.py:525
  198.9 1.3 copy-done.6
  202.3 10.0 %all-to-all-start.6 = ((bf16[32,8,8,128]{3,2,1,0:T(8,128)(2,1)}), bf16[32,8,8,128]{3,2,1,0:T(8,128)(2,1)S(1)}, u32[]{:S(2)}, u32[]{:S(2)}) async-start(bf16[32,8,8,128]{3,2,1,0:T(8,128)(2,1)} %bitcast.53), calls=%async_computation.6 | async-start | bytes 1048576 | tf_op jit(solution)/shard_map/all_to_all | solution.py:18
  215.0 1.9 collective-permute-done.9.gright
  216.9 3.5 %collective-permute-done.8.gbelow = bf16[32,8,128]{2,1,0:T(8,128)(2,1)S(1)} collective-permute-done((bf16[32,8,128]{2,1,0:T(8,128)(2,1)}, bf16[32,8,128]{2,1,0:T(8,128)(2,1)S(1)}, u32[]{:S(2)}, u32[]{:S(2)}) %collective-permute-start.8) | collective-permute-done | bytes 65568 | tf_op jit(solution)/shard_map/ppermute | solution.py:29
  220.4 1.6 copy-done.7
  222.9 3.2 %shard_map.110 = f32[8,128]{1,0:T(8,128)S(1)} custom-call(s32[1]{0:T(128)} %bitcast.base_ref, s32[512,128]{1,0:T(8,128)S(1)} %bitcast.45, f32[512,128]{1,0:T(8,128)S(1)} %bitcast.36, f32[16,32,8,128]{3,2,1,0:T(8,128)S(1)} %copy-done.5, f32[32,8,128]{2,1,0:T(8,128)S(1)} %copy-done.27, f32[16,8,128]{2,1,0:T(8,128)S(1)} %copy-done.29, ...), custom_call_target="tpu_custom_call" | custom-call | tf_op jit(solution)/shard_map/pallas_call | solution.py:205
  226.3 1.6 all-to-all-done.6
  227.9 5.8 %copy-done.3 = bf16[4,512,4096]{2,1,0:T(8,128)(2,1)S(1)} copy-done((bf16[4,512,4096]{2,1,0:T(8,128)(2,1)S(1)}, bf16[4,512,4096]{2,1,0:T(8,128)(2,1)}, u32[]{:S(2)}) %copy-start.3) | copy-done | bytes 16777240
  233.7 11.5 %shard_map.109 = (f32[4,8,512]{2,1,0:T(8,128)S(1)}, f32[8,512]{1,0:T(8,128)S(1)}) custom-call(s32[128]{0:T(128)S(1)} %copy-done.36, bf16[256,8,128]{2,1,0:T(8,128)(2,1)S(1)} %bitcast.48, bf16[4,512,4096]{2,1,0:T(8,128)(2,1)S(1)} %copy-done.3, f32[4,1,512]{2,1,0:T(1,128)S(1)} %mul.81.weight_ref), custom_call_target="tpu_custom_call" | custom-call | tf_op jit(solution)/shard_map/pallas_call | solution.py:418
  245.4 16.4 %all_to_all.44 = f32[32,1,128]{2,1,0:T(1,128)S(1)} all-to-all(f32[32,1,128]{2,1,0:T(1,128)S(1)} %broadcast_in_dim.25), channel_id=1, replica_groups=mesh['region'=8,'survey'=4] {'region','survey'}, dimensions={0} | all-to-all | bytes 32768 | tf_op jit(solution)/shard_map/all_to_all | solution.py:18
  261.9 3.2 %multiply_subtract_fusion = f32[16,32,8,128]{3,2,1,0:T(8,128)} fusion(f32[16,32,8,128]{3,2,1,0:T(8,128)S(1)} %copy-done.5, f32[16,32,8,128]{3,2,1,0:T(8,128)} %bitcast.37, f32[8]{0:T(128)S(1)} %add_divide_fusion), kind=kLoop, calls=%fused_computation.2 | loop fusion | flops 1048576 | bytes 6291488 | tf_op jit(solution)/shard_map/sub | solution.py:641
  (147 shorter events, 40.5 us)
Async XLA Ops:
  1.9 36.1 %copy-start.33 = (s32[128]{0:T(128)}, s32[128]{0:T(128)S(1)}, u32[]{:S(2)}) copy-start(s32[128]{0:T(128)S(1)} %multiply_add_fusion.slot_ref) | copy-start | bytes 1540
  2.7 14.4 %all-to-all-start = ((s32[32,1,8]{2,1,0:T(1,128)}), s32[32,1,8]{2,1,0:T(1,128)S(1)}, u32[]{:S(2)}, u32[]{:S(2)}) async-start(s32[32,1,8]{2,1,0:T(1,128)} %bitcast.7), calls=%async_computation | async-start | bytes 32768 | tf_op jit(solution)/shard_map/all_to_all | solution.py:18
  14.5 7.8 %copy-start.49 = (f32[4,512]{1,0:T(4,128)S(1)}, f32[4,512]{1,0:T(4,128)}, u32[]{:S(2)}) copy-start(f32[4,512]{1,0:T(4,128)} %param.11) | copy-start | bytes 24580
  14.5 7.8 %copy-start.53 = (s32[4]{0:T(128)S(1)}, s32[4]{0:T(128)}, u32[]{:S(2)}) copy-start(s32[4]{0:T(128)} %param.12) | copy-start | bytes 52
  14.5 23.4 %copy-start.21 = (f32[4,8,512]{2,1,0:T(8,128)S(1)}, f32[4,8,512]{2,1,0:T(8,128)}, u32[]{:S(2)}) copy-start(f32[4,8,512]{2,1,0:T(8,128)} %refs_0_.1) | copy-start | bytes 196612
  17.1 20.8 %copy-start.46 = (s32[32,1,8]{2,1,0:T(1,128)}, s32[32,1,8]{2,1,0:T(1,128)S(1)}, u32[]{:S(2)}) copy-start(s32[32,1,8]{2,1,0:T(1,128)S(1)} %all-to-all-done) | copy-start | bytes 3076
  18.8 19.1 %all-to-all-start.1 = ((bf16[32,8,8,128]{3,2,1,0:T(8,128)(2,1)}), bf16[32,8,8,128]{3,2,1,0:T(8,128)(2,1)S(1)}, u32[]{:S(2)}, u32[]{:S(2)}) async-start(bf16[32,8,8,128]{3,2,1,0:T(8,128)(2,1)} %bitcast.10), calls=%async_computation.1 | async-start | bytes 1048576 | tf_op jit(solution)/shard_map/all_to_all | solution.py:18
  37.9 5.8 %copy-start = (bf16[4,512,4096]{2,1,0:T(8,128)(2,1)S(1)}, bf16[4,512,4096]{2,1,0:T(8,128)(2,1)}, u32[]{:S(2)}) copy-start(bf16[4,512,4096]{2,1,0:T(8,128)(2,1)} %sensor_ref.7) | copy-start | bytes 50331652
  58.5 14.2 %copy-start.30 = (f32[4,8,512]{2,1,0:T(8,128)}, f32[4,8,512]{2,1,0:T(8,128)S(1)}, u32[]{:S(2)}) copy-start(f32[4,8,512]{2,1,0:T(8,128)S(1)} %get-tuple-element.46) | copy-start | bytes 196612
  58.5 25.2 %all-to-all-start.2 = ((bf16[32,8,8,128]{3,2,1,0:T(8,128)(2,1)}), bf16[32,8,8,128]{3,2,1,0:T(8,128)(2,1)S(1)}, u32[]{:S(2)}, u32[]{:S(2)}) async-start(bf16[32,8,8,128]{3,2,1,0:T(8,128)(2,1)} %bitcast.12), calls=%async_computation.2 | async-start | bytes 1048576 | tf_op jit(solution)/shard_map/all_to_all | solution.py:18
  63.2 14.7 %collective-permute-start.2 = (f32[32,8,128]{2,1,0:T(8,128)}, f32[32,8,128]{2,1,0:T(8,128)S(1)}, u32[]{:S(2)}, u32[]{:S(2)}) collective-permute-start(f32[32,8,128]{2,1,0:T(8,128)} %get-tuple-element.52), channel_id=1, source_target_pairs={{0,4},{4,8},{8,12},{12,16},{16,20},{20,24},{24,28},{1,5},{5,9},{9,... | collective-permute-start | bytes 393224 | tf_op jit(solution)/shard_map/ppermute | solution.py:31
  66.9 11.0 %collective-permute-start = (f32[32,8,128]{2,1,0:T(8,128)}, f32[32,8,128]{2,1,0:T(8,128)S(1)}, u32[]{:S(2)}, u32[]{:S(2)}) collective-permute-start(f32[32,8,128]{2,1,0:T(8,128)} %get-tuple-element.53), channel_id=1, source_target_pairs={{4,0},{8,4},{12,8},{16,12},{20,16},{24,20},{28,24},{5,1},{9,5},{13... | collective-permute-start | bytes 393224 | tf_op jit(solution)/shard_map/ppermute | solution.py:29
  69.7 8.2 %collective-permute-start.3 = (f32[16,8,128]{2,1,0:T(8,128)}, f32[16,8,128]{2,1,0:T(8,128)S(1)}, u32[]{:S(2)}, u32[]{:S(2)}) collective-permute-start(f32[16,8,128]{2,1,0:T(8,128)} %get-tuple-element.50), channel_id=1, source_target_pairs={{0,1},{1,2},{2,3},{4,5},{5,6},{6,7},{8,9},{9,10},{10,11},{12,13},{... | collective-permute-start | bytes 196616 | tf_op jit(solution)/shard_map/ppermute | solution.py:31
  71.4 6.4 %collective-permute-start.1 = (f32[16,8,128]{2,1,0:T(8,128)}, f32[16,8,128]{2,1,0:T(8,128)S(1)}, u32[]{:S(2)}, u32[]{:S(2)}) collective-permute-start(f32[16,8,128]{2,1,0:T(8,128)} %get-tuple-element.51), channel_id=1, source_target_pairs={{1,0},{2,1},{3,2},{5,4},{6,5},{7,6},{9,8},{10,9},{11,10},{13,12},{... | collective-permute-start | bytes 196616 | tf_op jit(solution)/shard_map/ppermute | solution.py:29
  72.8 5.9 %copy-start.13 = (s32[16,32,128]{2,1,0:T(8,128)S(1)}, s32[16,32,128]{2,1,0:T(8,128)}, u32[]{:S(2)}) copy-start(s32[16,32,128]{2,1,0:T(8,128)} %param.16) | copy-start | bytes 786436
  77.9 5.9 %copy-start.37 = (s32[256]{0:T(256)}, s32[256]{0:T(256)S(1)}, u32[]{:S(2)}) copy-start(s32[256]{0:T(256)S(1)} %reshape.186.ids_ref) | copy-start | bytes 3076
  83.7 1.6 copy-start.12
  90.2 1.3 copy-start.15
  95.4 25.0 %all-to-all-start.3 = ((bf16[32,8,8,128]{3,2,1,0:T(8,128)(2,1)}), bf16[32,8,8,128]{3,2,1,0:T(8,128)(2,1)S(1)}, u32[]{:S(2)}, u32[]{:S(2)}) async-start(bf16[32,8,8,128]{3,2,1,0:T(8,128)(2,1)} %bitcast.54), calls=%async_computation.3 | async-start | bytes 1048576 | tf_op jit(solution)/shard_map/all_to_all | solution.py:18
  104.8 8.2 %collective-permute-start.4 = (bf16[32,8,128]{2,1,0:T(8,128)(2,1)}, bf16[32,8,128]{2,1,0:T(8,128)(2,1)}, u32[]{:S(2)}, u32[]{:S(2)}) collective-permute-start(bf16[32,8,128]{2,1,0:T(8,128)(2,1)} %copy-done.42), channel_id=1, source_target_pairs={{4,0},{8,4},{12,8},{16,12},{20,16},{24,20},{28,24},{5,1},{9,5},{13... | collective-permute-start | bytes 196616 | tf_op jit(solution)/shard_map/ppermute | solution.py:29
  106.1 3.4 %collective-permute-start.5 = (bf16[16,8,128]{2,1,0:T(8,128)(2,1)}, bf16[16,8,128]{2,1,0:T(8,128)(2,1)}, u32[]{:S(2)}, u32[]{:S(2)}) collective-permute-start(bf16[16,8,128]{2,1,0:T(8,128)(2,1)} %copy-done.45), channel_id=1, source_target_pairs={{1,0},{2,1},{3,2},{5,4},{6,5},{7,6},{9,8},{10,9},{11,10},{13,12},{... | collective-permute-start | bytes 98312 | tf_op jit(solution)/shard_map/ppermute | solution.py:29
  113.0 1.6 copy-start.9
  120.4 5.8 %copy-start.1 = (bf16[4,512,4096]{2,1,0:T(8,128)(2,1)S(1)}, bf16[4,512,4096]{2,1,0:T(8,128)(2,1)}, u32[]{:S(2)}) copy-start(bf16[4,512,4096]{2,1,0:T(8,128)(2,1)} %sensor_ref.7) | copy-start | bytes 50331652
  126.9 24.9 %copy-start.35 = (s32[128]{0:T(128)S(1)}, s32[128]{0:T(128)}, u32[]{:S(2)}) copy-start(s32[128]{0:T(128)} %copy-done.33) | copy-start | bytes 1540
  141.8 22.4 %all-to-all-start.4 = ((f32[32,1,128]{2,1,0:T(1,128)}), f32[32,1,128]{2,1,0:T(1,128)S(1)}, u32[]{:S(2)}, u32[]{:S(2)}) async-start(f32[32,1,128]{2,1,0:T(1,128)} %broadcast_in_dim.23), calls=%async_computation.4 | async-start | bytes 32768 | tf_op jit(solution)/shard_map/all_to_all | solution.py:18
  151.7 5.8 %copy-start.2 = (bf16[4,512,4096]{2,1,0:T(8,128)(2,1)S(1)}, bf16[4,512,4096]{2,1,0:T(8,128)(2,1)}, u32[]{:S(2)}) copy-start(bf16[4,512,4096]{2,1,0:T(8,128)(2,1)} %sensor_ref.7) | copy-start | bytes 50331652
  164.8 26.0 %all-to-all-start.5 = ((bf16[32,8,8,128]{3,2,1,0:T(8,128)(2,1)}), bf16[32,8,8,128]{3,2,1,0:T(8,128)(2,1)S(1)}, u32[]{:S(2)}, u32[]{:S(2)}) async-start(bf16[32,8,8,128]{3,2,1,0:T(8,128)(2,1)} %bitcast.47), calls=%async_computation.5 | async-start | bytes 1048576 | tf_op jit(solution)/shard_map/all_to_all | solution.py:18
  170.6 8.4 %collective-permute-start.7 = (bf16[16,8,128]{2,1,0:T(8,128)(2,1)}, bf16[16,8,128]{2,1,0:T(8,128)(2,1)}, u32[]{:S(2)}, u32[]{:S(2)}) collective-permute-start(bf16[16,8,128]{2,1,0:T(8,128)(2,1)} %copy-done.43), channel_id=1, source_target_pairs={{0,1},{1,2},{2,3},{4,5},{5,6},{6,7},{8,9},{9,10},{10,11},{12,13},{... | collective-permute-start | bytes 98312 | tf_op jit(solution)/shard_map/ppermute | solution.py:31
  173.4 6.5 %collective-permute-start.6 = (bf16[32,8,128]{2,1,0:T(8,128)(2,1)}, bf16[32,8,128]{2,1,0:T(8,128)(2,1)}, u32[]{:S(2)}, u32[]{:S(2)}) collective-permute-start(bf16[32,8,128]{2,1,0:T(8,128)(2,1)} %copy-done.40), channel_id=1, source_target_pairs={{0,4},{4,8},{8,12},{12,16},{16,20},{20,24},{24,28},{1,5},{5,9},{9,... | collective-permute-start | bytes 196616 | tf_op jit(solution)/shard_map/ppermute | solution.py:31
  179.9 1.6 copy-start.10
  188.2 1.3 copy-start.17
  190.8 1.6 copy-start.16
  192.4 1.6 copy-start.18
  194.7 25.8 %copy-start.5 = (f32[16,32,8,128]{3,2,1,0:T(8,128)S(1)}, f32[16,32,8,128]{3,2,1,0:T(8,128)}, u32[]{:S(2)}) copy-start(f32[16,32,8,128]{3,2,1,0:T(8,128)} %copy-done.4) | copy-start | bytes 6291460
  194.7 25.8 %copy-start.29 = (f32[16,8,128]{2,1,0:T(8,128)S(1)}, f32[16,8,128]{2,1,0:T(8,128)}, u32[]{:S(2)}) copy-start(f32[16,8,128]{2,1,0:T(8,128)} %copy-done.28) | copy-start | bytes 196612
  198.9 1.3 copy-start.6
  202.3 25.6 %all-to-all-start.6 = ((bf16[32,8,8,128]{3,2,1,0:T(8,128)(2,1)}), bf16[32,8,8,128]{3,2,1,0:T(8,128)(2,1)S(1)}, u32[]{:S(2)}, u32[]{:S(2)}) async-start(bf16[32,8,8,128]{3,2,1,0:T(8,128)(2,1)} %bitcast.53), calls=%async_computation.6 | async-start | bytes 1048576 | tf_op jit(solution)/shard_map/all_to_all | solution.py:18
  212.3 8.1 %collective-permute-start.8 = (bf16[32,8,128]{2,1,0:T(8,128)(2,1)}, bf16[32,8,128]{2,1,0:T(8,128)(2,1)S(1)}, u32[]{:S(2)}, u32[]{:S(2)}) collective-permute-start(bf16[32,8,128]{2,1,0:T(8,128)(2,1)} %copy-done.41), channel_id=1, source_target_pairs={{4,0},{8,4},{12,8},{16,12},{20,16},{24,20},{28,24},{5,1},{9,5},{13... | collective-permute-start | bytes 196616 | tf_op jit(solution)/shard_map/ppermute | solution.py:29
  213.6 3.3 %collective-permute-start.9 = (bf16[16,8,128]{2,1,0:T(8,128)(2,1)}, bf16[16,8,128]{2,1,0:T(8,128)(2,1)S(1)}, u32[]{:S(2)}, u32[]{:S(2)}) collective-permute-start(bf16[16,8,128]{2,1,0:T(8,128)(2,1)} %copy-done.44), channel_id=1, source_target_pairs={{1,0},{2,1},{3,2},{5,4},{6,5},{7,6},{9,8},{10,9},{11,10},{13,12},{... | collective-permute-start | bytes 98312 | tf_op jit(solution)/shard_map/ppermute | solution.py:29
  220.4 1.6 copy-start.7
  222.9 5.0 %copy-start.36 = (s32[128]{0:T(128)S(1)}, s32[128]{0:T(128)}, u32[]{:S(2)}) copy-start(s32[128]{0:T(128)} %copy-done.33) | copy-start | bytes 1540
  227.9 5.8 %copy-start.3 = (bf16[4,512,4096]{2,1,0:T(8,128)(2,1)S(1)}, bf16[4,512,4096]{2,1,0:T(8,128)(2,1)}, u32[]{:S(2)}) copy-start(bf16[4,512,4096]{2,1,0:T(8,128)(2,1)} %sensor_ref.7) | copy-start | bytes 50331652
  233.7 28.1 %copy-start.52 = (f32[8]{0:T(128)S(1)}, f32[8]{0:T(128)}, u32[]{:S(2)}) copy-start(f32[8]{0:T(128)} %param.17) | copy-start | bytes 100
  261.8 3.3 %copy-start.22 = (f32[4,8,512]{2,1,0:T(8,128)S(1)}, f32[4,8,512]{2,1,0:T(8,128)}, u32[]{:S(2)}) copy-start(f32[4,8,512]{2,1,0:T(8,128)} %refs_0_.1) | copy-start | bytes 196612
  261.8 3.3 %copy-start.25 = (f32[4,8,512]{2,1,0:T(8,128)S(1)}, f32[4,8,512]{2,1,0:T(8,128)}, u32[]{:S(2)}) copy-start(f32[4,8,512]{2,1,0:T(8,128)} %copy-done.23) | copy-start | bytes 196612
  261.8 3.3 %copy-start.31 = (f32[4,8,512]{2,1,0:T(8,128)S(1)}, f32[4,8,512]{2,1,0:T(8,128)}, u32[]{:S(2)}) copy-start(f32[4,8,512]{2,1,0:T(8,128)} %copy-done.30) | copy-start | bytes 196612
  261.9 3.3 %copy-start.48 = (f32[4,512]{1,0:T(4,128)S(1)}, f32[4,512]{1,0:T(4,128)}, u32[]{:S(2)}) copy-start(f32[4,512]{1,0:T(4,128)} %get-tuple-element.54) | copy-start | bytes 24580
  261.9 3.3 %copy-start.51 = (f32[8]{0:T(128)S(1)}, f32[8]{0:T(128)}, u32[]{:S(2)}) copy-start(f32[8]{0:T(128)} %copy-done.50) | copy-start | bytes 100
  (23 other events, 17.7 us)

commit v3 on v2

v3 whole, which is shorter than its diff:
```python
import functools

import jax
import jax.numpy as jnp
from jax import lax
from jax.experimental import pallas as pl
from jax.experimental.pallas import tpu as pltpu
from jax.sharding import PartitionSpec as P


AXES = ("region", "survey")
EPS_SQ = 0.09
KERNEL_VMEM = 32 * 1024 * 1024
PART = 256
GROUP = 8


def swap(field):
    return lax.all_to_all(field, AXES, split_axis=0, concat_axis=0, tiled=True)


def edges(parts, both=True):
    rims = [[], []]
    for axis, (first, last) in (("region", parts[:2]), ("survey", parts[2:])):
        count = lax.axis_size(axis)
        rims[0].append(lax.ppermute(first, axis, [(i + 1, i) for i in range(count - 1)]))
        if both:
            rims[1].append(lax.ppermute(last, axis, [(i, i + 1) for i in range(count - 1)]))
    return rims[0] + rims[1]


WHOLE = pl.BlockSpec(memory_space=pltpu.VMEM)
FAR = pl.BlockSpec(memory_space=pltpu.HBM)


def far(array):
    return pltpu.with_memory_space_constraint(array, pltpu.HBM)


def kernel_call(kernel, table, near, distant, outs, distant_outs, scratch):
    near_specs = [WHOLE] * len(near)
    out_shapes = [pltpu.HBM(o.shape, o.dtype) for o in (*outs, *distant_outs)]
    return pl.pallas_call(
        kernel,
        out_shape=out_shapes,
        grid_spec=pltpu.PrefetchScalarGridSpec(
            num_scalar_prefetch=1,
            grid=(),
            in_specs=near_specs + [FAR] * len(distant),
            out_specs=[pl.BlockSpec(o.shape, functools.partial(origin, o.ndim)) for o in outs]
            + [FAR] * len(distant_outs),
            scratch_shapes=scratch,
        ),
        compiler_params=pltpu.CompilerParams(vmem_limit_bytes=KERNEL_VMEM),
    )(table, *near, *[far(d) for d in distant])


def origin(ndim, *_):
    return (0,) * ndim


def shape_of(dtype, *shape):
    return jax.ShapeDtypeStruct(shape, dtype)


def held(arrays):
    return [pltpu.VMEM(a.shape, a.dtype) for a in arrays] + [
        pltpu.SemaphoreType.DMA((len(arrays),))
    ]


def start_all(sources, targets, sems):
    copies = [
        pltpu.make_async_copy(source, target, sems.at[i])
        for i, (source, target) in enumerate(zip(sources, targets))
    ]
    for copy in copies:
        copy.start()
    return copies


def wait_all(copies):
    for copy in copies:
        copy.wait()


def start_pads(field_ref, pad, sem):
    layers, rows = field_ref.shape[:2]
    copy = pltpu.make_async_copy(field_ref, pad.at[pl.ds(0, layers), pl.ds(0, rows)], sem)
    copy.start()
    return copy


def fill_pads(pad, below, right):
    layers, rows = (pad.shape[0] - 1, pad.shape[1] - 1)
    pad[layers, pl.ds(0, rows)] = below[...].astype(pad.dtype)
    for layer in range(layers):
        pad[layer, rows] = right[layer].astype(pad.dtype)


def face(here, there, link):
    difference = here - there
    return difference, link * lax.rsqrt(difference * difference + EPS_SQ)


def levels(base, layer, depth_count):
    depth = (base + layer).astype(jnp.float32)
    return [1.0 + (2.0 * depth + offset) / depth_count for offset in (-1.0, 0.0, 1.0)]


def link_of(codes, number, level):
    return (lax.shift_right_logical(codes, number) & 1).astype(jnp.float32) * level


def next_lane(value):
    return pltpu.roll(value, value.shape[-1] - 1, value.ndim - 1)


def inner_lanes(cells):
    lane = lax.broadcasted_iota(jnp.int32, (GROUP, cells), 1)
    return (lane < cells - 1).astype(jnp.float32)


def step_from(got_ref, scale):
    sums = jnp.sum(got_ref[...], axis=0)
    norm, data, faces = (sums[:, i : i + 1] for i in range(3))
    return jnp.broadcast_to(norm / (data + scale[:, :1] * faces), scale.shape)


def prepare_kernel(start_ref, active_ref, model_ref, low_ref, top, bottom, left, right):
    layer = pl.program_id(0)
    rows = start_ref.shape[1]
    for start in range(0, rows, GROUP):
        live = active_ref[0, pl.ds(start, GROUP), :]
        for k in range(GROUP):
            value = start_ref[0, start + k] * live[k : k + 1]
            model_ref[0, start + k] = value
            low_ref[0, start + k] = value.astype(jnp.bfloat16)
    left[0] = model_ref[0, 0]
    right[0] = model_ref[0, rows - 1]

    @pl.when(layer == 0)
    def _():
        top[...] = model_ref[0]

    @pl.when(layer == pl.num_programs(0) - 1)
    def _():
        bottom[...] = model_ref[0]


def prepare_call(start_model, active):
    layers, rows, samples, cells = start_model.shape
    block = pl.BlockSpec((1, rows, samples, cells), lambda i: (i, 0, 0, 0))
    layer = pl.BlockSpec((rows, samples, cells), lambda i: (0, 0, 0))
    column = pl.BlockSpec((1, samples, cells), lambda i: (i, 0, 0))
    outs = [
        (start_model.shape, jnp.float32),
        (start_model.shape, jnp.bfloat16),
        *[((rows, samples, cells), jnp.float32)] * 2,
        *[((layers, samples, cells), jnp.float32)] * 2,
    ]
    return pl.pallas_call(
        prepare_kernel,
        name="prepare",
        grid=(layers,),
        in_specs=[block, pl.BlockSpec((1, rows, cells), lambda i: (i, 0, 0))],
        out_specs=[block, block, layer, layer, column, column],
        out_shape=[pltpu.HBM(*o) for o in outs],
        compiler_params=pltpu.CompilerParams(vmem_limit_bytes=KERNEL_VMEM),
    )(far(start_model), far(active))


def reg_kernel(first, depth_count, base_ref, *refs):
    if not first:
        got_ref, *refs = refs
    small_refs, refs = (refs[: 7 if first else 11], refs[7 if first else 11 :])
    if first:
        field_ref, edge_z, edge_y, reg_ref, *refs = refs
        out, pad, flow, sems, *refs = refs
    else:
        field_ref, grad_ref, edge_z, edge_y, step_ref, reg_ref, new_ref, *refs = refs
        out, pad, flow, sems, gpad, *refs = refs
    small, small_sems = (refs[:-1], refs[-1])
    copies = [start_pads(field_ref, pad, sems.at[0])]
    if not first:
        copies.append(start_pads(grad_ref, gpad, sems.at[1]))
    wait_all(start_all(small_refs, small, small_sems))
    links_ref, active_ref, scale_ref, below, right, above, left = small[:7]
    layers, rows = field_ref.shape[:2]
    base = base_ref[0]
    scale = scale_ref[...]
    fill_pads(pad, below, right)
    if not first:
        gbelow, gright, gabove, gleft = small[7:]
        fill_pads(gpad, gbelow, gright)
        step = step_from(got_ref, scale)
        step_ref[...] = step
    wait_all(copies)
    if not first:

        def move(layer, carry):
            for row in range(rows + 1):
                pad[layer, row] = pad[layer, row] - step * gpad[layer, row]
            return carry

        lax.fori_loop(0, layers, move, 0)
        for row in range(rows):
            pad[layers, row] = pad[layers, row] - step * gpad[layers, row]
        store = pltpu.make_async_copy(
            pad.at[pl.ds(0, layers), pl.ds(0, rows)], new_ref, sems.at[2]
        )
        store.start()
    inner = inner_lanes(pad.shape[-1])

    def prior(ref, gref, index):
        value = ref[index]
        if first:
            return value
        return value - step * gref[index].astype(jnp.float32)

    for start in range(0, rows, GROUP):
        codes = links_ref[pl.ds(start, GROUP), :]
        link = link_of(codes, 0, levels(base, 0, depth_count)[0])
        for k in range(GROUP):
            row = start + k
            came = prior(above, None if first else gabove, row)
            difference, weight = face(came, pad[0, row], link[k : k + 1])
            flow[row] = weight * difference

    def one(layer, carry):
        _, level, level_below = levels(base, layer, depth_count)
        flow_y = None
        for start in range(0, rows, GROUP):
            place = pl.ds(pl.multiple_of(layer * rows + start, GROUP), GROUP)
            codes = links_ref[place, :]
            link_z = link_of(codes, 1, level_below)
            link_y = link_of(codes, 3, level)
            link_x = link_of(codes, 5, level) * inner
            live = active_ref[place, :] * level
            if start == 0:
                came = prior(left, None if first else gleft, layer)
                link = link_of(codes, 2, level)
                difference, weight = face(came, pad[layer, 0], link[:1])
                flow_y = weight * difference
            for k in range(GROUP):
                row = start + k
                one_row = slice(k, k + 1)
                here = pad[layer, row]
                total = live[one_row] * lax.rsqrt(here * here + EPS_SQ) * here
                difference, weight = face(here, next_lane(here), link_x[one_row])
                flow_x = weight * difference
                total = total + flow_x - pltpu.roll(flow_x, 1, 1)
                difference, weight = face(here, pad[layer, row + 1], link_y[one_row])
                if row == rows - 1:
                    edge_y[layer] = weight
                out_y = weight * difference
                total = total + out_y - flow_y
                flow_y = out_y
                difference, weight = face(here, pad[layer + 1, row], link_z[one_row])
                edge_z[row] = weight
                out_z = weight * difference
                total = total + out_z - flow[row]
                flow[row] = out_z
                out[layer, row] = scale * total
        return carry

    lax.fori_loop(0, layers, one, 0)
    final = pltpu.make_async_copy(out, reg_ref, sems.at[3])
    final.start()
    final.wait()
    if not first:
        store.wait()


def reg_call(depth_count, base, links, active, scale, field, rims, moved=()):
    layers, rows, samples, cells = field.shape
    f32 = jnp.float32
    pad = pltpu.VMEM((layers + 1, rows + 1, samples, cells), f32)
    scratch = [
        pltpu.VMEM(field.shape, f32),
        pad,
        pltpu.VMEM((rows, samples, cells), f32),
        pltpu.SemaphoreType.DMA((4,)),
    ]
    near = []
    small = [links, active, scale, *rims]
    distant = [field]
    outs = [shape_of(f32, rows, samples, cells), shape_of(f32, layers, samples, cells)]
    distant_outs = [shape_of(f32, *field.shape)]
    if moved:
        got, grad, grad_rims = moved
        near = [got]
        small += grad_rims
        distant.append(grad)
        scratch.append(pad)
        outs.append(shape_of(f32, samples, cells))
        distant_outs *= 2
    return kernel_call(
        functools.partial(reg_kernel, not moved, depth_count),
        base,
        near,
        small + distant,
        outs,
        distant_outs,
        scratch + held(small),
    )


def curvature_kernel(
    depth_count, base_ref, links_ref, active_ref, field_ref, grad_ref, curv_ref, *refs
):
    links, active, field, grad, sems = refs
    layers, rows = field.shape[:2]
    base = base_ref[0]
    wait_all(
        start_all((field_ref, grad_ref, links_ref, active_ref), (field, grad, links, active), sems)
    )
    inner = inner_lanes(field.shape[-1])

    def one(layer, total):
        _, level, level_below = levels(base, layer, depth_count)
        below = jnp.minimum(layer + 1, layers - 1)
        level_below = jnp.where(layer + 1 < layers, level_below, 0.0)
        for start in range(0, rows, GROUP):
            place = pl.ds(pl.multiple_of(layer * rows + start, GROUP), GROUP)
            codes = links[place, :]
            link_z = link_of(codes, 1, level_below)
            link_y = link_of(codes, 3, level)
            link_x = link_of(codes, 5, level) * inner
            live = active[place, :] * level
            for k in range(GROUP):
                row = start + k
                one_row = slice(k, k + 1)
                here = field[layer, row]
                slope = grad[layer, row]
                part = live[one_row] * lax.rsqrt(here * here + EPS_SQ) * slope * slope
                pairs = [
                    (next_lane(here), next_lane(slope), link_x),
                    (field[below, row], grad[below, row], link_z),
                ]
                if row + 1 < rows:
                    pairs.append((field[layer, row + 1], grad[layer, row + 1], link_y))
                for there, gthere, link in pairs:
                    _, weight = face(here, there, link[one_row])
                    change = slope - gthere
                    part = part + weight * change * change
                total = total + part
        return total

    curv_ref[...] = lax.fori_loop(0, layers, one, jnp.zeros(curv_ref.shape, jnp.float32))


def curvature_call(depth_count, base, links, active, field, grad):
    (curv,) = kernel_call(
        functools.partial(curvature_kernel, depth_count),
        base,
        [],
        [links, active, field, grad],
        [shape_of(jnp.float32, *field.shape[2:])],
        [],
        held([links, active, field, grad]),
    )
    return curv


def load_sensors(sensor_ref, held_ref, sems, parts):
    height = held_ref.shape[1]
    copies = []
    for chunk in range(held_ref.shape[0]):
        rows = pl.ds(chunk % parts * height, height)
        copies.append(
            pltpu.make_async_copy(
                sensor_ref.at[chunk // parts, rows], held_ref.at[chunk], sems.at[chunk]
            )
        )
        copies[-1].start()


def wait_part(sensor_ref, held_ref, sems, tile, part, parts):
    height = held_ref.shape[1]
    chunk = tile * parts + part
    rows = pl.ds(part * height, height)
    pltpu.make_async_copy(
        sensor_ref.at[tile, rows], held_ref.at[chunk], sems.at[chunk]
    ).wait()


def gather_rows(width, slot_ref, arrived_ref, rows_ref):
    cells = arrived_ref.shape[2]

    def one(tile, carry):
        for entry in range(width):
            slot = slot_ref[tile * width + entry]
            rows_ref[tile, :, entry * cells : (entry + 1) * cells] = arrived_ref[slot]
        return carry

    lax.fori_loop(0, rows_ref.shape[0], one, 0)


def scatter_rows(tile, width, slot_ref, blocks, buffer_ref):
    cells = buffer_ref.shape[2]
    for entry in range(width):
        slot = slot_ref[tile * width + entry]
        block = blocks[:, entry * cells : (entry + 1) * cells]
        buffer_ref[slot] = block.astype(buffer_ref.dtype)


def project(rows, sensor):
    return lax.dot_general(
        rows, sensor, (((1,), (1,)), ((), ())), preferred_element_type=jnp.float32
    )


def forward_tile(tile, weight_of, rows_ref, held_ref, sensor_ref, sems, pred_ref, parts):
    height = held_ref.shape[1]
    given = []
    for part in range(parts):
        span = slice(part * height, (part + 1) * height)
        wait_part(sensor_ref, held_ref, sems, tile, part, parts)
        pred = project(rows_ref[tile], held_ref[tile * parts + part])
        pred_ref[tile, :, span] = pred
        given.append(weight_of(span, pred))
    return given


def backward_tile(tile, sent, held_ref, parts):
    blocks = 0.0
    for part in range(parts):
        blocks += jnp.dot(
            sent[part], held_ref[tile * parts + part], preferred_element_type=jnp.float32
        )
    return blocks


def residual_kernel(slot_ref, arrived_ref, sensor_ref, *refs):
    small_refs, refs = (refs[:2], refs[2:])
    pred_ref, buffer_ref, rows_ref, held_ref, sems, *small, small_sems = refs
    tiles = pred_ref.shape[0]
    parts = held_ref.shape[0] // tiles
    width = slot_ref.shape[0] // tiles
    copies = start_all(small_refs, small, small_sems)
    load_sensors(sensor_ref, held_ref, sems, parts)
    buffer_ref[...] = jnp.zeros_like(buffer_ref)
    gather_rows(width, slot_ref, arrived_ref, rows_ref)
    wait_all(copies)
    weight, observed = small

    def one(tile, carry):
        def weight_of(span, pred):
            residual = pred - observed[tile, :, span]
            return (weight[tile, :, span] * residual).astype(jnp.bfloat16)

        sent = forward_tile(
            tile, weight_of, rows_ref, held_ref, sensor_ref, sems, pred_ref, parts
        )
        blocks = backward_tile(tile, sent, held_ref, parts)
        scatter_rows(tile, width, slot_ref, blocks, buffer_ref)
        return carry

    lax.fori_loop(0, tiles, one, 0)


def forward_kernel(slot_ref, arrived_ref, sensor_ref, *refs):
    small_refs, refs = (refs[:9], refs[9:])
    pred_ref, sent_ref, rows_ref, held_ref, sems, *small, small_sems = refs
    tiles, samples = pred_ref.shape[:2]
    parts = held_ref.shape[0] // tiles
    width = slot_ref.shape[0] // tiles
    copies = start_all(small_refs, small, small_sems)
    load_sensors(sensor_ref, held_ref, sems, parts)
    gather_rows(width, slot_ref, arrived_ref, rows_ref)
    wait_all(copies)
    weight, norm, faces, *rims = small
    total = faces[...]
    for edge, mine, theirs in (rims[:3], rims[3:]):
        for row in range(edge.shape[0]):
            change = mine[row].astype(jnp.float32) - theirs[row].astype(jnp.float32)
            total = total + edge[row] * change * change

    def one(tile, curv):
        def weight_of(span, pred):
            return jnp.sum(weight[tile, :, span] * pred * pred, axis=1, keepdims=True)

        given = forward_tile(
            tile, weight_of, rows_ref, held_ref, sensor_ref, sems, pred_ref, parts
        )
        return curv + sum(given)

    data = lax.fori_loop(0, tiles, one, jnp.zeros((samples, 1), jnp.float32))
    sums = [jnp.sum(norm[...], axis=1, keepdims=True), data, jnp.sum(total, axis=1, keepdims=True)]
    lane = lax.broadcasted_iota(jnp.int32, total.shape, 1)
    block = jnp.zeros(total.shape, jnp.float32)
    for i, value in enumerate(sums):
        block = jnp.where(lane == i, value, block)
    sent_ref[...] = jnp.broadcast_to(block[None], sent_ref.shape)


def backward_kernel(slot_ref, sensor_ref, *refs):
    small_refs, refs = (refs[:2], refs[2:])
    buffer_ref, held_ref, sems, *small, small_sems = refs
    weight, pred = small
    tiles, samples = pred.shape[:2]
    height = held_ref.shape[1]
    parts = held_ref.shape[0] // tiles
    width = slot_ref.shape[0] // tiles
    copies = start_all(small_refs, small, small_sems)
    load_sensors(sensor_ref, held_ref, sems, parts)
    buffer_ref[...] = jnp.zeros_like(buffer_ref)
    wait_all(copies)

    def one(tile, carry):
        weighted = weight[tile] * pred[tile]
        upper = weighted.astype(jnp.bfloat16).astype(jnp.float32)
        both = jnp.concatenate([upper, weighted - upper], axis=0).astype(jnp.bfloat16)
        sent = [both[:, part * height : (part + 1) * height] for part in range(parts)]
        for part in range(parts):
            wait_part(sensor_ref, held_ref, sems, tile, part, parts)
        blocks = backward_tile(tile, sent, held_ref, parts)
        scatter_rows(tile, width, slot_ref, blocks[:samples] + blocks[samples:], buffer_ref)
        return carry

    lax.fori_loop(0, tiles, one, 0)


def tile_call(kernel, slot_of, near, sensor, small, outs, samples):
    tiles, data_slots, length = sensor.shape
    height = PART if data_slots % PART == 0 else data_slots
    chunks = tiles * data_slots // height
    scratch = [
        pltpu.VMEM((chunks, height, length), jnp.bfloat16),
        pltpu.SemaphoreType.DMA((chunks,)),
    ]
    if near:
        scratch = [pltpu.VMEM((tiles, samples, length), jnp.bfloat16)] + scratch
    return kernel_call(kernel, slot_of, near, [sensor, *small], outs, [], scratch + held(small))


def sum_kernel(first, layers, ids_ref, arrived_ref, *refs):
    active_ref, reg_ref, *refs = refs
    if not first:
        base_ref, step_ref, *refs = refs
    reply_ref, norm_ref, top, bottom, left, right, grad_ref, *refs = refs
    if first:
        data_ref, *refs = refs
        total, grad, out_sems, active, reg, sems = refs
        sources, targets = ((active_ref, reg_ref), (active, reg))
    else:
        total, grad, out_sems, active, reg, base, step_rows, sems = refs
        sources = (active_ref, reg_ref, base_ref, step_ref)
        targets = (active, reg, base, step_rows)
    copies = start_all(sources, targets, sems)
    count = ids_ref.shape[0]
    bricks = grad.shape[0]
    rows = bricks // layers
    total[...] = jnp.zeros_like(total)

    def add(i, carry):
        for k in range(GROUP):
            j = i * GROUP + k
            row = ids_ref[j]
            total[row] += arrived_ref[j].astype(jnp.float32)
        return carry

    lax.fori_loop(0, count // GROUP, add, 0)
    wait_all(copies)
    if not first:
        step = step_rows[...]

    def combine(i, norm):
        live = active[pl.ds(pl.multiple_of(i * GROUP, GROUP), GROUP), :]
        for k in range(GROUP):
            j = i * GROUP + k
            data = total[j]
            if not first:
                data = base[j] - step * data
            value = live[k : k + 1] * data + reg[j]
            grad[j] = value
            norm = norm + value * value
        return norm

    norm = lax.fori_loop(0, bricks // GROUP, combine, jnp.zeros(norm_ref.shape, jnp.float32))
    norm_ref[...] = norm
    if first:
        stores = start_all((grad, total), (grad_ref, data_ref), out_sems)
    else:
        stores = start_all((grad,), (grad_ref,), out_sems)

    def reply(i, carry):
        for k in range(GROUP):
            j = i * GROUP + k
            reply_ref[j] = grad[ids_ref[j]].astype(reply_ref.dtype)
        return carry

    lax.fori_loop(0, count // GROUP, reply, 0)
    top[...] = grad[pl.ds(0, rows)].astype(top.dtype)
    bottom[...] = grad[pl.ds(bricks - rows, rows)].astype(bottom.dtype)
    for layer in range(layers):
        left[layer] = grad[layer * rows].astype(left.dtype)
        right[layer] = grad[layer * rows + rows - 1].astype(right.dtype)
    wait_all(stores)


def sum_call(first, layers, ids, arrived, active, reg, *more):
    bricks, samples, cells = reg.shape
    small = [active, reg, *more]
    field = shape_of(jnp.float32, bricks, samples, cells)
    outs = [shape_of(jnp.bfloat16, *arrived.shape), shape_of(jnp.float32, samples, cells)]
    for length in (bricks // layers, bricks // layers, layers, layers):
        outs.append(shape_of(jnp.bfloat16, length, samples, cells))
    scratch = [
        pltpu.VMEM(field.shape, jnp.float32),
        pltpu.VMEM(field.shape, jnp.float32),
        pltpu.SemaphoreType.DMA((2 if first else 1,)),
    ]
    return kernel_call(
        functools.partial(sum_kernel, first, layers),
        ids,
        [arrived],
        small,
        outs,
        [field, field] if first else [field],
        scratch + held(small),
    )


def finish_kernel(
    got_ref, scale_ref, before_ref, mask_ref, observed_ref, pred_ref, moved_ref, last_ref,
    field_ref, grad_ref, model_ref, misfit_ref
):
    step = step_from(got_ref, scale_ref[...])
    model_ref[...] = field_ref[...] - step[None, None] * grad_ref[...]

    @pl.when(pl.program_id(0) == 0)
    def _():
        for tile in range(pred_ref.shape[0]):
            pred = pred_ref[tile] - before_ref[:, :1] * moved_ref[tile]
            pred = pred - step[:, :1] * last_ref[tile]
            misfit_ref[tile] = mask_ref[tile] * (pred - observed_ref[tile])


def finish_call(got, scale, before, mask, observed, pred, moved, last, field, grad):
    layers, rows, samples, cells = field.shape
    block = 4 if layers % 4 == 0 else 1
    spec = pl.BlockSpec((block, rows, samples, cells), lambda i: (i, 0, 0, 0))

    def fixed(array):
        return pl.BlockSpec(array.shape, lambda i: (0,) * array.ndim)

    small = [scale, before, mask, observed, pred, moved, last]
    return pl.pallas_call(
        finish_kernel,
        name="finish",
        grid=(layers // block,),
        in_specs=[WHOLE] + [fixed(a) for a in small] + [spec, spec],
        out_specs=[spec, fixed(observed)],
        out_shape=[pltpu.HBM(a.shape, a.dtype) for a in (field, observed)],
        compiler_params=pltpu.CompilerParams(vmem_limit_bytes=KERNEL_VMEM),
    )(got, *[far(a) for a in (*small, field, grad)])


def shards(
    sensitivity,
    observed,
    data_weight,
    data_counts,
    tile_bricks,
    start_model,
    active_cells,
    face_links,
    reg_weight,
):
    layers, strip_rows, samples, cells_x = start_model.shape
    tiles, tile_width = tile_bricks.shape
    data_slots = sensitivity.shape[1]
    owners = lax.axis_size("region") * lax.axis_size("survey")
    per_owner = layers * strip_rows
    capacity = max(2, 2 * tiles * tile_width // owners)
    slots = owners * capacity
    depth_count = layers * lax.axis_size("region")
    requests = tile_bricks.reshape(-1)
    owner_of = requests // per_owner
    local_of = requests % per_owner
    owner_hits = (owner_of[:, None] == jnp.arange(owners, dtype=jnp.int32)[None, :]).astype(
        jnp.int32
    )
    before = jnp.cumsum(owner_hits, axis=0) - owner_hits
    rank_of = jnp.sum(before * owner_hits, axis=1)
    slot_of = owner_of * capacity + rank_of
    slot_hits = slot_of[:, None] == jnp.arange(slots, dtype=jnp.int32)[None, :]
    asking = jnp.sum(jnp.where(slot_hits, local_of[:, None], 0), axis=0).reshape(owners, capacity)
    asked_ids = swap(asking).reshape(-1)

    active_rows = active_cells.astype(jnp.float32)
    active_flat = active_rows.reshape(per_owner, cells_x)
    links = face_links.reshape(per_owner, cells_x)
    base = (lax.axis_index("region") * layers).astype(jnp.int32).reshape(1)
    row_mask = (
        jnp.arange(data_slots, dtype=jnp.int32)[None, None, :] < data_counts[:, None, None]
    ).astype(jnp.float32)
    weight_sq = row_mask * (data_weight * data_weight)[:, None, :]
    mask = row_mask * data_weight[:, None, :]
    reg_rows = jnp.broadcast_to(reg_weight[:, None], (samples, cells_x))
    f32, bf16 = (jnp.float32, jnp.bfloat16)
    pred_shape = shape_of(f32, tiles, samples, data_slots)
    buffer_shape = shape_of(bf16, slots, samples, cells_x)

    def exchange(blocks):
        return swap(blocks.reshape(owners, capacity, samples, cells_x)).reshape(
            slots, samples, cells_x
        )

    def flat(field):
        return field.reshape(per_owner, samples, cells_x)

    def forward(arrived, norm, faces, edge_z, edge_y, rims, theirs):
        small = [weight_sq, norm, faces, edge_z, rims[1], theirs[0], edge_y, rims[3], theirs[1]]
        outs = [pred_shape, shape_of(f32, owners, samples, cells_x)]
        return tile_call(forward_kernel, slot_of, [arrived], sensitivity, small, outs, samples)

    grid = (depth_count, base, links, active_flat)
    model, bricks, *rims = prepare_call(start_model, active_rows)
    replies = flat(bricks)[asked_ids]
    arrived = exchange(replies)
    model_rims = edges(rims)
    pred, buffer = tile_call(
        residual_kernel,
        slot_of,
        [arrived],
        sensitivity,
        [weight_sq, observed],
        [pred_shape, buffer_shape],
        samples,
    )

    arrived = exchange(buffer)
    edge_z, edge_y, reg = reg_call(*grid, reg_rows, model, model_rims)
    replies, norm, *rims, grad, data_sum = sum_call(
        True, layers, asked_ids, arrived, active_flat, flat(reg)
    )
    arrived = exchange(replies)
    grad_rims = edges(rims)
    grad = grad.reshape(start_model.shape)
    faces = curvature_call(*grid, model, grad)
    step_pred, sums = forward(arrived, norm, faces, edge_z, edge_y, rims, grad_rims)
    got = swap(sums)
    (buffer,) = tile_call(
        backward_kernel, slot_of, [], sensitivity, [weight_sq, step_pred], [buffer_shape], samples
    )
    arrived = exchange(buffer)

    edge_z, edge_y, step, reg, model = reg_call(
        *grid, reg_rows, model, model_rims, (got, grad, grad_rims)
    )
    replies, norm, *rims, grad = sum_call(
        False, layers, asked_ids, arrived, active_flat, flat(reg), data_sum, step
    )
    arrived = exchange(replies)
    grad_rims = edges(rims, both=False)
    grad = grad.reshape(start_model.shape)
    faces = curvature_call(*grid, model, grad)
    last_pred, sums = forward(arrived, norm, faces, edge_z, edge_y, rims, grad_rims)
    got = swap(sums)
    return tuple(
        finish_call(got, reg_rows, step, mask, observed, pred, step_pred, last_pred, model, grad)
    )


def solution(mesh):
    return jax.shard_map(
        shards,
        mesh=mesh,
        in_specs=(
            P(("region", "survey"), None, None),
            P(("region", "survey"), None, None),
            P(("region", "survey"), None),
            P(("region", "survey")),
            P(("region", "survey"), None),
            P("region", "survey", None, None),
            P("region", "survey", None),
            P("region", "survey", None),
            P(),
        ),
        out_specs=(P("region", "survey", None, None), P(("region", "survey"), None, None)),
        check_vma=False,
    )
```

time: 268 us -> 240 us (0.90)
  local copies, waits for them, and re-layouts: 64.8 us -> 7.68 us
  Pallas kernels: 67 us -> 116 us
  blocking collectives: 16.4 us -> 0 us
  other arithmetic: 16.9 us -> 3.01 us
  waiting for transfers between devices: 30.5 us -> 40 us
    unnamed x108 -> x38, local copies, waits for them, and re-layouts: 53.4 us -> 0.86 us
    pallas_call x10 -> x12, Pallas kernels: 67 us -> 116 us  [the longest x10 101 us: kernel_call(): pl.pallas_call(kernel, out_shape=out_shapes, grid_spec=pltpu.PrefetchScal...]
    all_to_all x7 -> x8, waiting for transfers between devices: 20 us -> 36.9 us  [swap(): return lax.all_to_all(field, AXES, split_axis=0, concat_axis=0, tiled=True)]
    all_to_all x1 -> x0, blocking collectives: 16.4 us -> none  [swap(): return lax.all_to_all(field, AXES, split_axis=0, concat_axis=0, tiled=True)]
    ppermute x6, waiting for transfers between devices: 9.72 us -> 0.02 us  [edges(): lax.ppermute(first, axis, [(i + 1, i) for i in range(count - 1)])]
    reduce_sum x8 -> x0, other arithmetic: 3.92 us -> none  [the longest x2 1.41 us: step_of(): jnp.sum(norm, axis=1)]
    convert_element_type x1 -> x0, other arithmetic: 3.32 us -> none  [shards(): bricks = model.astype(jnp.bfloat16).reshape(per_owner, samples, cells_x)]
    sub x1 -> x0, other arithmetic: 3.23 us -> none  [shards(): model = model - step[None, None, :, None] * grad]
  transfers between devices with their start and end apart: 17 -> 18, of which waited for: 9 -> 7; matrix products, arithmetic and copies ran while one was open for 7% -> 2% of each run, Pallas kernels for 8% -> 20%
where the time goes in v3:
time: 240 us; the launch traced here: 238 us
  Pallas kernels  116 us (48%)
  starting transfers between devices  70.3 us (29%)
  waiting for transfers between devices  40 us (17%)
  local copies, waits for them, and re-layouts  7.68 us (3%)
  other arithmetic  3.01 us (1%)
    pallas_call x10, Pallas kernels, kernel_call(): pl.pallas_call(kernel, out_shape=out_shapes, grid_spec=pltpu.PrefetchScal...  101 us
    all_to_all x8, starting transfers between devices, swap(): return lax.all_to_all(field, AXES, split_axis=0, concat_axis=0, tiled=True)  49.5 us
    all_to_all x8, waiting for transfers between devices, swap(): return lax.all_to_all(field, AXES, split_axis=0, concat_axis=0, tiled=True)  36.9 us
    ppermute x4, starting transfers between devices, edges(): lax.ppermute(last, axis, [(i, i + 1) for i in range(count - 1)])  13 us
    pallas_call x1, Pallas kernels, prepare_call(): pl.pallas_call(prepare_kernel, name='prepare', grid=(layers,), in_specs=[...  9.84 us
    ppermute x6, starting transfers between devices, edges(): lax.ppermute(first, axis, [(i + 1, i) for i in range(count - 1)])  7.75 us
    pallas_call x1, Pallas kernels, finish_call(): pl.pallas_call(finish_kernel, name='finish', grid=(layers // block,), in_...  4.97 us
  transfers between devices with their start and end apart: 18, of which 7 were waited for; matrix products, arithmetic and copies ran while one was open for 2% of the time, Pallas kernels for 20%

profile of v3, /device:TPU:0, one launch (start us, length us, event | category | flops | bytes accessed | tf_op | source)
XLA Modules:
  0.0 238.2 jit_solution(2628218411243936478)
XLA Ops:
  0.6 0.8 reshape.170
  1.5 0.2 reduce_window_sum.11
  2.0 0.7 all_to_all.27
  2.7 7.3 %all-to-all-start = ((s32[32,1,8]{2,1,0:T(1,128)}), s32[32,1,8]{2,1,0:T(1,128)S(1)}, u32[]{:S(2)}, u32[]{:S(2)}) async-start(s32[32,1,8]{2,1,0:T(1,128)} %bitcast), calls=%async_computation | async-start | bytes 32768 | tf_op jit(solution)/shard_map/all_to_all | solution.py:19
  10.0 1.7 convert_element_type.8.active_ref
  11.7 9.8 %prepare.1 = (f32[16,32,8,128]{3,2,1,0:T(8,128)}, bf16[16,32,8,128]{3,2,1,0:T(8,128)(2,1)}, f32[32,8,128]{2,1,0:T(8,128)}, f32[32,8,128]{2,1,0:T(8,128)}, f32[16,8,128]{2,1,0:T(8,128)}, /*index=5*/f32[16,8,128]{2,1,0:T(8,128)}) custom-call(f32[16,32,8,128]{3,2,1,0:T(8,128)} %start_ref.1, f32[16,32,128]{2,1,0:T(8,128)} %convert_element_type.8.active_ref), custom_call_target="tpu_custom_call" | custom-call | tf_op jit(solution)/shard_map/prepare/pallas_call | solution.py:162
  21.7 2.8 %gather_fusion = bf16[256,8,128]{2,1,0:T(8,128)(2,1)} fusion(bf16[512,8,128]{2,1,0:T(8,128)(2,1)} %bitcast.48, s32[1024]{0:T(1024)S(1)} %pad_clamp_fusion), kind=kCustom, calls=%fused_computation | custom fusion | bytes 1049600 | tf_op jit(solution)/shard_map/gather | solution.py:722
  24.5 5.8 %all-to-all-start.1 = ((bf16[32,8,8,128]{3,2,1,0:T(8,128)(2,1)}), bf16[32,8,8,128]{3,2,1,0:T(8,128)(2,1)S(1)}, u32[]{:S(2)}, u32[]{:S(2)}) async-start(bf16[32,8,8,128]{3,2,1,0:T(8,128)(2,1)} %bitcast.4), calls=%async_computation.1 | async-start | bytes 1048576 | tf_op jit(solution)/shard_map/all_to_all | solution.py:19
  30.4 0.6 copy.27.refs_0_
  31.0 14.9 %all-to-all-done.1 = bf16[32,8,8,128]{3,2,1,0:T(8,128)(2,1)S(1)} async-done(((bf16[32,8,8,128]{3,2,1,0:T(8,128)(2,1)}), bf16[32,8,8,128]{3,2,1,0:T(8,128)(2,1)S(1)}, u32[]{:S(2)}, u32[]{:S(2)}) %all-to-all-start.1) | async-done | bytes 524320 | tf_op jit(solution)/shard_map/all_to_all | solution.py:19
  45.9 18.6 %shard_map.104 = (f32[4,8,512]{2,1,0:T(8,128)}, bf16[256,8,128]{2,1,0:T(8,128)(2,1)}) custom-call(s32[128]{0:T(128)S(1)} %multiply_add_fusion.slot_ref, bf16[256,8,128]{2,1,0:T(8,128)(2,1)S(1)} %bitcast.26, bf16[4,512,4096]{2,1,0:T(8,128)(2,1)} %sensor_ref.7, f32[4,1,512]{2,1,0:T(1,128)} %copy.27.refs_0_, f32[4,8,512]{2,1,0:T(8,128)} %observed_ref.1), custom_call_target="tpu_custom_call" | custom-call | tf_op jit(solution)/shard_map/pallas_call | solution.py:43
  64.5 3.0 %all-to-all-start.2 = ((bf16[32,8,8,128]{3,2,1,0:T(8,128)(2,1)}), bf16[32,8,8,128]{3,2,1,0:T(8,128)(2,1)S(1)}, u32[]{:S(2)}, u32[]{:S(2)}) async-start(bf16[32,8,8,128]{3,2,1,0:T(8,128)(2,1)} %bitcast.45), calls=%async_computation.2 | async-start | bytes 1048576 | tf_op jit(solution)/shard_map/all_to_all | solution.py:19
  67.5 1.3 collective-permute-start
  68.9 4.6 %collective-permute-start.2 = (f32[32,8,128]{2,1,0:T(8,128)S(1)}, f32[32,8,128]{2,1,0:T(8,128)S(1)}, u32[]{:S(2)}, u32[]{:S(2)}) collective-permute-start(f32[32,8,128]{2,1,0:T(8,128)S(1)} %copy-done.15), channel_id=1, source_target_pairs={{0,4},{4,8},{8,12},{12,16},{16,20},{20,24},{24,28},{1,5},{5,9},{9,... | collective-permute-start | bytes 393224 | tf_op jit(solution)/shard_map/ppermute | solution.py:28
  73.4 1.3 collective-permute-start.1
  74.7 3.0 %collective-permute-start.3 = (f32[16,8,128]{2,1,0:T(8,128)S(1)}, f32[16,8,128]{2,1,0:T(8,128)S(1)}, u32[]{:S(2)}, u32[]{:S(2)}) collective-permute-start(f32[16,8,128]{2,1,0:T(8,128)S(1)} %copy-done.17), channel_id=1, source_target_pairs={{0,1},{1,2},{2,3},{4,5},{5,6},{6,7},{8,9},{9,10},{10,11},{12,13},{... | collective-permute-start | bytes 196616 | tf_op jit(solution)/shard_map/ppermute | solution.py:28
  77.8 0.5 broadcast.134
  78.3 0.7 reduce.5
  79.1 1.9 collective-permute-done.2.refs_5_.refs_6_
  81.0 0.7 broadcast_in_dim.16.refs_2_.refs_3_.scale_ref
  81.7 7.4 %shard_map.105 = (f32[32,8,128]{2,1,0:T(8,128)}, f32[16,8,128]{2,1,0:T(8,128)}, f32[16,32,8,128]{3,2,1,0:T(8,128)}) custom-call(s32[1]{0:T(128)} %bitcast.9.base_ref, s32[512,128]{1,0:T(8,128)} %bitcast.38, f32[512,128]{1,0:T(8,128)} %bitcast.28, f32[8,128]{1,0:T(8,128)} %broadcast_in_dim.16.refs_2_.refs_3_.scale_ref, f32[32,8,128]{2,1,0:T(8,128)} %copy-done, ...), custom_call_target="tpu_custom_call" | custom-call | tf_op jit(solution)/shard_map/pallas_call | solution.py:43
  89.1 6.0 %shard_map.106 = (bf16[256,8,128]{2,1,0:T(8,128)(2,1)}, f32[8,128]{1,0:T(8,128)}, bf16[32,8,128]{2,1,0:T(8,128)(2,1)}, bf16[32,8,128]{2,1,0:T(8,128)(2,1)}, bf16...) custom-call(s32[256]{0:T(256)S(1)} %reshape.171.ids_ref, ...), custom_call_target="tpu_custom_call" | custom-call | tf_op jit(solution)/shard_map/pallas_call | solution.py:43
  95.1 7.1 %all-to-all-start.3 = ((bf16[32,8,8,128]{3,2,1,0:T(8,128)(2,1)}), bf16[32,8,8,128]{3,2,1,0:T(8,128)(2,1)S(1)}, u32[]{:S(2)}, u32[]{:S(2)}) async-start(bf16[32,8,8,128]{3,2,1,0:T(8,128)(2,1)} %bitcast.47), calls=%async_computation.3 | async-start | bytes 1048576 | tf_op jit(solution)/shard_map/all_to_all | solution.py:19
  102.2 1.3 collective-permute-start.4
  103.5 1.3 collective-permute-start.5
  104.8 5.8 %shard_map.107.refs_2_ = f32[8,128]{1,0:T(8,128)} custom-call(s32[1]{0:T(128)} %bitcast.9.base_ref, s32[512,128]{1,0:T(8,128)} %bitcast.39, f32[512,128]{1,0:T(8,128)} %bitcast.30, f32[16,32,8,128]{3,2,1,0:T(8,128)} %get-tuple-element.43.refs_7_.field_ref.refs_12_, f32[16,32,8,128]{3,2,1,0:T(8,128)} %bitcast.34), custom_call_target="tpu_custom_call" | custom-call | tf_op jit(solution)/shard_map/pallas_call | solution.py:43
  110.6 7.2 %all-to-all-done.3 = bf16[32,8,8,128]{3,2,1,0:T(8,128)(2,1)S(1)} async-done(((bf16[32,8,8,128]{3,2,1,0:T(8,128)(2,1)}), bf16[32,8,8,128]{3,2,1,0:T(8,128)(2,1)S(1)}, u32[]{:S(2)}, u32[]{:S(2)}) %all-to-all-start.3) | async-done | bytes 524320 | tf_op jit(solution)/shard_map/all_to_all | solution.py:19
  117.8 16.7 %shard_map.108 = (f32[4,8,512]{2,1,0:T(8,128)}, f32[32,8,128]{2,1,0:T(8,128)}) custom-call(s32[128]{0:T(128)S(1)} %multiply_add_fusion.slot_ref, bf16[256,8,128]{2,1,0:T(8,128)(2,1)S(1)} %bitcast.25, bf16[4,512,4096]{2,1,0:T(8,128)(2,1)} %sensor_ref.7, f32[4,1,512]{2,1,0:T(1,128)} %copy.27.refs_0_, f32[8,128]{1,0:T(8,128)} %get-tuple-element.46.refs_1_, ...), custom_call_target="tpu_custom_call" | custom-call | tf_op jit(solution)/shard_map/pallas_call | solution.py:43
  134.6 4.1 %all-to-all-start.5 = ((f32[32,8,128]{2,1,0:T(8,128)}), f32[32,8,128]{2,1,0:T(8,128)S(1)}, u32[]{:S(2)}, u32[]{:S(2)}) async-start(f32[32,8,128]{2,1,0:T(8,128)} %get-tuple-element.55), calls=%async_computation.5 | async-start | bytes 262144 | tf_op jit(solution)/shard_map/all_to_all | solution.py:19
  138.7 9.2 %shard_map.109 = bf16[256,8,128]{2,1,0:T(8,128)(2,1)} custom-call(s32[128]{0:T(128)S(1)} %multiply_add_fusion.slot_ref, bf16[4,512,4096]{2,1,0:T(8,128)(2,1)} %sensor_ref.7, f32[4,1,512]{2,1,0:T(1,128)} %copy.27.refs_0_, f32[4,8,512]{2,1,0:T(8,128)} %get-tuple-element.54.refs_1_.moved_ref), custom_call_target="tpu_custom_call" | custom-call | tf_op jit(solution)/shard_map/pallas_call | solution.py:43
  148.0 5.8 %all-to-all-start.4 = ((bf16[32,8,8,128]{3,2,1,0:T(8,128)(2,1)}), bf16[32,8,8,128]{3,2,1,0:T(8,128)(2,1)S(1)}, u32[]{:S(2)}, u32[]{:S(2)}) async-start(bf16[32,8,8,128]{3,2,1,0:T(8,128)(2,1)} %bitcast.42), calls=%async_computation.4 | async-start | bytes 1048576 | tf_op jit(solution)/shard_map/all_to_all | solution.py:19
  153.8 3.7 %collective-permute-start.6 = (bf16[32,8,128]{2,1,0:T(8,128)(2,1)S(1)}, bf16[32,8,128]{2,1,0:T(8,128)(2,1)S(1)}, u32[]{:S(2)}, u32[]{:S(2)}) collective-permute-start(bf16[32,8,128]{2,1,0:T(8,128)(2,1)S(1)} %copy-done.6), channel_id=1, source_target_pairs={{0,4},{4,8},{8,12},{12,16},{16,20},{20,24},{24,28},{1,5},{5,9},{9,... | collective-permute-start | bytes 196616 | tf_op jit(solution)/shard_map/ppermute | solution.py:28
  157.5 1.7 collective-permute-start.7
  159.3 0.8 collective-permute-done.7.refs_11_
  160.1 0.4 collective-permute-done.6.refs_10_
  160.7 0.6 copy-done.8
  161.3 8.8 %shard_map.110 = (f32[32,8,128]{2,1,0:T(8,128)}, f32[16,8,128]{2,1,0:T(8,128)}, f32[8,128]{1,0:T(8,128)}, f32[16,32,8,128]{3,2,1,0:T(8,128)}, f32[16,32,8,128]{3,2,1,0:T(8,128)}) custom-call(s32[1]{0:T(128)} %bitcast.9.base_ref, f32[32,8,128]{2,1,0:T(8,128)S(1)} %all-to-all-done.5.refs_0_, s32[512,128]{1,0:T(8,128)} %bitcast.40, f32[512,128]{1,0:T(8,128)} %bitcast.31, ...), custom_call_target="tpu_custom_call" | custom-call | tf_op jit(solution)/shard_map/pallas_call | solution.py:43
  170.1 6.1 %shard_map.111 = (bf16[256,8,128]{2,1,0:T(8,128)(2,1)}, f32[8,128]{1,0:T(8,128)}, bf16[32,8,128]{2,1,0:T(8,128)(2,1)}, bf16[32,8,128]{2,1,0:T(8,128)(2,1)}, bf16...) custom-call(s32[256]{0:T(256)S(1)} %reshape.171.ids_ref, ...), custom_call_target="tpu_custom_call" | custom-call | tf_op jit(solution)/shard_map/pallas_call | solution.py:43
  176.3 12.2 %all-to-all-start.6 = ((bf16[32,8,8,128]{3,2,1,0:T(8,128)(2,1)}), bf16[32,8,8,128]{3,2,1,0:T(8,128)(2,1)S(1)}, u32[]{:S(2)}, u32[]{:S(2)}) async-start(bf16[32,8,8,128]{3,2,1,0:T(8,128)(2,1)} %bitcast.46), calls=%async_computation.6 | async-start | bytes 1048576 | tf_op jit(solution)/shard_map/all_to_all | solution.py:19
  188.5 1.3 collective-permute-start.8
  189.8 1.3 collective-permute-start.9
  191.1 5.8 %shard_map.112.refs_2_ = f32[8,128]{1,0:T(8,128)} custom-call(s32[1]{0:T(128)} %bitcast.9.base_ref, s32[512,128]{1,0:T(8,128)} %bitcast.41, f32[512,128]{1,0:T(8,128)} %bitcast.33, f32[16,32,8,128]{3,2,1,0:T(8,128)} %get-tuple-element.61.field_ref, f32[16,32,8,128]{3,2,1,0:T(8,128)} %bitcast.36), custom_call_target="tpu_custom_call" | custom-call | tf_op jit(solution)/shard_map/pallas_call | solution.py:43
  197.0 7.2 %all-to-all-done.6 = bf16[32,8,8,128]{3,2,1,0:T(8,128)(2,1)S(1)} async-done(((bf16[32,8,8,128]{3,2,1,0:T(8,128)(2,1)}), bf16[32,8,8,128]{3,2,1,0:T(8,128)(2,1)S(1)}, u32[]{:S(2)}, u32[]{:S(2)}) %all-to-all-start.6) | async-done | bytes 524320 | tf_op jit(solution)/shard_map/all_to_all | solution.py:19
  204.1 16.7 %shard_map.113 = (f32[4,8,512]{2,1,0:T(8,128)}, f32[32,8,128]{2,1,0:T(8,128)}) custom-call(s32[128]{0:T(128)S(1)} %multiply_add_fusion.slot_ref, bf16[256,8,128]{2,1,0:T(8,128)(2,1)S(1)} %bitcast.24, bf16[4,512,4096]{2,1,0:T(8,128)(2,1)} %sensor_ref.7, f32[4,1,512]{2,1,0:T(1,128)} %copy.27.refs_0_, f32[8,128]{1,0:T(8,128)} %get-tuple-element.60.refs_1_, ...), custom_call_target="tpu_custom_call" | custom-call | tf_op jit(solution)/shard_map/pallas_call | solution.py:43
  220.9 4.1 %all-to-all-start.7 = ((f32[32,8,128]{2,1,0:T(8,128)}), f32[32,8,128]{2,1,0:T(8,128)S(1)}, u32[]{:S(2)}, u32[]{:S(2)}) async-start(f32[32,8,128]{2,1,0:T(8,128)} %get-tuple-element.69), calls=%async_computation.7 | async-start | bytes 262144 | tf_op jit(solution)/shard_map/all_to_all | solution.py:19
  225.0 0.6 mul.37.mask_ref
  225.6 7.6 %all-to-all-done.7.got_ref = f32[32,8,128]{2,1,0:T(8,128)S(1)} async-done(((f32[32,8,128]{2,1,0:T(8,128)}), f32[32,8,128]{2,1,0:T(8,128)S(1)}, u32[]{:S(2)}, u32[]{:S(2)}) %all-to-all-start.7) | async-done | bytes 131104 | tf_op jit(solution)/shard_map/all_to_all | solution.py:19
  233.2 5.0 %finish.1 = (f32[16,32,8,128]{3,2,1,0:T(8,128)}, f32[4,8,512]{2,1,0:T(8,128)}) custom-call(f32[32,8,128]{2,1,0:T(8,128)S(1)} %all-to-all-done.7.got_ref, f32[8,128]{1,0:T(8,128)} %broadcast_in_dim.16.refs_2_.refs_3_.scale_ref, f32[8,128]{1,0:T(8,128)} %get-tuple-element.58.refs_3_.before_ref, f32[4,1,512]{2,1,0:T(1,128)} %mul.37.mask_ref, ...), custom_call_target="tpu_custom_call" | custom-call | tf_op jit(solution)/shard_map/finish/pallas_call | solution.py:650
  (58 shorter events, 0.9 us)
Async XLA Ops:
  2.7 18.9 %all-to-all-start = ((s32[32,1,8]{2,1,0:T(1,128)}), s32[32,1,8]{2,1,0:T(1,128)S(1)}, u32[]{:S(2)}, u32[]{:S(2)}) async-start(s32[32,1,8]{2,1,0:T(1,128)} %bitcast), calls=%async_computation | async-start | bytes 32768 | tf_op jit(solution)/shard_map/all_to_all | solution.py:19
  11.7 18.6 %copy-start.12 = (f32[4,512]{1,0:T(4,128)S(1)}, f32[4,512]{1,0:T(4,128)}, u32[]{:S(2)}) copy-start(f32[4,512]{1,0:T(4,128)} %param.11) | copy-start | bytes 24580
  11.7 18.6 %copy-start.13 = (s32[4]{0:T(128)S(1)}, s32[4]{0:T(128)}, u32[]{:S(2)}) copy-start(s32[4]{0:T(128)} %param.12) | copy-start | bytes 52
  24.5 21.5 %all-to-all-start.1 = ((bf16[32,8,8,128]{3,2,1,0:T(8,128)(2,1)}), bf16[32,8,8,128]{3,2,1,0:T(8,128)(2,1)S(1)}, u32[]{:S(2)}, u32[]{:S(2)}) async-start(bf16[32,8,8,128]{3,2,1,0:T(8,128)(2,1)} %bitcast.4), calls=%async_computation.1 | async-start | bytes 1048576 | tf_op jit(solution)/shard_map/all_to_all | solution.py:19
  45.9 21.6 %copy-start.16 = (f32[32,8,128]{2,1,0:T(8,128)S(1)}, f32[32,8,128]{2,1,0:T(8,128)}, u32[]{:S(2)}) copy-start(f32[32,8,128]{2,1,0:T(8,128)} %get-tuple-element.39) | copy-start | bytes 393220
  45.9 22.9 %copy-start.15 = (f32[32,8,128]{2,1,0:T(8,128)S(1)}, f32[32,8,128]{2,1,0:T(8,128)}, u32[]{:S(2)}) copy-start(f32[32,8,128]{2,1,0:T(8,128)} %get-tuple-element.41) | copy-start | bytes 393220
  45.9 27.5 %copy-start.18 = (f32[16,8,128]{2,1,0:T(8,128)S(1)}, f32[16,8,128]{2,1,0:T(8,128)}, u32[]{:S(2)}) copy-start(f32[16,8,128]{2,1,0:T(8,128)} %get-tuple-element.40) | copy-start | bytes 196612
  45.9 28.8 %copy-start.17 = (f32[16,8,128]{2,1,0:T(8,128)S(1)}, f32[16,8,128]{2,1,0:T(8,128)}, u32[]{:S(2)}) copy-start(f32[16,8,128]{2,1,0:T(8,128)} %get-tuple-element.42) | copy-start | bytes 196612
  45.9 35.1 %copy-start.14 = (f32[8]{0:T(128)S(1)}, f32[8]{0:T(128)}, u32[]{:S(2)}) copy-start(f32[8]{0:T(128)} %param.17) | copy-start | bytes 100
  64.5 24.5 %all-to-all-start.2 = ((bf16[32,8,8,128]{3,2,1,0:T(8,128)(2,1)}), bf16[32,8,8,128]{3,2,1,0:T(8,128)(2,1)S(1)}, u32[]{:S(2)}, u32[]{:S(2)}) async-start(bf16[32,8,8,128]{3,2,1,0:T(8,128)(2,1)} %bitcast.45), calls=%async_computation.2 | async-start | bytes 1048576 | tf_op jit(solution)/shard_map/all_to_all | solution.py:19
  67.5 11.6 %collective-permute-start = (f32[32,8,128]{2,1,0:T(8,128)S(1)}, f32[32,8,128]{2,1,0:T(8,128)S(1)}, u32[]{:S(2)}, u32[]{:S(2)}) collective-permute-start(f32[32,8,128]{2,1,0:T(8,128)S(1)} %copy-done.16), channel_id=1, source_target_pairs={{4,0},{8,4},{12,8},{16,12},{20,16},{24,20},{28,24},{5,1},{9,5},{13... | collective-permute-start | bytes 393224 | tf_op jit(solution)/shard_map/ppermute | solution.py:26
  68.9 12.1 %collective-permute-start.2 = (f32[32,8,128]{2,1,0:T(8,128)S(1)}, f32[32,8,128]{2,1,0:T(8,128)S(1)}, u32[]{:S(2)}, u32[]{:S(2)}) collective-permute-start(f32[32,8,128]{2,1,0:T(8,128)S(1)} %copy-done.15), channel_id=1, source_target_pairs={{0,4},{4,8},{8,12},{12,16},{16,20},{20,24},{24,28},{1,5},{5,9},{9,... | collective-permute-start | bytes 393224 | tf_op jit(solution)/shard_map/ppermute | solution.py:28
  73.4 5.7 %collective-permute-start.1 = (f32[16,8,128]{2,1,0:T(8,128)S(1)}, f32[16,8,128]{2,1,0:T(8,128)S(1)}, u32[]{:S(2)}, u32[]{:S(2)}) collective-permute-start(f32[16,8,128]{2,1,0:T(8,128)S(1)} %copy-done.18), channel_id=1, source_target_pairs={{1,0},{2,1},{3,2},{5,4},{6,5},{7,6},{9,8},{10,9},{11,10},{13,12},{... | collective-permute-start | bytes 196616 | tf_op jit(solution)/shard_map/ppermute | solution.py:26
  74.7 4.4 %collective-permute-start.3 = (f32[16,8,128]{2,1,0:T(8,128)S(1)}, f32[16,8,128]{2,1,0:T(8,128)S(1)}, u32[]{:S(2)}, u32[]{:S(2)}) collective-permute-start(f32[16,8,128]{2,1,0:T(8,128)S(1)} %copy-done.17), channel_id=1, source_target_pairs={{0,1},{1,2},{2,3},{4,5},{5,6},{6,7},{8,9},{9,10},{10,11},{12,13},{... | collective-permute-start | bytes 196616 | tf_op jit(solution)/shard_map/ppermute | solution.py:28
  79.1 2.6 %copy-start.3 = (f32[16,8,128]{2,1,0:T(8,128)}, f32[16,8,128]{2,1,0:T(8,128)S(1)}, u32[]{:S(2)}) copy-start(f32[16,8,128]{2,1,0:T(8,128)S(1)} %collective-permute-done.1.refs_4_.refs_5_) | copy-start | bytes 196612
  79.1 2.6 %copy-start.4 = (f32[16,8,128]{2,1,0:T(8,128)}, f32[16,8,128]{2,1,0:T(8,128)S(1)}, u32[]{:S(2)}) copy-start(f32[16,8,128]{2,1,0:T(8,128)S(1)} %collective-permute-done.3.refs_6_.refs_7_) | copy-start | bytes 196612
  79.1 2.5 %copy-start = (f32[32,8,128]{2,1,0:T(8,128)}, f32[32,8,128]{2,1,0:T(8,128)S(1)}, u32[]{:S(2)}) copy-start(f32[32,8,128]{2,1,0:T(8,128)S(1)} %collective-permute-done.refs_3_.refs_4_) | copy-start | bytes 393220
  81.0 0.7 copy-start.1
  95.1 22.7 %all-to-all-start.3 = ((bf16[32,8,8,128]{3,2,1,0:T(8,128)(2,1)}), bf16[32,8,8,128]{3,2,1,0:T(8,128)(2,1)S(1)}, u32[]{:S(2)}, u32[]{:S(2)}) async-start(bf16[32,8,8,128]{3,2,1,0:T(8,128)(2,1)} %bitcast.47), calls=%async_computation.3 | async-start | bytes 1048576 | tf_op jit(solution)/shard_map/all_to_all | solution.py:19
  102.2 8.4 %collective-permute-start.4 = (bf16[32,8,128]{2,1,0:T(8,128)(2,1)}, bf16[32,8,128]{2,1,0:T(8,128)(2,1)S(1)}, u32[]{:S(2)}, u32[]{:S(2)}) collective-permute-start(bf16[32,8,128]{2,1,0:T(8,128)(2,1)} %get-tuple-element.50), channel_id=1, source_target_pairs={{4,0},{8,4},{12,8},{16,12},{20,16},{24,20},{28,24},{5,1},{9,5},{13... | collective-permute-start | bytes 196616 | tf_op jit(solution)/shard_map/ppermute | solution.py:26
  103.5 7.1 %collective-permute-start.5 = (bf16[16,8,128]{2,1,0:T(8,128)(2,1)}, bf16[16,8,128]{2,1,0:T(8,128)(2,1)S(1)}, u32[]{:S(2)}, u32[]{:S(2)}) collective-permute-start(bf16[16,8,128]{2,1,0:T(8,128)(2,1)} %get-tuple-element.53), channel_id=1, source_target_pairs={{1,0},{2,1},{3,2},{5,4},{6,5},{7,6},{9,8},{10,9},{11,10},{13,12},{... | collective-permute-start | bytes 98312 | tf_op jit(solution)/shard_map/ppermute | solution.py:26
  110.6 7.2 %copy-start.5 = (bf16[16,8,128]{2,1,0:T(8,128)(2,1)}, bf16[16,8,128]{2,1,0:T(8,128)(2,1)S(1)}, u32[]{:S(2)}) copy-start(bf16[16,8,128]{2,1,0:T(8,128)(2,1)S(1)} %collective-permute-done.5.refs_8_.refs_9_) | copy-start | bytes 98308
  110.6 7.2 %copy-start.2 = (bf16[32,8,128]{2,1,0:T(8,128)(2,1)}, bf16[32,8,128]{2,1,0:T(8,128)(2,1)S(1)}, u32[]{:S(2)}) copy-start(bf16[32,8,128]{2,1,0:T(8,128)(2,1)S(1)} %collective-permute-done.4.refs_5_.refs_8_) | copy-start | bytes 196612
  134.6 13.4 %all-to-all-start.5 = ((f32[32,8,128]{2,1,0:T(8,128)}), f32[32,8,128]{2,1,0:T(8,128)S(1)}, u32[]{:S(2)}, u32[]{:S(2)}) async-start(f32[32,8,128]{2,1,0:T(8,128)} %get-tuple-element.55), calls=%async_computation.5 | async-start | bytes 262144 | tf_op jit(solution)/shard_map/all_to_all | solution.py:19
  138.7 15.1 %copy-start.6 = (bf16[32,8,128]{2,1,0:T(8,128)(2,1)S(1)}, bf16[32,8,128]{2,1,0:T(8,128)(2,1)}, u32[]{:S(2)}) copy-start(bf16[32,8,128]{2,1,0:T(8,128)(2,1)} %get-tuple-element.49.refs_4_) | copy-start | bytes 196612
  138.7 18.8 %copy-start.9 = (bf16[16,8,128]{2,1,0:T(8,128)(2,1)S(1)}, bf16[16,8,128]{2,1,0:T(8,128)(2,1)}, u32[]{:S(2)}) copy-start(bf16[16,8,128]{2,1,0:T(8,128)(2,1)} %get-tuple-element.52.refs_7_) | copy-start | bytes 98308
  148.0 22.2 %all-to-all-start.4 = ((bf16[32,8,8,128]{3,2,1,0:T(8,128)(2,1)}), bf16[32,8,8,128]{3,2,1,0:T(8,128)(2,1)S(1)}, u32[]{:S(2)}, u32[]{:S(2)}) async-start(bf16[32,8,8,128]{3,2,1,0:T(8,128)(2,1)} %bitcast.42), calls=%async_computation.4 | async-start | bytes 1048576 | tf_op jit(solution)/shard_map/all_to_all | solution.py:19
  153.8 6.7 %collective-permute-start.6 = (bf16[32,8,128]{2,1,0:T(8,128)(2,1)S(1)}, bf16[32,8,128]{2,1,0:T(8,128)(2,1)S(1)}, u32[]{:S(2)}, u32[]{:S(2)}) collective-permute-start(bf16[32,8,128]{2,1,0:T(8,128)(2,1)S(1)} %copy-done.6), channel_id=1, source_target_pairs={{0,4},{4,8},{8,12},{12,16},{16,20},{20,24},{24,28},{1,5},{5,9},{9,... | collective-permute-start | bytes 196616 | tf_op jit(solution)/shard_map/ppermute | solution.py:28
  157.5 2.6 %collective-permute-start.7 = (bf16[16,8,128]{2,1,0:T(8,128)(2,1)S(1)}, bf16[16,8,128]{2,1,0:T(8,128)(2,1)S(1)}, u32[]{:S(2)}, u32[]{:S(2)}) collective-permute-start(bf16[16,8,128]{2,1,0:T(8,128)(2,1)S(1)} %copy-done.9), channel_id=1, source_target_pairs={{0,1},{1,2},{2,3},{4,5},{5,6},{6,7},{8,9},{9,10},{10,11},{12,13},{... | collective-permute-start | bytes 98312 | tf_op jit(solution)/shard_map/ppermute | solution.py:28
  160.1 0.6 copy-start.11
  160.7 0.6 copy-start.8
  176.3 27.8 %all-to-all-start.6 = ((bf16[32,8,8,128]{3,2,1,0:T(8,128)(2,1)}), bf16[32,8,8,128]{3,2,1,0:T(8,128)(2,1)S(1)}, u32[]{:S(2)}, u32[]{:S(2)}) async-start(bf16[32,8,8,128]{3,2,1,0:T(8,128)(2,1)} %bitcast.46), calls=%async_computation.6 | async-start | bytes 1048576 | tf_op jit(solution)/shard_map/all_to_all | solution.py:19
  188.5 8.4 %collective-permute-start.8 = (bf16[32,8,128]{2,1,0:T(8,128)(2,1)}, bf16[32,8,128]{2,1,0:T(8,128)(2,1)S(1)}, u32[]{:S(2)}, u32[]{:S(2)}) collective-permute-start(bf16[32,8,128]{2,1,0:T(8,128)(2,1)} %get-tuple-element.65), channel_id=1, source_target_pairs={{4,0},{8,4},{12,8},{16,12},{20,16},{24,20},{28,24},{5,1},{9,5},{13... | collective-permute-start | bytes 196616 | tf_op jit(solution)/shard_map/ppermute | solution.py:26
  189.8 7.1 %collective-permute-start.9 = (bf16[16,8,128]{2,1,0:T(8,128)(2,1)}, bf16[16,8,128]{2,1,0:T(8,128)(2,1)S(1)}, u32[]{:S(2)}, u32[]{:S(2)}) collective-permute-start(bf16[16,8,128]{2,1,0:T(8,128)(2,1)} %get-tuple-element.68), channel_id=1, source_target_pairs={{1,0},{2,1},{3,2},{5,4},{6,5},{7,6},{9,8},{10,9},{11,10},{13,12},{... | collective-permute-start | bytes 98312 | tf_op jit(solution)/shard_map/ppermute | solution.py:26
  196.9 7.2 %copy-start.10 = (bf16[16,8,128]{2,1,0:T(8,128)(2,1)}, bf16[16,8,128]{2,1,0:T(8,128)(2,1)S(1)}, u32[]{:S(2)}) copy-start(bf16[16,8,128]{2,1,0:T(8,128)(2,1)S(1)} %collective-permute-done.9.refs_8_) | copy-start | bytes 98308
  196.9 7.2 %copy-start.7 = (bf16[32,8,128]{2,1,0:T(8,128)(2,1)}, bf16[32,8,128]{2,1,0:T(8,128)(2,1)S(1)}, u32[]{:S(2)}) copy-start(bf16[32,8,128]{2,1,0:T(8,128)(2,1)S(1)} %collective-permute-done.8.refs_5_) | copy-start | bytes 196612
  220.9 12.3 %all-to-all-start.7 = ((f32[32,8,128]{2,1,0:T(8,128)}), f32[32,8,128]{2,1,0:T(8,128)S(1)}, u32[]{:S(2)}, u32[]{:S(2)}) async-start(f32[32,8,128]{2,1,0:T(8,128)} %get-tuple-element.69), calls=%async_computation.7 | async-start | bytes 262144 | tf_op jit(solution)/shard_map/all_to_all | solution.py:19

commit v4 on v3

--- a/solution.py
+++ b/solution.py
@@ -11,7 +11,7 @@
 AXES = ("region", "survey")
 EPS_SQ = 0.09
 KERNEL_VMEM = 32 * 1024 * 1024
-PART = 256
+PARTS = {"residual": 1, "forward": 4, "backward": 2}
 GROUP = 8
 
 
@@ -128,31 +128,36 @@
 
 
 def prepare_kernel(start_ref, active_ref, model_ref, low_ref, top, bottom, left, right):
-    layer = pl.program_id(0)
-    rows = start_ref.shape[1]
-    for start in range(0, rows, GROUP):
-        live = active_ref[0, pl.ds(start, GROUP), :]
-        for k in range(GROUP):
-            value = start_ref[0, start + k] * live[k : k + 1]
-            model_ref[0, start + k] = value
-            low_ref[0, start + k] = value.astype(jnp.bfloat16)
-    left[0] = model_ref[0, 0]
-    right[0] = model_ref[0, rows - 1]
-
-    @pl.when(layer == 0)
+    block, rows = start_ref.shape[:2]
+
+    def one(layer, carry):
+        for start in range(0, rows, GROUP):
+            live = active_ref[layer, pl.ds(start, GROUP), :].astype(jnp.float32)
+            for k in range(GROUP):
+                value = start_ref[layer, start + k] * live[k : k + 1]
+                model_ref[layer, start + k] = value
+                low_ref[layer, start + k] = value.astype(jnp.bfloat16)
+        left[layer] = model_ref[layer, 0]
+        right[layer] = model_ref[layer, rows - 1]
+        return carry
+
+    lax.fori_loop(0, block, one, 0)
+
+    @pl.when(pl.program_id(0) == 0)
     def _():
         top[...] = model_ref[0]
 
-    @pl.when(layer == pl.num_programs(0) - 1)
+    @pl.when(pl.program_id(0) == pl.num_programs(0) - 1)
     def _():
-        bottom[...] = model_ref[0]
+        bottom[...] = model_ref[block - 1]
 
 
 def prepare_call(start_model, active):
     layers, rows, samples, cells = start_model.shape
-    block = pl.BlockSpec((1, rows, samples, cells), lambda i: (i, 0, 0, 0))
+    step = 4 if layers % 4 == 0 else 1
+    block = pl.BlockSpec((step, rows, samples, cells), lambda i: (i, 0, 0, 0))
     layer = pl.BlockSpec((rows, samples, cells), lambda i: (0, 0, 0))
-    column = pl.BlockSpec((1, samples, cells), lambda i: (i, 0, 0))
+    column = pl.BlockSpec((step, samples, cells), lambda i: (i, 0, 0))
     outs = [
         (start_model.shape, jnp.float32),
         (start_model.shape, jnp.bfloat16),
@@ -162,10 +167,12 @@
     return pl.pallas_call(
         prepare_kernel,
         name="prepare",
-        grid=(layers,),
-        in_specs=[block, pl.BlockSpec((1, rows, cells), lambda i: (i, 0, 0))],
+        grid=(layers // step,),
+        in_specs=[block, pl.BlockSpec((step, rows, cells), lambda i: (i, 0, 0))],
         out_specs=[block, block, layer, layer, column, column],
-        out_shape=[pltpu.HBM(*o) for o in outs],
+        out_shape=[
+            jax.ShapeDtypeStruct(*o) if o[1] == jnp.bfloat16 else pltpu.HBM(*o) for o in outs
+        ],
         compiler_params=pltpu.CompilerParams(vmem_limit_bytes=KERNEL_VMEM),
     )(far(start_model), far(active))
 
@@ -236,7 +243,7 @@
             link_z = link_of(codes, 1, level_below)
             link_y = link_of(codes, 3, level)
             link_x = link_of(codes, 5, level) * inner
-            live = active_ref[place, :] * level
+            live = active_ref[place, :].astype(jnp.float32) * level
             if start == 0:
                 came = prior(left, None if first else gleft, layer)
                 link = link_of(codes, 2, level)
@@ -327,7 +334,7 @@
             link_z = link_of(codes, 1, level_below)
             link_y = link_of(codes, 3, level)
             link_x = link_of(codes, 5, level) * inner
-            live = active[place, :] * level
+            live = active[place, :].astype(jnp.float32) * level
             for k in range(GROUP):
                 row = start + k
                 one_row = slice(k, k + 1)
@@ -363,26 +370,29 @@
     return curv
 
 
-def load_sensors(sensor_ref, held_ref, sems, parts):
-    height = held_ref.shape[1]
-    copies = []
-    for chunk in range(held_ref.shape[0]):
-        rows = pl.ds(chunk % parts * height, height)
-        copies.append(
+def sensor_copies(sensor_ref, held_ref, sems):
+    tiles, _, length = held_ref.shape
+    parts = sems.shape[1]
+    columns = length // parts
+    return [
+        [
             pltpu.make_async_copy(
-                sensor_ref.at[chunk // parts, rows], held_ref.at[chunk], sems.at[chunk]
+                sensor_ref.at[tile, :, pl.ds(part * columns, columns)],
+                held_ref.at[tile, :, pl.ds(part * columns, columns)],
+                sems.at[tile, part],
             )
-        )
-        copies[-1].start()
-
-
-def wait_part(sensor_ref, held_ref, sems, tile, part, parts):
-    height = held_ref.shape[1]
-    chunk = tile * parts + part
-    rows = pl.ds(part * height, height)
-    pltpu.make_async_copy(
-        sensor_ref.at[tile, rows], held_ref.at[chunk], sems.at[chunk]
-    ).wait()
+            for part in range(parts)
+        ]
+        for tile in range(tiles)
+    ]
+
+
+def start_copies(copies, small):
+    flat = [copy for tile in copies for copy in tile]
+    flat[0].start()
+    wait_all(small)
+    for copy in flat[1:]:
+        copy.start()
 
 
 def gather_rows(width, slot_ref, arrived_ref, rows_ref):
@@ -397,101 +407,74 @@
     lax.fori_loop(0, rows_ref.shape[0], one, 0)
 
 
-def scatter_rows(tile, width, slot_ref, blocks, buffer_ref):
+def scatter_rows(tile, width, slot_ref, blocks, first, buffer_ref):
     cells = buffer_ref.shape[2]
-    for entry in range(width):
-        slot = slot_ref[tile * width + entry]
+    for entry in range(blocks.shape[1] // cells):
+        slot = slot_ref[tile * width + first + entry]
         block = blocks[:, entry * cells : (entry + 1) * cells]
         buffer_ref[slot] = block.astype(buffer_ref.dtype)
 
 
-def project(rows, sensor):
-    return lax.dot_general(
-        rows, sensor, (((1,), (1,)), ((), ())), preferred_element_type=jnp.float32
-    )
-
-
-def forward_tile(tile, weight_of, rows_ref, held_ref, sensor_ref, sems, pred_ref, parts):
-    height = held_ref.shape[1]
-    given = []
+def project(tile, copies, rows_ref, held_ref):
+    parts = len(copies[tile])
+    columns = held_ref.shape[2] // parts
+    pred = 0.0
     for part in range(parts):
-        span = slice(part * height, (part + 1) * height)
-        wait_part(sensor_ref, held_ref, sems, tile, part, parts)
-        pred = project(rows_ref[tile], held_ref[tile * parts + part])
-        pred_ref[tile, :, span] = pred
-        given.append(weight_of(span, pred))
-    return given
-
-
-def backward_tile(tile, sent, held_ref, parts):
-    blocks = 0.0
-    for part in range(parts):
-        blocks += jnp.dot(
-            sent[part], held_ref[tile * parts + part], preferred_element_type=jnp.float32
+        span = slice(part * columns, (part + 1) * columns)
+        copies[tile][part].wait()
+        pred += lax.dot_general(
+            rows_ref[tile, :, span],
+            held_ref[tile, :, span],
+            (((1,), (1,)), ((), ())),
+            preferred_element_type=jnp.float32,
         )
-    return blocks
+    return pred
 
 
 def residual_kernel(slot_ref, arrived_ref, sensor_ref, *refs):
     small_refs, refs = (refs[:2], refs[2:])
     pred_ref, buffer_ref, rows_ref, held_ref, sems, *small, small_sems = refs
     tiles = pred_ref.shape[0]
-    parts = held_ref.shape[0] // tiles
     width = slot_ref.shape[0] // tiles
-    copies = start_all(small_refs, small, small_sems)
-    load_sensors(sensor_ref, held_ref, sems, parts)
+    copies = sensor_copies(sensor_ref, held_ref, sems)
+    start_copies(copies, start_all(small_refs, small, small_sems))
+    weight, observed = small
     buffer_ref[...] = jnp.zeros_like(buffer_ref)
     gather_rows(width, slot_ref, arrived_ref, rows_ref)
-    wait_all(copies)
-    weight, observed = small
-
-    def one(tile, carry):
-        def weight_of(span, pred):
-            residual = pred - observed[tile, :, span]
-            return (weight[tile, :, span] * residual).astype(jnp.bfloat16)
-
-        sent = forward_tile(
-            tile, weight_of, rows_ref, held_ref, sensor_ref, sems, pred_ref, parts
-        )
-        blocks = backward_tile(tile, sent, held_ref, parts)
-        scatter_rows(tile, width, slot_ref, blocks, buffer_ref)
-        return carry
-
-    lax.fori_loop(0, tiles, one, 0)
+    blocks = None
+    for tile in range(tiles):
+        pred = project(tile, copies, rows_ref, held_ref)
+        if tile > 0:
+            scatter_rows(tile - 1, width, slot_ref, blocks, 0, buffer_ref)
+        pred_ref[tile] = pred
+        weighted = (weight[tile] * (pred - observed[tile])).astype(jnp.bfloat16)
+        blocks = jnp.dot(weighted, held_ref[tile], preferred_element_type=jnp.float32)
+    scatter_rows(tiles - 1, width, slot_ref, blocks, 0, buffer_ref)
 
 
 def forward_kernel(slot_ref, arrived_ref, sensor_ref, *refs):
     small_refs, refs = (refs[:9], refs[9:])
     pred_ref, sent_ref, rows_ref, held_ref, sems, *small, small_sems = refs
-    tiles, samples = pred_ref.shape[:2]
-    parts = held_ref.shape[0] // tiles
+    tiles = pred_ref.shape[0]
     width = slot_ref.shape[0] // tiles
-    copies = start_all(small_refs, small, small_sems)
-    load_sensors(sensor_ref, held_ref, sems, parts)
+    copies = sensor_copies(sensor_ref, held_ref, sems)
+    start_copies(copies, [])
+    small_copies = start_all(small_refs, small, small_sems)
     gather_rows(width, slot_ref, arrived_ref, rows_ref)
-    wait_all(copies)
+    for tile in range(tiles):
+        pred_ref[tile] = project(tile, copies, rows_ref, held_ref)
+    wait_all(small_copies)
     weight, norm, faces, *rims = small
     total = faces[...]
     for edge, mine, theirs in (rims[:3], rims[3:]):
         for row in range(edge.shape[0]):
             change = mine[row].astype(jnp.float32) - theirs[row].astype(jnp.float32)
             total = total + edge[row] * change * change
-
-    def one(tile, curv):
-        def weight_of(span, pred):
-            return jnp.sum(weight[tile, :, span] * pred * pred, axis=1, keepdims=True)
-
-        given = forward_tile(
-            tile, weight_of, rows_ref, held_ref, sensor_ref, sems, pred_ref, parts
-        )
-        return curv + sum(given)
-
-    data = lax.fori_loop(0, tiles, one, jnp.zeros((samples, 1), jnp.float32))
-    sums = [jnp.sum(norm[...], axis=1, keepdims=True), data, jnp.sum(total, axis=1, keepdims=True)]
+    data = sum(weight[tile] * pred_ref[tile] * pred_ref[tile] for tile in range(tiles))
     lane = lax.broadcasted_iota(jnp.int32, total.shape, 1)
     block = jnp.zeros(total.shape, jnp.float32)
-    for i, value in enumerate(sums):
-        block = jnp.where(lane == i, value, block)
+    for i, value in enumerate((norm[...], data, total)):
+        block = jnp.where(lane == i, jnp.sum(value, axis=1, keepdims=True), block)
     sent_ref[...] = jnp.broadcast_to(block[None], sent_ref.shape)
 
 
@@ -500,35 +483,39 @@
     buffer_ref, held_ref, sems, *small, small_sems = refs
     weight, pred = small
     tiles, samples = pred.shape[:2]
-    height = held_ref.shape[1]
-    parts = held_ref.shape[0] // tiles
     width = slot_ref.shape[0] // tiles
-    copies = start_all(small_refs, small, small_sems)
-    load_sensors(sensor_ref, held_ref, sems, parts)
+    parts = sems.shape[1]
+    columns = held_ref.shape[2] // parts
+    copies = sensor_copies(sensor_ref, held_ref, sems)
+    start_copies(copies, start_all(small_refs, small, small_sems))
     buffer_ref[...] = jnp.zeros_like(buffer_ref)
-    wait_all(copies)
-
-    def one(tile, carry):
+    for tile in range(tiles):
         weighted = weight[tile] * pred[tile]
         upper = weighted.astype(jnp.bfloat16).astype(jnp.float32)
         both = jnp.concatenate([upper, weighted - upper], axis=0).astype(jnp.bfloat16)
-        sent = [both[:, part * height : (part + 1) * height] for part in range(parts)]
         for part in range(parts):
-            wait_part(sensor_ref, held_ref, sems, tile, part, parts)
-        blocks = backward_tile(tile, sent, held_ref, parts)
-        scatter_rows(tile, width, slot_ref, blocks[:samples] + blocks[samples:], buffer_ref)
-        return carry
-
-    lax.fori_loop(0, tiles, one, 0)
-
-
-def tile_call(kernel, slot_of, near, sensor, small, outs, samples):
-    tiles, data_slots, length = sensor.shape
-    height = PART if data_slots % PART == 0 else data_slots
-    chunks = tiles * data_slots // height
+            copies[tile][part].wait()
+            blocks = jnp.dot(
+                both,
+                held_ref[tile, :, part * columns : (part + 1) * columns],
+                preferred_element_type=jnp.float32,
+            )
+            scatter_rows(
+                tile,
+                width,
+                slot_ref,
+                blocks[:samples] + blocks[samples:],
+                part * width // parts,
+                buffer_ref,
+            )
+
+
+def tile_call(kernel, name, slot_of, near, sensor, small, outs, samples):
+    tiles, _, length = sensor.shape
+    parts = PARTS[name] if slot_of.shape[0] // tiles % PARTS[name] == 0 else 1
     scratch = [
-        pltpu.VMEM((chunks, height, length), jnp.bfloat16),
-        pltpu.SemaphoreType.DMA((chunks,)),
+        pltpu.VMEM(sensor.shape, jnp.bfloat16),
+        pltpu.SemaphoreType.DMA((tiles, parts)),
     ]
     if near:
         scratch = [pltpu.VMEM((tiles, samples, length), jnp.bfloat16)] + scratch
@@ -567,7 +554,7 @@
         step = step_rows[...]
 
     def combine(i, norm):
-        live = active[pl.ds(pl.multiple_of(i * GROUP, GROUP), GROUP), :]
+        live = active[pl.ds(pl.multiple_of(i * GROUP, GROUP), GROUP), :].astype(jnp.float32)
         for k in range(GROUP):
             j = i * GROUP + k
             data = total[j]
@@ -690,8 +677,7 @@
     asking = jnp.sum(jnp.where(slot_hits, local_of[:, None], 0), axis=0).reshape(owners, capacity)
     asked_ids = swap(asking).reshape(-1)
 
-    active_rows = active_cells.astype(jnp.float32)
-    active_flat = active_rows.reshape(per_owner, cells_x)
+    active_flat = active_cells.reshape(per_owner, cells_x)
     links = face_links.reshape(per_owner, cells_x)
     base = (lax.axis_index("region") * layers).astype(jnp.int32).reshape(1)
     row_mask = (
@@ -715,15 +701,18 @@
     def forward(arrived, norm, faces, edge_z, edge_y, rims, theirs):
         small = [weight_sq, norm, faces, edge_z, rims[1], theirs[0], edge_y, rims[3], theirs[1]]
         outs = [pred_shape, shape_of(f32, owners, samples, cells_x)]
-        return tile_call(forward_kernel, slot_of, [arrived], sensitivity, small, outs, samples)
+        return tile_call(
+            forward_kernel, "forward", slot_of, [arrived], sensitivity, small, outs, samples
+        )
 
     grid = (depth_count, base, links, active_flat)
-    model, bricks, *rims = prepare_call(start_model, active_rows)
+    model, bricks, *rims = prepare_call(start_model, active_cells)
     replies = flat(bricks)[asked_ids]
     arrived = exchange(replies)
     model_rims = edges(rims)
     pred, buffer = tile_call(
         residual_kernel,
+        "residual",
         slot_of,
         [arrived],
         sensitivity,
@@ -744,7 +733,14 @@
     step_pred, sums = forward(arrived, norm, faces, edge_z, edge_y, rims, grad_rims)
     got = swap(sums)
     (buffer,) = tile_call(
-        backward_kernel, slot_of, [], sensitivity, [weight_sq, step_pred], [buffer_shape], samples
+        backward_kernel,
+        "backward",
+        slot_of,
+        [],
+        sensitivity,
+        [weight_sq, step_pred],
+        [buffer_shape],
+        samples,
     )
     arrived = exchange(buffer)
 

time: 240 us -> 204 us (0.85)
  Pallas kernels: 116 us -> 84.3 us
  starting transfers between devices: 70.3 us -> 67.2 us
  waiting for transfers between devices: 40 us -> 43 us
    pallas_call x10, Pallas kernels: 101 us -> 75.3 us  [kernel_call(): pl.pallas_call(kernel, out_shape=out_shapes, grid_spec=pltpu.PrefetchScal...]
    pallas_call x1, Pallas kernels: 9.84 us -> 4.04 us  [prepare_call(): pl.pallas_call(prepare_kernel, name='prepare', grid=(layers // step,), in...]
    all_to_all x8, starting transfers between devices: 49.5 us -> 46.4 us  [swap(): return lax.all_to_all(field, AXES, split_axis=0, concat_axis=0, tiled=True)]
    all_to_all x8, waiting for transfers between devices: 36.9 us -> 39.8 us  [swap(): return lax.all_to_all(field, AXES, split_axis=0, concat_axis=0, tiled=True)]
  transfers between devices with their start and end apart: 18 -> 18, of which waited for: 7 -> 8; matrix products, arithmetic and copies ran while one was open for 2% -> 2% of each run, Pallas kernels for 20% -> 20%
where the time goes in v4:
time: 204 us; the launch traced here: 203 us
  Pallas kernels  84.3 us (41%)
  starting transfers between devices  67.2 us (33%)
  waiting for transfers between devices  43 us (21%)
  local copies, waits for them, and re-layouts  6.43 us (3%)
    pallas_call x10, Pallas kernels, kernel_call(): pl.pallas_call(kernel, out_shape=out_shapes, grid_spec=pltpu.PrefetchScal...  75.3 us
    all_to_all x8, starting transfers between devices, swap(): return lax.all_to_all(field, AXES, split_axis=0, concat_axis=0, tiled=True)  46.4 us
    all_to_all x8, waiting for transfers between devices, swap(): return lax.all_to_all(field, AXES, split_axis=0, concat_axis=0, tiled=True)  39.8 us
    ppermute x4, starting transfers between devices, edges(): lax.ppermute(last, axis, [(i, i + 1) for i in range(count - 1)])  13 us
    ppermute x6, starting transfers between devices, edges(): lax.ppermute(first, axis, [(i + 1, i) for i in range(count - 1)])  7.75 us
    pallas_call x1, Pallas kernels, finish_call(): pl.pallas_call(finish_kernel, name='finish', grid=(layers // block,), in_...  4.97 us
  transfers between devices with their start and end apart: 18, of which 8 were waited for; matrix products, arithmetic and copies ran while one was open for 2% of the time, Pallas kernels for 20%

profile of v4, /device:TPU:0, one launch (start us, length us, event | category | flops | bytes accessed | tf_op | source)
XLA Modules:
  0.0 203.4 jit_solution(5417722372856168288)
XLA Ops:
  0.6 0.8 reshape.170
  1.5 0.2 reduce_window_sum.11
  2.0 0.7 all_to_all.27
  2.7 7.3 %all-to-all-start = ((s32[32,1,8]{2,1,0:T(1,128)}), s32[32,1,8]{2,1,0:T(1,128)S(1)}, u32[]{:S(2)}, u32[]{:S(2)}) async-start(s32[32,1,8]{2,1,0:T(1,128)} %bitcast), calls=%async_computation | async-start | bytes 32768 | tf_op jit(solution)/shard_map/all_to_all | solution.py:19
  10.0 4.0 %prepare.1 = (f32[16,32,8,128]{3,2,1,0:T(8,128)}, bf16[16,32,8,128]{3,2,1,0:T(8,128)(2,1)S(1)}, f32[32,8,128]{2,1,0:T(8,128)}, f32[32,8,128]{2,1,0:T(8,128)}, f3...) custom-call(f32[16,32,8,128]{3,2,1,0:T(8,128)} %start_ref.1, s32[16,32,128]{2,1,0:T(8,128)} %active_ref.1), custom_call_target="tpu_custom_call" | custom-call | tf_op jit(solution)/shard_map/prepare/pallas_call | solution.py:167
  14.1 3.1 %all-to-all-done = s32[32,1,8]{2,1,0:T(1,128)S(1)} async-done(((s32[32,1,8]{2,1,0:T(1,128)}), s32[32,1,8]{2,1,0:T(1,128)S(1)}, u32[]{:S(2)}, u32[]{:S(2)}) %all-to-all-start) | async-done | bytes 1056 | tf_op jit(solution)/shard_map/all_to_all | solution.py:19
  17.3 1.6 gather_fusion
  18.9 2.7 %all-to-all-start.1 = ((bf16[32,8,8,128]{3,2,1,0:T(8,128)(2,1)}), bf16[32,8,8,128]{3,2,1,0:T(8,128)(2,1)S(1)}, u32[]{:S(2)}, u32[]{:S(2)}) async-start(bf16[32,8,8,128]{3,2,1,0:T(8,128)(2,1)} %bitcast.4), calls=%async_computation.1 | async-start | bytes 1048576 | tf_op jit(solution)/shard_map/all_to_all | solution.py:19
  21.7 0.6 copy.27.refs_0_
  22.3 14.9 %all-to-all-done.1 = bf16[32,8,8,128]{3,2,1,0:T(8,128)(2,1)S(1)} async-done(((bf16[32,8,8,128]{3,2,1,0:T(8,128)(2,1)}), bf16[32,8,8,128]{3,2,1,0:T(8,128)(2,1)S(1)}, u32[]{:S(2)}, u32[]{:S(2)}) %all-to-all-start.1) | async-done | bytes 524320 | tf_op jit(solution)/shard_map/all_to_all | solution.py:19
  37.2 10.9 %shard_map.104 = (f32[4,8,512]{2,1,0:T(8,128)}, bf16[256,8,128]{2,1,0:T(8,128)(2,1)}) custom-call(s32[128]{0:T(128)S(1)} %multiply_add_fusion.slot_ref, bf16[256,8,128]{2,1,0:T(8,128)(2,1)S(1)} %bitcast.26, bf16[4,512,4096]{2,1,0:T(8,128)(2,1)} %sensor_ref.7, f32[4,1,512]{2,1,0:T(1,128)} %copy.27.refs_0_, f32[4,8,512]{2,1,0:T(8,128)} %observed_ref.1), custom_call_target="tpu_custom_call" | custom-call | tf_op jit(solution)/shard_map/pallas_call | solution.py:43
  48.2 3.0 %all-to-all-start.2 = ((bf16[32,8,8,128]{3,2,1,0:T(8,128)(2,1)}), bf16[32,8,8,128]{3,2,1,0:T(8,128)(2,1)S(1)}, u32[]{:S(2)}, u32[]{:S(2)}) async-start(bf16[32,8,8,128]{3,2,1,0:T(8,128)(2,1)} %bitcast.46), calls=%async_computation.2 | async-start | bytes 1048576 | tf_op jit(solution)/shard_map/all_to_all | solution.py:19
  51.2 1.3 collective-permute-start
  52.5 4.6 %collective-permute-start.2 = (f32[32,8,128]{2,1,0:T(8,128)S(1)}, f32[32,8,128]{2,1,0:T(8,128)S(1)}, u32[]{:S(2)}, u32[]{:S(2)}) collective-permute-start(f32[32,8,128]{2,1,0:T(8,128)S(1)} %copy-done.15), channel_id=1, source_target_pairs={{0,4},{4,8},{8,12},{12,16},{16,20},{20,24},{24,28},{1,5},{5,9},{9,... | collective-permute-start | bytes 393224 | tf_op jit(solution)/shard_map/ppermute | solution.py:28
  57.0 1.3 collective-permute-start.1
  58.4 3.0 %collective-permute-start.3 = (f32[16,8,128]{2,1,0:T(8,128)S(1)}, f32[16,8,128]{2,1,0:T(8,128)S(1)}, u32[]{:S(2)}, u32[]{:S(2)}) collective-permute-start(f32[16,8,128]{2,1,0:T(8,128)S(1)} %copy-done.17), channel_id=1, source_target_pairs={{0,1},{1,2},{2,3},{4,5},{5,6},{6,7},{8,9},{9,10},{10,11},{12,13},{... | collective-permute-start | bytes 196616 | tf_op jit(solution)/shard_map/ppermute | solution.py:28
  61.4 0.5 broadcast.134
  61.9 0.7 reduce.5
  62.8 1.9 collective-permute-done.2.refs_5_.refs_6_
  64.6 0.7 broadcast_in_dim.16.refs_2_.refs_3_.scale_ref
  65.3 7.4 %shard_map.105 = (f32[32,8,128]{2,1,0:T(8,128)}, f32[16,8,128]{2,1,0:T(8,128)}, f32[16,32,8,128]{3,2,1,0:T(8,128)}) custom-call(s32[1]{0:T(128)} %bitcast.9.base_ref, s32[512,128]{1,0:T(8,128)} %bitcast.39, s32[512,128]{1,0:T(8,128)} %bitcast.29, f32[8,128]{1,0:T(8,128)} %broadcast_in_dim.16.refs_2_.refs_3_.scale_ref, f32[32,8,128]{2,1,0:T(8,128)} %copy-done, ...), custom_call_target="tpu_custom_call" | custom-call | tf_op jit(solution)/shard_map/pallas_call | solution.py:43
  72.7 6.1 %shard_map.106 = (bf16[256,8,128]{2,1,0:T(8,128)(2,1)}, f32[8,128]{1,0:T(8,128)}, bf16[32,8,128]{2,1,0:T(8,128)(2,1)}, bf16[32,8,128]{2,1,0:T(8,128)(2,1)}, bf16...) custom-call(s32[256]{0:T(256)S(1)} %reshape.171.ids_ref, ...), custom_call_target="tpu_custom_call" | custom-call | tf_op jit(solution)/shard_map/pallas_call | solution.py:43
  78.8 7.1 %all-to-all-start.3 = ((bf16[32,8,8,128]{3,2,1,0:T(8,128)(2,1)}), bf16[32,8,8,128]{3,2,1,0:T(8,128)(2,1)S(1)}, u32[]{:S(2)}, u32[]{:S(2)}) async-start(bf16[32,8,8,128]{3,2,1,0:T(8,128)(2,1)} %bitcast.48), calls=%async_computation.3 | async-start | bytes 1048576 | tf_op jit(solution)/shard_map/all_to_all | solution.py:19
  85.9 1.3 collective-permute-start.4
  87.2 1.3 collective-permute-start.5
  88.5 5.9 %shard_map.107.refs_2_ = f32[8,128]{1,0:T(8,128)} custom-call(s32[1]{0:T(128)} %bitcast.9.base_ref, s32[512,128]{1,0:T(8,128)} %bitcast.40, s32[512,128]{1,0:T(8,128)} %bitcast.31, f32[16,32,8,128]{3,2,1,0:T(8,128)} %get-tuple-element.43.refs_7_.field_ref.refs_12_, f32[16,32,8,128]{3,2,1,0:T(8,128)} %bitcast.35), custom_call_target="tpu_custom_call" | custom-call | tf_op jit(solution)/shard_map/pallas_call | solution.py:43
  94.4 7.1 %all-to-all-done.3 = bf16[32,8,8,128]{3,2,1,0:T(8,128)(2,1)S(1)} async-done(((bf16[32,8,8,128]{3,2,1,0:T(8,128)(2,1)}), bf16[32,8,8,128]{3,2,1,0:T(8,128)(2,1)S(1)}, u32[]{:S(2)}, u32[]{:S(2)}) %all-to-all-start.3) | async-done | bytes 524320 | tf_op jit(solution)/shard_map/all_to_all | solution.py:19
  101.5 8.2 %shard_map.108 = (f32[4,8,512]{2,1,0:T(8,128)}, f32[32,8,128]{2,1,0:T(8,128)}) custom-call(s32[128]{0:T(128)S(1)} %multiply_add_fusion.slot_ref, bf16[256,8,128]{2,1,0:T(8,128)(2,1)S(1)} %bitcast.25, bf16[4,512,4096]{2,1,0:T(8,128)(2,1)} %sensor_ref.7, f32[4,1,512]{2,1,0:T(1,128)} %copy.27.refs_0_, f32[8,128]{1,0:T(8,128)} %get-tuple-element.46.refs_1_, ...), custom_call_target="tpu_custom_call" | custom-call | tf_op jit(solution)/shard_map/pallas_call | solution.py:43
  109.6 4.3 %all-to-all-start.5 = ((f32[32,8,128]{2,1,0:T(8,128)}), f32[32,8,128]{2,1,0:T(8,128)S(1)}, u32[]{:S(2)}, u32[]{:S(2)}) async-start(f32[32,8,128]{2,1,0:T(8,128)} %get-tuple-element.55), calls=%async_computation.5 | async-start | bytes 262144 | tf_op jit(solution)/shard_map/all_to_all | solution.py:19
  114.0 8.1 %shard_map.109 = bf16[256,8,128]{2,1,0:T(8,128)(2,1)} custom-call(s32[128]{0:T(128)S(1)} %multiply_add_fusion.slot_ref, bf16[4,512,4096]{2,1,0:T(8,128)(2,1)} %sensor_ref.7, f32[4,1,512]{2,1,0:T(1,128)} %copy.27.refs_0_, f32[4,8,512]{2,1,0:T(8,128)} %get-tuple-element.54.refs_1_.moved_ref), custom_call_target="tpu_custom_call" | custom-call | tf_op jit(solution)/shard_map/pallas_call | solution.py:43
  122.0 5.7 %all-to-all-start.4 = ((bf16[32,8,8,128]{3,2,1,0:T(8,128)(2,1)}), bf16[32,8,8,128]{3,2,1,0:T(8,128)(2,1)S(1)}, u32[]{:S(2)}, u32[]{:S(2)}) async-start(bf16[32,8,8,128]{3,2,1,0:T(8,128)(2,1)} %bitcast.43), calls=%async_computation.4 | async-start | bytes 1048576 | tf_op jit(solution)/shard_map/all_to_all | solution.py:19
  127.7 3.7 %collective-permute-start.6 = (bf16[32,8,128]{2,1,0:T(8,128)(2,1)S(1)}, bf16[32,8,128]{2,1,0:T(8,128)(2,1)S(1)}, u32[]{:S(2)}, u32[]{:S(2)}) collective-permute-start(bf16[32,8,128]{2,1,0:T(8,128)(2,1)S(1)} %copy-done.6), channel_id=1, source_target_pairs={{0,4},{4,8},{8,12},{12,16},{16,20},{20,24},{24,28},{1,5},{5,9},{9,... | collective-permute-start | bytes 196616 | tf_op jit(solution)/shard_map/ppermute | solution.py:28
  131.4 1.7 collective-permute-start.7
  133.2 0.8 collective-permute-done.7.refs_11_
  134.0 0.4 collective-permute-done.6.refs_10_
  134.6 0.6 copy-done.8
  135.2 8.7 %shard_map.110 = (f32[32,8,128]{2,1,0:T(8,128)}, f32[16,8,128]{2,1,0:T(8,128)}, f32[8,128]{1,0:T(8,128)}, f32[16,32,8,128]{3,2,1,0:T(8,128)}, f32[16,32,8,128]{3,2,1,0:T(8,128)}) custom-call(s32[1]{0:T(128)} %bitcast.9.base_ref, f32[32,8,128]{2,1,0:T(8,128)S(1)} %all-to-all-done.5.refs_0_, s32[512,128]{1,0:T(8,128)} %bitcast.41, s32[512,128]{1,0:T(8,128)} %bitcast.32, ...), custom_call_target="tpu_custom_call" | custom-call | tf_op jit(solution)/shard_map/pallas_call | solution.py:43
  143.9 6.1 %shard_map.111 = (bf16[256,8,128]{2,1,0:T(8,128)(2,1)}, f32[8,128]{1,0:T(8,128)}, bf16[32,8,128]{2,1,0:T(8,128)(2,1)}, bf16[32,8,128]{2,1,0:T(8,128)(2,1)}, bf16...) custom-call(s32[256]{0:T(256)S(1)} %reshape.171.ids_ref, ...), custom_call_target="tpu_custom_call" | custom-call | tf_op jit(solution)/shard_map/pallas_call | solution.py:43
  150.0 12.2 %all-to-all-start.6 = ((bf16[32,8,8,128]{3,2,1,0:T(8,128)(2,1)}), bf16[32,8,8,128]{3,2,1,0:T(8,128)(2,1)S(1)}, u32[]{:S(2)}, u32[]{:S(2)}) async-start(bf16[32,8,8,128]{3,2,1,0:T(8,128)(2,1)} %bitcast.47), calls=%async_computation.6 | async-start | bytes 1048576 | tf_op jit(solution)/shard_map/all_to_all | solution.py:19
  162.3 1.3 collective-permute-start.8
  163.6 1.3 collective-permute-start.9
  164.9 5.9 %shard_map.112.refs_2_ = f32[8,128]{1,0:T(8,128)} custom-call(s32[1]{0:T(128)} %bitcast.9.base_ref, s32[512,128]{1,0:T(8,128)} %bitcast.42, s32[512,128]{1,0:T(8,128)} %bitcast.34, f32[16,32,8,128]{3,2,1,0:T(8,128)} %get-tuple-element.61.field_ref, f32[16,32,8,128]{3,2,1,0:T(8,128)} %bitcast.37), custom_call_target="tpu_custom_call" | custom-call | tf_op jit(solution)/shard_map/pallas_call | solution.py:43
  170.8 7.1 %all-to-all-done.6 = bf16[32,8,8,128]{3,2,1,0:T(8,128)(2,1)S(1)} async-done(((bf16[32,8,8,128]{3,2,1,0:T(8,128)(2,1)}), bf16[32,8,8,128]{3,2,1,0:T(8,128)(2,1)S(1)}, u32[]{:S(2)}, u32[]{:S(2)}) %all-to-all-start.6) | async-done | bytes 524320 | tf_op jit(solution)/shard_map/all_to_all | solution.py:19
  177.9 8.2 %shard_map.113 = (f32[4,8,512]{2,1,0:T(8,128)}, f32[32,8,128]{2,1,0:T(8,128)}) custom-call(s32[128]{0:T(128)S(1)} %multiply_add_fusion.slot_ref, bf16[256,8,128]{2,1,0:T(8,128)(2,1)S(1)} %bitcast.24, bf16[4,512,4096]{2,1,0:T(8,128)(2,1)} %sensor_ref.7, f32[4,1,512]{2,1,0:T(1,128)} %copy.27.refs_0_, f32[8,128]{1,0:T(8,128)} %get-tuple-element.60.refs_1_, ...), custom_call_target="tpu_custom_call" | custom-call | tf_op jit(solution)/shard_map/pallas_call | solution.py:43
  186.1 4.1 %all-to-all-start.7 = ((f32[32,8,128]{2,1,0:T(8,128)}), f32[32,8,128]{2,1,0:T(8,128)S(1)}, u32[]{:S(2)}, u32[]{:S(2)}) async-start(f32[32,8,128]{2,1,0:T(8,128)} %get-tuple-element.69), calls=%async_computation.7 | async-start | bytes 262144 | tf_op jit(solution)/shard_map/all_to_all | solution.py:19
  190.2 0.6 mul.37.mask_ref
  190.8 7.6 %all-to-all-done.7.got_ref = f32[32,8,128]{2,1,0:T(8,128)S(1)} async-done(((f32[32,8,128]{2,1,0:T(8,128)}), f32[32,8,128]{2,1,0:T(8,128)S(1)}, u32[]{:S(2)}, u32[]{:S(2)}) %all-to-all-start.7) | async-done | bytes 131104 | tf_op jit(solution)/shard_map/all_to_all | solution.py:19
  198.4 5.0 %finish.1 = (f32[16,32,8,128]{3,2,1,0:T(8,128)}, f32[4,8,512]{2,1,0:T(8,128)}) custom-call(f32[32,8,128]{2,1,0:T(8,128)S(1)} %all-to-all-done.7.got_ref, f32[8,128]{1,0:T(8,128)} %broadcast_in_dim.16.refs_2_.refs_3_.scale_ref, f32[8,128]{1,0:T(8,128)} %get-tuple-element.58.refs_3_.before_ref, f32[4,1,512]{2,1,0:T(1,128)} %mul.37.mask_ref, ...), custom_call_target="tpu_custom_call" | custom-call | tf_op jit(solution)/shard_map/finish/pallas_call | solution.py:637
  (57 shorter events, 0.9 us)
Async XLA Ops:
  2.7 14.5 %all-to-all-start = ((s32[32,1,8]{2,1,0:T(1,128)}), s32[32,1,8]{2,1,0:T(1,128)S(1)}, u32[]{:S(2)}, u32[]{:S(2)}) async-start(s32[32,1,8]{2,1,0:T(1,128)} %bitcast), calls=%async_computation | async-start | bytes 32768 | tf_op jit(solution)/shard_map/all_to_all | solution.py:19
  10.0 11.6 %copy-start.12 = (f32[4,512]{1,0:T(4,128)S(1)}, f32[4,512]{1,0:T(4,128)}, u32[]{:S(2)}) copy-start(f32[4,512]{1,0:T(4,128)} %param.11) | copy-start | bytes 24580
  10.0 11.6 %copy-start.13 = (s32[4]{0:T(128)S(1)}, s32[4]{0:T(128)}, u32[]{:S(2)}) copy-start(s32[4]{0:T(128)} %param.12) | copy-start | bytes 52
  18.9 18.4 %all-to-all-start.1 = ((bf16[32,8,8,128]{3,2,1,0:T(8,128)(2,1)}), bf16[32,8,8,128]{3,2,1,0:T(8,128)(2,1)S(1)}, u32[]{:S(2)}, u32[]{:S(2)}) async-start(bf16[32,8,8,128]{3,2,1,0:T(8,128)(2,1)} %bitcast.4), calls=%async_computation.1 | async-start | bytes 1048576 | tf_op jit(solution)/shard_map/all_to_all | solution.py:19
  37.2 13.9 %copy-start.16 = (f32[32,8,128]{2,1,0:T(8,128)S(1)}, f32[32,8,128]{2,1,0:T(8,128)}, u32[]{:S(2)}) copy-start(f32[32,8,128]{2,1,0:T(8,128)} %get-tuple-element.39) | copy-start | bytes 393220
  37.2 15.2 %copy-start.15 = (f32[32,8,128]{2,1,0:T(8,128)S(1)}, f32[32,8,128]{2,1,0:T(8,128)}, u32[]{:S(2)}) copy-start(f32[32,8,128]{2,1,0:T(8,128)} %get-tuple-element.41) | copy-start | bytes 393220
  37.2 19.8 %copy-start.18 = (f32[16,8,128]{2,1,0:T(8,128)S(1)}, f32[16,8,128]{2,1,0:T(8,128)}, u32[]{:S(2)}) copy-start(f32[16,8,128]{2,1,0:T(8,128)} %get-tuple-element.40) | copy-start | bytes 196612
  37.2 21.1 %copy-start.17 = (f32[16,8,128]{2,1,0:T(8,128)S(1)}, f32[16,8,128]{2,1,0:T(8,128)}, u32[]{:S(2)}) copy-start(f32[16,8,128]{2,1,0:T(8,128)} %get-tuple-element.42) | copy-start | bytes 196612
  37.2 27.4 %copy-start.14 = (f32[8]{0:T(128)S(1)}, f32[8]{0:T(128)}, u32[]{:S(2)}) copy-start(f32[8]{0:T(128)} %param.17) | copy-start | bytes 100
  48.2 24.5 %all-to-all-start.2 = ((bf16[32,8,8,128]{3,2,1,0:T(8,128)(2,1)}), bf16[32,8,8,128]{3,2,1,0:T(8,128)(2,1)S(1)}, u32[]{:S(2)}, u32[]{:S(2)}) async-start(bf16[32,8,8,128]{3,2,1,0:T(8,128)(2,1)} %bitcast.46), calls=%async_computation.2 | async-start | bytes 1048576 | tf_op jit(solution)/shard_map/all_to_all | solution.py:19
  51.2 11.6 %collective-permute-start = (f32[32,8,128]{2,1,0:T(8,128)S(1)}, f32[32,8,128]{2,1,0:T(8,128)S(1)}, u32[]{:S(2)}, u32[]{:S(2)}) collective-permute-start(f32[32,8,128]{2,1,0:T(8,128)S(1)} %copy-done.16), channel_id=1, source_target_pairs={{4,0},{8,4},{12,8},{16,12},{20,16},{24,20},{28,24},{5,1},{9,5},{13... | collective-permute-start | bytes 393224 | tf_op jit(solution)/shard_map/ppermute | solution.py:26
  52.5 12.1 %collective-permute-start.2 = (f32[32,8,128]{2,1,0:T(8,128)S(1)}, f32[32,8,128]{2,1,0:T(8,128)S(1)}, u32[]{:S(2)}, u32[]{:S(2)}) collective-permute-start(f32[32,8,128]{2,1,0:T(8,128)S(1)} %copy-done.15), channel_id=1, source_target_pairs={{0,4},{4,8},{8,12},{12,16},{16,20},{20,24},{24,28},{1,5},{5,9},{9,... | collective-permute-start | bytes 393224 | tf_op jit(solution)/shard_map/ppermute | solution.py:28
  57.0 5.7 %collective-permute-start.1 = (f32[16,8,128]{2,1,0:T(8,128)S(1)}, f32[16,8,128]{2,1,0:T(8,128)S(1)}, u32[]{:S(2)}, u32[]{:S(2)}) collective-permute-start(f32[16,8,128]{2,1,0:T(8,128)S(1)} %copy-done.18), channel_id=1, source_target_pairs={{1,0},{2,1},{3,2},{5,4},{6,5},{7,6},{9,8},{10,9},{11,10},{13,12},{... | collective-permute-start | bytes 196616 | tf_op jit(solution)/shard_map/ppermute | solution.py:26
  58.4 4.4 %collective-permute-start.3 = (f32[16,8,128]{2,1,0:T(8,128)S(1)}, f32[16,8,128]{2,1,0:T(8,128)S(1)}, u32[]{:S(2)}, u32[]{:S(2)}) collective-permute-start(f32[16,8,128]{2,1,0:T(8,128)S(1)} %copy-done.17), channel_id=1, source_target_pairs={{0,1},{1,2},{2,3},{4,5},{5,6},{6,7},{8,9},{9,10},{10,11},{12,13},{... | collective-permute-start | bytes 196616 | tf_op jit(solution)/shard_map/ppermute | solution.py:28
  62.7 2.6 %copy-start.3 = (f32[16,8,128]{2,1,0:T(8,128)}, f32[16,8,128]{2,1,0:T(8,128)S(1)}, u32[]{:S(2)}) copy-start(f32[16,8,128]{2,1,0:T(8,128)S(1)} %collective-permute-done.1.refs_4_.refs_5_) | copy-start | bytes 196612
  62.7 2.6 %copy-start.4 = (f32[16,8,128]{2,1,0:T(8,128)}, f32[16,8,128]{2,1,0:T(8,128)S(1)}, u32[]{:S(2)}) copy-start(f32[16,8,128]{2,1,0:T(8,128)S(1)} %collective-permute-done.3.refs_6_.refs_7_) | copy-start | bytes 196612
  62.7 2.5 %copy-start = (f32[32,8,128]{2,1,0:T(8,128)}, f32[32,8,128]{2,1,0:T(8,128)S(1)}, u32[]{:S(2)}) copy-start(f32[32,8,128]{2,1,0:T(8,128)S(1)} %collective-permute-done.refs_3_.refs_4_) | copy-start | bytes 393220
  64.6 0.7 copy-start.1
  78.8 22.7 %all-to-all-start.3 = ((bf16[32,8,8,128]{3,2,1,0:T(8,128)(2,1)}), bf16[32,8,8,128]{3,2,1,0:T(8,128)(2,1)S(1)}, u32[]{:S(2)}, u32[]{:S(2)}) async-start(bf16[32,8,8,128]{3,2,1,0:T(8,128)(2,1)} %bitcast.48), calls=%async_computation.3 | async-start | bytes 1048576 | tf_op jit(solution)/shard_map/all_to_all | solution.py:19
  85.9 8.5 %collective-permute-start.4 = (bf16[32,8,128]{2,1,0:T(8,128)(2,1)}, bf16[32,8,128]{2,1,0:T(8,128)(2,1)S(1)}, u32[]{:S(2)}, u32[]{:S(2)}) collective-permute-start(bf16[32,8,128]{2,1,0:T(8,128)(2,1)} %get-tuple-element.50), channel_id=1, source_target_pairs={{4,0},{8,4},{12,8},{16,12},{20,16},{24,20},{28,24},{5,1},{9,5},{13... | collective-permute-start | bytes 196616 | tf_op jit(solution)/shard_map/ppermute | solution.py:26
  87.2 7.2 %collective-permute-start.5 = (bf16[16,8,128]{2,1,0:T(8,128)(2,1)}, bf16[16,8,128]{2,1,0:T(8,128)(2,1)S(1)}, u32[]{:S(2)}, u32[]{:S(2)}) collective-permute-start(bf16[16,8,128]{2,1,0:T(8,128)(2,1)} %get-tuple-element.53), channel_id=1, source_target_pairs={{1,0},{2,1},{3,2},{5,4},{6,5},{7,6},{9,8},{10,9},{11,10},{13,12},{... | collective-permute-start | bytes 98312 | tf_op jit(solution)/shard_map/ppermute | solution.py:26
  94.3 7.1 %copy-start.5 = (bf16[16,8,128]{2,1,0:T(8,128)(2,1)}, bf16[16,8,128]{2,1,0:T(8,128)(2,1)S(1)}, u32[]{:S(2)}) copy-start(bf16[16,8,128]{2,1,0:T(8,128)(2,1)S(1)} %collective-permute-done.5.refs_8_.refs_9_) | copy-start | bytes 98308
  94.4 7.1 %copy-start.2 = (bf16[32,8,128]{2,1,0:T(8,128)(2,1)}, bf16[32,8,128]{2,1,0:T(8,128)(2,1)S(1)}, u32[]{:S(2)}) copy-start(bf16[32,8,128]{2,1,0:T(8,128)(2,1)S(1)} %collective-permute-done.4.refs_5_.refs_8_) | copy-start | bytes 196612
  109.6 12.4 %all-to-all-start.5 = ((f32[32,8,128]{2,1,0:T(8,128)}), f32[32,8,128]{2,1,0:T(8,128)S(1)}, u32[]{:S(2)}, u32[]{:S(2)}) async-start(f32[32,8,128]{2,1,0:T(8,128)} %get-tuple-element.55), calls=%async_computation.5 | async-start | bytes 262144 | tf_op jit(solution)/shard_map/all_to_all | solution.py:19
  113.9 13.8 %copy-start.6 = (bf16[32,8,128]{2,1,0:T(8,128)(2,1)S(1)}, bf16[32,8,128]{2,1,0:T(8,128)(2,1)}, u32[]{:S(2)}) copy-start(bf16[32,8,128]{2,1,0:T(8,128)(2,1)} %get-tuple-element.49.refs_4_) | copy-start | bytes 196612
  113.9 17.5 %copy-start.9 = (bf16[16,8,128]{2,1,0:T(8,128)(2,1)S(1)}, bf16[16,8,128]{2,1,0:T(8,128)(2,1)}, u32[]{:S(2)}) copy-start(bf16[16,8,128]{2,1,0:T(8,128)(2,1)} %get-tuple-element.52.refs_7_) | copy-start | bytes 98308
  122.0 21.9 %all-to-all-start.4 = ((bf16[32,8,8,128]{3,2,1,0:T(8,128)(2,1)}), bf16[32,8,8,128]{3,2,1,0:T(8,128)(2,1)S(1)}, u32[]{:S(2)}, u32[]{:S(2)}) async-start(bf16[32,8,8,128]{3,2,1,0:T(8,128)(2,1)} %bitcast.43), calls=%async_computation.4 | async-start | bytes 1048576 | tf_op jit(solution)/shard_map/all_to_all | solution.py:19
  127.7 6.7 %collective-permute-start.6 = (bf16[32,8,128]{2,1,0:T(8,128)(2,1)S(1)}, bf16[32,8,128]{2,1,0:T(8,128)(2,1)S(1)}, u32[]{:S(2)}, u32[]{:S(2)}) collective-permute-start(bf16[32,8,128]{2,1,0:T(8,128)(2,1)S(1)} %copy-done.6), channel_id=1, source_target_pairs={{0,4},{4,8},{8,12},{12,16},{16,20},{20,24},{24,28},{1,5},{5,9},{9,... | collective-permute-start | bytes 196616 | tf_op jit(solution)/shard_map/ppermute | solution.py:28
  131.4 2.6 %collective-permute-start.7 = (bf16[16,8,128]{2,1,0:T(8,128)(2,1)S(1)}, bf16[16,8,128]{2,1,0:T(8,128)(2,1)S(1)}, u32[]{:S(2)}, u32[]{:S(2)}) collective-permute-start(bf16[16,8,128]{2,1,0:T(8,128)(2,1)S(1)} %copy-done.9), channel_id=1, source_target_pairs={{0,1},{1,2},{2,3},{4,5},{5,6},{6,7},{8,9},{9,10},{10,11},{12,13},{... | collective-permute-start | bytes 98312 | tf_op jit(solution)/shard_map/ppermute | solution.py:28
  134.0 0.6 copy-start.11
  134.6 0.6 copy-start.8
  150.0 27.8 %all-to-all-start.6 = ((bf16[32,8,8,128]{3,2,1,0:T(8,128)(2,1)}), bf16[32,8,8,128]{3,2,1,0:T(8,128)(2,1)S(1)}, u32[]{:S(2)}, u32[]{:S(2)}) async-start(bf16[32,8,8,128]{3,2,1,0:T(8,128)(2,1)} %bitcast.47), calls=%async_computation.6 | async-start | bytes 1048576 | tf_op jit(solution)/shard_map/all_to_all | solution.py:19
  162.3 8.5 %collective-permute-start.8 = (bf16[32,8,128]{2,1,0:T(8,128)(2,1)}, bf16[32,8,128]{2,1,0:T(8,128)(2,1)S(1)}, u32[]{:S(2)}, u32[]{:S(2)}) collective-permute-start(bf16[32,8,128]{2,1,0:T(8,128)(2,1)} %get-tuple-element.65), channel_id=1, source_target_pairs={{4,0},{8,4},{12,8},{16,12},{20,16},{24,20},{28,24},{5,1},{9,5},{13... | collective-permute-start | bytes 196616 | tf_op jit(solution)/shard_map/ppermute | solution.py:26
  163.6 7.2 %collective-permute-start.9 = (bf16[16,8,128]{2,1,0:T(8,128)(2,1)}, bf16[16,8,128]{2,1,0:T(8,128)(2,1)S(1)}, u32[]{:S(2)}, u32[]{:S(2)}) collective-permute-start(bf16[16,8,128]{2,1,0:T(8,128)(2,1)} %get-tuple-element.68), channel_id=1, source_target_pairs={{1,0},{2,1},{3,2},{5,4},{6,5},{7,6},{9,8},{10,9},{11,10},{13,12},{... | collective-permute-start | bytes 98312 | tf_op jit(solution)/shard_map/ppermute | solution.py:26
  170.7 7.1 %copy-start.10 = (bf16[16,8,128]{2,1,0:T(8,128)(2,1)}, bf16[16,8,128]{2,1,0:T(8,128)(2,1)S(1)}, u32[]{:S(2)}) copy-start(bf16[16,8,128]{2,1,0:T(8,128)(2,1)S(1)} %collective-permute-done.9.refs_8_) | copy-start | bytes 98308
  170.8 7.1 %copy-start.7 = (bf16[32,8,128]{2,1,0:T(8,128)(2,1)}, bf16[32,8,128]{2,1,0:T(8,128)(2,1)S(1)}, u32[]{:S(2)}) copy-start(bf16[32,8,128]{2,1,0:T(8,128)(2,1)S(1)} %collective-permute-done.8.refs_5_) | copy-start | bytes 196612
  186.1 12.3 %all-to-all-start.7 = ((f32[32,8,128]{2,1,0:T(8,128)}), f32[32,8,128]{2,1,0:T(8,128)S(1)}, u32[]{:S(2)}, u32[]{:S(2)}) async-start(f32[32,8,128]{2,1,0:T(8,128)} %get-tuple-element.69), calls=%async_computation.7 | async-start | bytes 262144 | tf_op jit(solution)/shard_map/all_to_all | solution.py:19

commit v5 on v4

--- a/solution.py
+++ b/solution.py
@@ -11,7 +11,7 @@
 AXES = ("region", "survey")
 EPS_SQ = 0.09
 KERNEL_VMEM = 32 * 1024 * 1024
-PARTS = {"residual": 1, "forward": 4, "backward": 2}
+PARTS = {"residual": 1, "forward": 4, "both": 1}
 GROUP = 8
 
 
@@ -69,9 +69,9 @@
     ]
 
 
-def start_all(sources, targets, sems):
+def start_all(sources, targets, sems, base=0):
     copies = [
-        pltpu.make_async_copy(source, target, sems.at[i])
+        pltpu.make_async_copy(source, target, sems.at[base + i])
         for i, (source, target) in enumerate(zip(sources, targets))
     ]
     for copy in copies:
@@ -177,62 +177,16 @@
     )(far(start_model), far(active))
 
 
-def reg_kernel(first, depth_count, base_ref, *refs):
-    if not first:
-        got_ref, *refs = refs
-    small_refs, refs = (refs[: 7 if first else 11], refs[7 if first else 11 :])
-    if first:
-        field_ref, edge_z, edge_y, reg_ref, *refs = refs
-        out, pad, flow, sems, *refs = refs
-    else:
-        field_ref, grad_ref, edge_z, edge_y, step_ref, reg_ref, new_ref, *refs = refs
-        out, pad, flow, sems, gpad, *refs = refs
-    small, small_sems = (refs[:-1], refs[-1])
-    copies = [start_pads(field_ref, pad, sems.at[0])]
-    if not first:
-        copies.append(start_pads(grad_ref, gpad, sems.at[1]))
-    wait_all(start_all(small_refs, small, small_sems))
-    links_ref, active_ref, scale_ref, below, right, above, left = small[:7]
-    layers, rows = field_ref.shape[:2]
-    base = base_ref[0]
-    scale = scale_ref[...]
-    fill_pads(pad, below, right)
-    if not first:
-        gbelow, gright, gabove, gleft = small[7:]
-        fill_pads(gpad, gbelow, gright)
-        step = step_from(got_ref, scale)
-        step_ref[...] = step
-    wait_all(copies)
-    if not first:
-
-        def move(layer, carry):
-            for row in range(rows + 1):
-                pad[layer, row] = pad[layer, row] - step * gpad[layer, row]
-            return carry
-
-        lax.fori_loop(0, layers, move, 0)
-        for row in range(rows):
-            pad[layers, row] = pad[layers, row] - step * gpad[layers, row]
-        store = pltpu.make_async_copy(
-            pad.at[pl.ds(0, layers), pl.ds(0, rows)], new_ref, sems.at[2]
-        )
-        store.start()
+def face_pass(depth_count, base, links_ref, active_ref, pad, flow, above, left, edges_out, put):
+    edge_z, edge_y = edges_out
+    layers, rows = (pad.shape[0] - 1, pad.shape[1] - 1)
     inner = inner_lanes(pad.shape[-1])
-
-    def prior(ref, gref, index):
-        value = ref[index]
-        if first:
-            return value
-        return value - step * gref[index].astype(jnp.float32)
-
     for start in range(0, rows, GROUP):
         codes = links_ref[pl.ds(start, GROUP), :]
         link = link_of(codes, 0, levels(base, 0, depth_count)[0])
         for k in range(GROUP):
-            row = start + k
-            came = prior(above, None if first else gabove, row)
-            difference, weight = face(came, pad[0, row], link[k : k + 1])
-            flow[row] = weight * difference
+            difference, weight = face(above(start + k), pad[0, start + k], link[k : k + 1])
+            flow[start + k] = weight * difference
 
     def one(layer, carry):
         _, level, level_below = levels(base, layer, depth_count)
@@ -243,17 +197,17 @@
             link_z = link_of(codes, 1, level_below)
             link_y = link_of(codes, 3, level)
             link_x = link_of(codes, 5, level) * inner
-            live = active_ref[place, :].astype(jnp.float32) * level
+            live = active_ref[place, :].astype(jnp.float32)
+            small = live * level
             if start == 0:
-                came = prior(left, None if first else gleft, layer)
                 link = link_of(codes, 2, level)
-                difference, weight = face(came, pad[layer, 0], link[:1])
+                difference, weight = face(left(layer), pad[layer, 0], link[:1])
                 flow_y = weight * difference
             for k in range(GROUP):
                 row = start + k
                 one_row = slice(k, k + 1)
                 here = pad[layer, row]
-                total = live[one_row] * lax.rsqrt(here * here + EPS_SQ) * here
+                total = small[one_row] * lax.rsqrt(here * here + EPS_SQ) * here
                 difference, weight = face(here, next_lane(here), link_x[one_row])
                 flow_x = weight * difference
                 total = total + flow_x - pltpu.roll(flow_x, 1, 1)
@@ -268,48 +222,181 @@
                 out_z = weight * difference
                 total = total + out_z - flow[row]
                 flow[row] = out_z
-                out[layer, row] = scale * total
+                carry = put(layer, row, live[one_row], total, carry)
         return carry
 
-    lax.fori_loop(0, layers, one, 0)
-    final = pltpu.make_async_copy(out, reg_ref, sems.at[3])
+    return lax.fori_loop(0, layers, one, jnp.zeros(pad.shape[2:], jnp.float32))
+
+
+def reg_kernel(depth_count, base_ref, *refs):
+    small_refs, refs = (refs[:7], refs[7:])
+    field_ref, edge_z, edge_y, reg_ref, out, pad, flow, sems, *small, small_sems = refs
+    copies = start_all(small_refs, small, small_sems)
+    field_copy = start_pads(field_ref, pad, sems.at[0])
+    wait_all(copies)
+    links_ref, active_ref, scale_ref, below, right, above, left = small
+    scale = scale_ref[...]
+    fill_pads(pad, below, right)
+    field_copy.wait()
+
+    def put(layer, row, live, value, carry):
+        out[layer, row] = scale * value
+        return carry
+
+    face_pass(
+        depth_count,
+        base_ref[0],
+        links_ref,
+        active_ref,
+        pad,
+        flow,
+        lambda row: above[row],
+        lambda layer: left[layer],
+        (edge_z, edge_y),
+        put,
+    )
+    final = pltpu.make_async_copy(out, reg_ref, sems.at[1])
     final.start()
     final.wait()
-    if not first:
-        store.wait()
-
-
-def reg_call(depth_count, base, links, active, scale, field, rims, moved=()):
+
+
+def reg_call(depth_count, base, links, active, scale, field, rims):
     layers, rows, samples, cells = field.shape
     f32 = jnp.float32
+    small = [links, active, scale, *rims]
+    return kernel_call(
+        functools.partial(reg_kernel, depth_count),
+        base,
+        [],
+        [*small, field],
+        [shape_of(f32, rows, samples, cells), shape_of(f32, layers, samples, cells)],
+        [shape_of(f32, *field.shape)],
+        [
+            pltpu.VMEM(field.shape, f32),
+            pltpu.VMEM((layers + 1, rows + 1, samples, cells), f32),
+            pltpu.VMEM((rows, samples, cells), f32),
+            pltpu.SemaphoreType.DMA((2,)),
+        ]
+        + held(small),
+    )
+
+
+def next_kernel(depth_count, capacity, ids_ref, arrived_ref, *refs):
+    small_refs, refs = (refs[:11], refs[11:])
+    field_ref, grad_ref, reg_ref, *refs = refs
+    reply_ref, norm_ref, top, bottom, first, last, edge_z, edge_y, step_ref, *refs = refs
+    new_ref, out_ref, total, out, reg, pad, gpad, flow, sems, *small, small_sems = refs
+    layers, rows = field_ref.shape[:2]
+    count = ids_ref.shape[0] - 1
+    copies = start_all(small_refs, small, small_sems)
+    big = [start_pads(field_ref, pad, sems.at[0]), start_pads(grad_ref, gpad, sems.at[1])]
+    big += start_all((reg_ref,), (reg,), sems, 2)
+    add_blocks(count, capacity, 1, ids_ref, arrived_ref, total)
+    owners = count // capacity
+    sums = lax.fori_loop(
+        0,
+        owners,
+        lambda i, v: v + arrived_ref[i * (capacity + 1) + capacity].astype(jnp.float32),
+        jnp.zeros(norm_ref.shape, jnp.float32),
+    )
+    norm, data, faces = (
+        sums[:, i : i + 1] + sums[:, i + 1 : i + 2] + sums[:, i + 2 : i + 3] for i in (0, 3, 6)
+    )
+    wait_all(copies)
+    links_ref, active_ref, scale_ref, below, right, above, left, *more = small
+    gbelow, gright, gabove, gleft = more
+    scale = scale_ref[...]
+    step = jnp.broadcast_to(norm / (data + scale[:, :1] * faces), scale.shape)
+    step_ref[...] = step
+    fill_pads(pad, below, right)
+    fill_pads(gpad, gbelow, gright)
+    wait_all(big)
+
+    def move(layer, carry):
+        for row in range(rows + 1):
+            pad[layer, row] = pad[layer, row] - step * gpad[layer, row]
+        return carry
+
+    lax.fori_loop(0, layers, move, 0)
+    for row in range(rows):
+        pad[layers, row] = pad[layers, row] - step * gpad[layers, row]
+    inside = pad.at[pl.ds(0, layers), pl.ds(0, rows)]
+    stores = start_all((inside,), (new_ref,), sems, 3)
+
+    def put(layer, row, live, value, norm):
+        data = step * (live * total[layer * rows + row])
+        value = scale * value + (gpad[layer, row] - reg[layer, row] - data)
+        out[layer, row] = value
+        return norm + value * value
+
+    norm_ref[...] = face_pass(
+        depth_count,
+        ids_ref[count],
+        links_ref,
+        active_ref,
+        pad,
+        flow,
+        lambda row: above[row] - step * gabove[row].astype(jnp.float32),
+        lambda layer: left[layer] - step * gleft[layer].astype(jnp.float32),
+        (edge_z, edge_y),
+        put,
+    )
+    stores += start_all((out,), (out_ref,), sems, 4)
+
+    def reply(i, carry):
+        for k in range(GROUP):
+            j = i * GROUP + k
+            row = ids_ref[j]
+            brick = out[lax.div(row, rows), lax.rem(row, rows)]
+            reply_ref[j] = brick.astype(reply_ref.dtype)
+        return carry
+
+    lax.fori_loop(0, count // GROUP, reply, 0)
+    top[...] = out[0].astype(top.dtype)
+    bottom[...] = out[layers - 1].astype(bottom.dtype)
+    for layer in range(layers):
+        first[layer] = out[layer, 0].astype(first.dtype)
+        last[layer] = out[layer, rows - 1].astype(last.dtype)
+    wait_all(stores)
+
+
+def next_call(
+    depth_count, base, links, active, scale, capacity, ids, arrived, field, rims, grad, grad_rims,
+    reg
+):
+    layers, rows, samples, cells = field.shape
+    f32, bf16 = (jnp.float32, jnp.bfloat16)
+    small = [links, active, scale, *rims, *grad_rims]
     pad = pltpu.VMEM((layers + 1, rows + 1, samples, cells), f32)
-    scratch = [
-        pltpu.VMEM(field.shape, f32),
-        pad,
-        pltpu.VMEM((rows, samples, cells), f32),
-        pltpu.SemaphoreType.DMA((4,)),
+    rim_z, rim_y = ((rows, samples, cells), (layers, samples, cells))
+    outs = [
+        shape_of(bf16, ids.shape[0], samples, cells),
+        shape_of(f32, samples, cells),
+        shape_of(bf16, *rim_z),
+        shape_of(bf16, *rim_z),
+        shape_of(bf16, *rim_y),
+        shape_of(bf16, *rim_y),
+        shape_of(f32, *rim_z),
+        shape_of(f32, *rim_y),
+        shape_of(f32, samples, cells),
     ]
-    near = []
-    small = [links, active, scale, *rims]
-    distant = [field]
-    outs = [shape_of(f32, rows, samples, cells), shape_of(f32, layers, samples, cells)]
-    distant_outs = [shape_of(f32, *field.shape)]
-    if moved:
-        got, grad, grad_rims = moved
-        near = [got]
-        small += grad_rims
-        distant.append(grad)
-        scratch.append(pad)
-        outs.append(shape_of(f32, samples, cells))
-        distant_outs *= 2
     return kernel_call(
-        functools.partial(reg_kernel, not moved, depth_count),
-        base,
-        near,
-        small + distant,
+        functools.partial(next_kernel, depth_count, capacity),
+        jnp.concatenate([ids, base]),
+        [arrived],
+        [*small, field, grad, reg],
         outs,
-        distant_outs,
-        scratch + held(small),
+        [shape_of(f32, *field.shape)] * 2,
+        [
+            pltpu.VMEM((layers * rows, samples, cells), f32),
+            pltpu.VMEM(field.shape, f32),
+            pltpu.VMEM(field.shape, f32),
+            pad,
+            pad,
+            pltpu.VMEM(rim_z, f32),
+            pltpu.SemaphoreType.DMA((5,)),
+        ]
+        + held(small),
     )
 
 
@@ -407,10 +494,16 @@
     lax.fori_loop(0, rows_ref.shape[0], one, 0)
 
 
-def scatter_rows(tile, width, slot_ref, blocks, first, buffer_ref):
+def spaced(slot, capacity, extra):
+    if not extra:
+        return slot
+    return slot + lax.div(slot, capacity) * extra
+
+
+def scatter_rows(tile, width, slot_ref, blocks, buffer_ref, capacity=1, extra=0):
     cells = buffer_ref.shape[2]
-    for entry in range(blocks.shape[1] // cells):
-        slot = slot_ref[tile * width + first + entry]
+    for entry in range(width):
+        slot = spaced(slot_ref[tile * width + entry], capacity, extra)
         block = blocks[:, entry * cells : (entry + 1) * cells]
         buffer_ref[slot] = block.astype(buffer_ref.dtype)
 
@@ -445,11 +538,38 @@
     for tile in range(tiles):
         pred = project(tile, copies, rows_ref, held_ref)
         if tile > 0:
-            scatter_rows(tile - 1, width, slot_ref, blocks, 0, buffer_ref)
+            scatter_rows(tile - 1, width, slot_ref, blocks, buffer_ref)
         pred_ref[tile] = pred
         weighted = (weight[tile] * (pred - observed[tile])).astype(jnp.bfloat16)
         blocks = jnp.dot(weighted, held_ref[tile], preferred_element_type=jnp.float32)
-    scatter_rows(tiles - 1, width, slot_ref, blocks, 0, buffer_ref)
+    scatter_rows(tiles - 1, width, slot_ref, blocks, buffer_ref)
+
+
+def local_sums(weight, pred_ref, norm, faces, rims):
+    total = faces[...]
+    for edge, mine, theirs in (rims[:3], rims[3:]):
+        for row in range(edge.shape[0]):
+            change = mine[row].astype(jnp.float32) - theirs[row].astype(jnp.float32)
+            total = total + edge[row] * change * change
+    tiles = pred_ref.shape[0]
+    data = sum(weight[tile] * pred_ref[tile] * pred_ref[tile] for tile in range(tiles))
+    return [jnp.sum(value, axis=1, keepdims=True) for value in (norm[...], data, total)]
+
+
+def columns_of(values, shape):
+    lane = lax.broadcasted_iota(jnp.int32, shape, 1)
+    block = jnp.zeros(shape, jnp.float32)
+    for i, value in enumerate(values):
+        block = jnp.where(lane == i, value, block)
+    return block
+
+
+def in_parts(value):
+    parts = []
+    for _ in range(3):
+        parts.append(value.astype(jnp.bfloat16).astype(jnp.float32))
+        value = value - parts[-1]
+    return parts
 
 
 def forward_kernel(slot_ref, arrived_ref, sensor_ref, *refs):
@@ -465,49 +585,48 @@
         pred_ref[tile] = project(tile, copies, rows_ref, held_ref)
     wait_all(small_copies)
     weight, norm, faces, *rims = small
-    total = faces[...]
-    for edge, mine, theirs in (rims[:3], rims[3:]):
-        for row in range(edge.shape[0]):
-            change = mine[row].astype(jnp.float32) - theirs[row].astype(jnp.float32)
-            total = total + edge[row] * change * change
-    data = sum(weight[tile] * pred_ref[tile] * pred_ref[tile] for tile in range(tiles))
-    lane = lax.broadcasted_iota(jnp.int32, total.shape, 1)
-    block = jnp.zeros(total.shape, jnp.float32)
-    for i, value in enumerate((norm[...], data, total)):
-        block = jnp.where(lane == i, jnp.sum(value, axis=1, keepdims=True), block)
-    sent_ref[...] = jnp.broadcast_to(block[None], sent_ref.shape)
-
-
-def backward_kernel(slot_ref, sensor_ref, *refs):
-    small_refs, refs = (refs[:2], refs[2:])
-    buffer_ref, held_ref, sems, *small, small_sems = refs
-    weight, pred = small
-    tiles, samples = pred.shape[:2]
+    sums = local_sums(weight, pred_ref, norm, faces, rims)
+    sent_ref[...] = jnp.broadcast_to(columns_of(sums, norm.shape)[None], sent_ref.shape)
+
+
+def both_kernel(capacity, slot_ref, arrived_ref, sensor_ref, *refs):
+    small_refs, refs = (refs[:9], refs[9:])
+    pred_ref, buffer_ref, rows_ref, held_ref, sems, *small, small_sems = refs
+    tiles, samples = pred_ref.shape[:2]
     width = slot_ref.shape[0] // tiles
-    parts = sems.shape[1]
-    columns = held_ref.shape[2] // parts
     copies = sensor_copies(sensor_ref, held_ref, sems)
-    start_copies(copies, start_all(small_refs, small, small_sems))
+    start_copies(copies, start_all(small_refs[:1], small[:1], small_sems))
+    later = start_all(small_refs[1:], small[1:], small_sems, 1)
+    weight, norm, faces, *rims = small
     buffer_ref[...] = jnp.zeros_like(buffer_ref)
+    gather_rows(width, slot_ref, arrived_ref, rows_ref)
+
+    def put(tile, blocks):
+        scatter_rows(
+            tile, width, slot_ref, blocks[:samples] + blocks[samples:], buffer_ref, capacity, 1
+        )
+
+    blocks = None
     for tile in range(tiles):
-        weighted = weight[tile] * pred[tile]
+        pred = project(tile, copies, rows_ref, held_ref)
+        if tile > 0:
+            put(tile - 1, blocks)
+        pred_ref[tile] = pred
+        weighted = weight[tile] * pred
         upper = weighted.astype(jnp.bfloat16).astype(jnp.float32)
-        both = jnp.concatenate([upper, weighted - upper], axis=0).astype(jnp.bfloat16)
-        for part in range(parts):
-            copies[tile][part].wait()
-            blocks = jnp.dot(
-                both,
-                held_ref[tile, :, part * columns : (part + 1) * columns],
-                preferred_element_type=jnp.float32,
-            )
-            scatter_rows(
-                tile,
-                width,
-                slot_ref,
-                blocks[:samples] + blocks[samples:],
-                part * width // parts,
-                buffer_ref,
-            )
+        pair = jnp.concatenate([upper, weighted - upper], axis=0).astype(jnp.bfloat16)
+        blocks = jnp.dot(pair, held_ref[tile], preferred_element_type=jnp.float32)
+    put(tiles - 1, blocks)
+    wait_all(later)
+    sums = local_sums(weight, pred_ref, norm, faces, rims)
+    split = [part for value in sums for part in in_parts(value)]
+    block = columns_of(split, norm.shape).astype(buffer_ref.dtype)
+
+    def send(owner, carry):
+        buffer_ref[owner * (capacity + 1) + capacity] = block
+        return carry
+
+    lax.fori_loop(0, buffer_ref.shape[0] // (capacity + 1), send, 0)
 
 
 def tile_call(kernel, name, slot_of, near, sensor, small, outs, samples):
@@ -522,55 +641,41 @@
     return kernel_call(kernel, slot_of, near, [sensor, *small], outs, [], scratch + held(small))
 
 
-def sum_kernel(first, layers, ids_ref, arrived_ref, *refs):
-    active_ref, reg_ref, *refs = refs
-    if not first:
-        base_ref, step_ref, *refs = refs
-    reply_ref, norm_ref, top, bottom, left, right, grad_ref, *refs = refs
-    if first:
-        data_ref, *refs = refs
-        total, grad, out_sems, active, reg, sems = refs
-        sources, targets = ((active_ref, reg_ref), (active, reg))
-    else:
-        total, grad, out_sems, active, reg, base, step_rows, sems = refs
-        sources = (active_ref, reg_ref, base_ref, step_ref)
-        targets = (active, reg, base, step_rows)
-    copies = start_all(sources, targets, sems)
-    count = ids_ref.shape[0]
-    bricks = grad.shape[0]
-    rows = bricks // layers
+def add_blocks(count, capacity, extra, ids_ref, arrived_ref, total):
     total[...] = jnp.zeros_like(total)
 
     def add(i, carry):
         for k in range(GROUP):
             j = i * GROUP + k
             row = ids_ref[j]
-            total[row] += arrived_ref[j].astype(jnp.float32)
+            total[row] += arrived_ref[spaced(j, capacity, extra)].astype(jnp.float32)
         return carry
 
     lax.fori_loop(0, count // GROUP, add, 0)
+
+
+def sum_kernel(layers, ids_ref, arrived_ref, *refs):
+    active_ref, reg_ref, reply_ref, norm_ref, top, bottom, left, right, *refs = refs
+    grad_ref, total, grad, out_sems, active, reg, sems = refs
+    copies = start_all((active_ref, reg_ref), (active, reg), sems)
+    count = ids_ref.shape[0]
+    bricks = grad.shape[0]
+    rows = bricks // layers
+    add_blocks(count, 1, 0, ids_ref, arrived_ref, total)
     wait_all(copies)
-    if not first:
-        step = step_rows[...]
 
     def combine(i, norm):
         live = active[pl.ds(pl.multiple_of(i * GROUP, GROUP), GROUP), :].astype(jnp.float32)
         for k in range(GROUP):
             j = i * GROUP + k
-            data = total[j]
-            if not first:
-                data = base[j] - step * data
-            value = live[k : k + 1] * data + reg[j]
+            value = live[k : k + 1] * total[j] + reg[j]
             grad[j] = value
             norm = norm + value * value
         return norm
 
     norm = lax.fori_loop(0, bricks // GROUP, combine, jnp.zeros(norm_ref.shape, jnp.float32))
     norm_ref[...] = norm
-    if first:
-        stores = start_all((grad, total), (grad_ref, data_ref), out_sems)
-    else:
-        stores = start_all((grad,), (grad_ref,), out_sems)
+    stores = start_all((grad,), (grad_ref,), out_sems)
 
     def reply(i, carry):
         for k in range(GROUP):
@@ -587,9 +692,9 @@
     wait_all(stores)
 
 
-def sum_call(first, layers, ids, arrived, active, reg, *more):
+def sum_call(layers, ids, arrived, active, reg):
     bricks, samples, cells = reg.shape
-    small = [active, reg, *more]
+    small = [active, reg]
     field = shape_of(jnp.float32, bricks, samples, cells)
     outs = [shape_of(jnp.bfloat16, *arrived.shape), shape_of(jnp.float32, samples, cells)]
     for length in (bricks // layers, bricks // layers, layers, layers):
@@ -597,52 +702,69 @@
     scratch = [
         pltpu.VMEM(field.shape, jnp.float32),
         pltpu.VMEM(field.shape, jnp.float32),
-        pltpu.SemaphoreType.DMA((2 if first else 1,)),
+        pltpu.SemaphoreType.DMA((1,)),
     ]
     return kernel_call(
-        functools.partial(sum_kernel, first, layers),
+        functools.partial(sum_kernel, layers),
         ids,
         [arrived],
         small,
         outs,
-        [field, field] if first else [field],
+        [field],
         scratch + held(small),
     )
 
 
-def finish_kernel(
-    got_ref, scale_ref, before_ref, mask_ref, observed_ref, pred_ref, moved_ref, last_ref,
-    field_ref, grad_ref, model_ref, misfit_ref
-):
-    step = step_from(got_ref, scale_ref[...])
-    model_ref[...] = field_ref[...] - step[None, None] * grad_ref[...]
-
-    @pl.when(pl.program_id(0) == 0)
-    def _():
-        for tile in range(pred_ref.shape[0]):
-            pred = pred_ref[tile] - before_ref[:, :1] * moved_ref[tile]
-            pred = pred - step[:, :1] * last_ref[tile]
-            misfit_ref[tile] = mask_ref[tile] * (pred - observed_ref[tile])
-
-
-def finish_call(got, scale, before, mask, observed, pred, moved, last, field, grad):
-    layers, rows, samples, cells = field.shape
-    block = 4 if layers % 4 == 0 else 1
-    spec = pl.BlockSpec((block, rows, samples, cells), lambda i: (i, 0, 0, 0))
-
-    def fixed(array):
-        return pl.BlockSpec(array.shape, lambda i: (0,) * array.ndim)
-
+def finish_kernel(_, got_ref, *refs):
+    small_refs, refs = (refs[:7], refs[7:])
+    field_ref, grad_ref, model_ref, misfit_ref, field, grad, misfit, sems, *refs = refs
+    small, small_sems = (refs[:-1], refs[-1])
+    copies = start_all(small_refs, small, small_sems)
+    layers = field.shape[0]
+    chunks = sems.shape[0] // 3
+    spans = [pl.ds(i * (layers // chunks), layers // chunks) for i in range(chunks)]
+    loads = [
+        start_all(
+            (field_ref.at[span], grad_ref.at[span]),
+            (field.at[span], grad.at[span]),
+            sems,
+            3 * i,
+        )
+        for i, span in enumerate(spans)
+    ]
+    wait_all(copies)
+    scale, before, mask, observed, pred_ref, moved, last = small
+    step = step_from(got_ref, scale[...])
+    for tile in range(misfit.shape[0]):
+        pred = pred_ref[tile] - before[:, :1] * moved[tile]
+        pred = pred - step[:, :1] * last[tile]
+        misfit[tile] = mask[tile] * (pred - observed[tile])
+    stores = start_all((misfit,), (misfit_ref,), sems, 3 * chunks)
+    for i, span in enumerate(spans):
+        wait_all(loads[i])
+        field[span] = field[span] - step[None, None] * grad[span]
+        stores += start_all((field.at[span],), (model_ref.at[span],), sems, 3 * i + 2)
+    wait_all(stores)
+
+
+def finish_call(table, got, scale, before, mask, observed, pred, moved, last, field, grad):
     small = [scale, before, mask, observed, pred, moved, last]
-    return pl.pallas_call(
+    chunks = 4 if field.shape[0] % 4 == 0 else 1
+    return kernel_call(
         finish_kernel,
-        name="finish",
-        grid=(layers // block,),
-        in_specs=[WHOLE] + [fixed(a) for a in small] + [spec, spec],
-        out_specs=[spec, fixed(observed)],
-        out_shape=[pltpu.HBM(a.shape, a.dtype) for a in (field, observed)],
-        compiler_params=pltpu.CompilerParams(vmem_limit_bytes=KERNEL_VMEM),
-    )(got, *[far(a) for a in (*small, field, grad)])
+        table,
+        [got],
+        [*small, field, grad],
+        [],
+        [shape_of(jnp.float32, *a.shape) for a in (field, observed)],
+        [
+            pltpu.VMEM(field.shape, jnp.float32),
+            pltpu.VMEM(field.shape, jnp.float32),
+            pltpu.VMEM(observed.shape, jnp.float32),
+            pltpu.SemaphoreType.DMA((3 * chunks + 1,)),
+        ]
+        + held(small),
+    )
 
 
 def shards(
@@ -688,77 +810,56 @@
     reg_rows = jnp.broadcast_to(reg_weight[:, None], (samples, cells_x))
     f32, bf16 = (jnp.float32, jnp.bfloat16)
     pred_shape = shape_of(f32, tiles, samples, data_slots)
-    buffer_shape = shape_of(bf16, slots, samples, cells_x)
 
     def exchange(blocks):
-        return swap(blocks.reshape(owners, capacity, samples, cells_x)).reshape(
-            slots, samples, cells_x
-        )
+        sent = blocks.reshape(owners, blocks.shape[0] // owners, samples, cells_x)
+        return swap(sent).reshape(blocks.shape)
 
     def flat(field):
         return field.reshape(per_owner, samples, cells_x)
 
-    def forward(arrived, norm, faces, edge_z, edge_y, rims, theirs):
-        small = [weight_sq, norm, faces, edge_z, rims[1], theirs[0], edge_y, rims[3], theirs[1]]
-        outs = [pred_shape, shape_of(f32, owners, samples, cells_x)]
+    def tile_stage(kernel, name, arrived, small, out):
         return tile_call(
-            forward_kernel, "forward", slot_of, [arrived], sensitivity, small, outs, samples
+            kernel, name, slot_of, [arrived], sensitivity, small, [pred_shape, out], samples
         )
+
+    def sums_inputs(norm, faces, edge_z, edge_y, mine, theirs):
+        return [weight_sq, norm, faces, edge_z, mine[0], theirs[0], edge_y, mine[1], theirs[1]]
 
     grid = (depth_count, base, links, active_flat)
     model, bricks, *rims = prepare_call(start_model, active_cells)
     replies = flat(bricks)[asked_ids]
     arrived = exchange(replies)
     model_rims = edges(rims)
-    pred, buffer = tile_call(
-        residual_kernel,
-        "residual",
-        slot_of,
-        [arrived],
-        sensitivity,
-        [weight_sq, observed],
-        [pred_shape, buffer_shape],
-        samples,
-    )
+    blocks_shape = shape_of(bf16, slots, samples, cells_x)
+    small = [weight_sq, observed]
+    pred, buffer = tile_stage(residual_kernel, "residual", arrived, small, blocks_shape)
 
     arrived = exchange(buffer)
     edge_z, edge_y, reg = reg_call(*grid, reg_rows, model, model_rims)
-    replies, norm, *rims, grad, data_sum = sum_call(
-        True, layers, asked_ids, arrived, active_flat, flat(reg)
-    )
+    replies, norm, *rims, grad = sum_call(layers, asked_ids, arrived, active_flat, flat(reg))
     arrived = exchange(replies)
     grad_rims = edges(rims)
     grad = grad.reshape(start_model.shape)
     faces = curvature_call(*grid, model, grad)
-    step_pred, sums = forward(arrived, norm, faces, edge_z, edge_y, rims, grad_rims)
-    got = swap(sums)
-    (buffer,) = tile_call(
-        backward_kernel,
-        "backward",
-        slot_of,
-        [],
-        sensitivity,
-        [weight_sq, step_pred],
-        [buffer_shape],
-        samples,
-    )
+    small = sums_inputs(norm, faces, edge_z, edge_y, rims[1::2], grad_rims)
+    blocks_shape = shape_of(bf16, slots + owners, samples, cells_x)
+    kernel = functools.partial(both_kernel, capacity)
+    step_pred, buffer = tile_stage(kernel, "both", arrived, small, blocks_shape)
     arrived = exchange(buffer)
 
-    edge_z, edge_y, step, reg, model = reg_call(
-        *grid, reg_rows, model, model_rims, (got, grad, grad_rims)
-    )
-    replies, norm, *rims, grad = sum_call(
-        False, layers, asked_ids, arrived, active_flat, flat(reg), data_sum, step
+    replies, norm, *rims, edge_z, edge_y, step, model, grad = next_call(
+        *grid, reg_rows, capacity, asked_ids, arrived, model, model_rims, grad, grad_rims, reg
     )
     arrived = exchange(replies)
     grad_rims = edges(rims, both=False)
-    grad = grad.reshape(start_model.shape)
     faces = curvature_call(*grid, model, grad)
-    last_pred, sums = forward(arrived, norm, faces, edge_z, edge_y, rims, grad_rims)
+    small = sums_inputs(norm, faces, edge_z, edge_y, rims[1::2], grad_rims)
+    sums_shape = shape_of(f32, owners, samples, cells_x)
+    last_pred, sums = tile_stage(forward_kernel, "forward", arrived, small, sums_shape)
     got = swap(sums)
-    return tuple(
-        finish_call(got, reg_rows, step, mask, observed, pred, step_pred, last_pred, model, grad)
-    )
+    fields = (mask, observed, pred, step_pred, last_pred, model, grad)
+    return tuple(finish_call(base, got, reg_rows, step, *fields))
 
 
 def solution(mesh):

time: 204 us -> 190 us (0.931)
  starting transfers between devices: 67.2 us -> 53.9 us
  Pallas kernels: 84.3 us -> 73.8 us
  waiting for transfers between devices: 43 us -> 52.6 us
    all_to_all x8 -> x7, starting transfers between devices: 46.4 us -> 32.7 us  [swap(): return lax.all_to_all(field, AXES, split_axis=0, concat_axis=0, tiled=True)]
    all_to_all x8 -> x7, waiting for transfers between devices: 39.8 us -> 48.5 us  [swap(): return lax.all_to_all(field, AXES, split_axis=0, concat_axis=0, tiled=True)]
    pallas_call x10 -> x9, Pallas kernels: 75.3 us -> 69.8 us  [kernel_call(): pl.pallas_call(kernel, out_shape=out_shapes, grid_spec=pltpu.PrefetchScal...]
    pallas_call x1 -> x0, Pallas kernels: 4.97 us -> none  [finish_call(): pl.pallas_call(finish_kernel, name='finish', grid=(layers // block,), in_...]
  transfers between devices with their start and end apart: 18 -> 17, of which waited for: 8 -> 8; matrix products, arithmetic and copies ran while one was open for 2% -> 2% of each run, Pallas kernels for 20% -> 12%
where the time goes in v5:
time: 190 us; the launch traced here: 189 us
  Pallas kernels  73.8 us (39%)
  starting transfers between devices  53.9 us (28%)
  waiting for transfers between devices  52.6 us (28%)
  local copies, waits for them, and re-layouts  5.68 us (3%)
    pallas_call x9, Pallas kernels, kernel_call(): pl.pallas_call(kernel, out_shape=out_shapes, grid_spec=pltpu.PrefetchScal...  69.8 us
    all_to_all x7, waiting for transfers between devices, swap(): return lax.all_to_all(field, AXES, split_axis=0, concat_axis=0, tiled=True)  48.5 us
    all_to_all x7, starting transfers between devices, swap(): return lax.all_to_all(field, AXES, split_axis=0, concat_axis=0, tiled=True)  32.7 us
    ppermute x4, starting transfers between devices, edges(): lax.ppermute(last, axis, [(i, i + 1) for i in range(count - 1)])  13.3 us
    ppermute x6, starting transfers between devices, edges(): lax.ppermute(first, axis, [(i + 1, i) for i in range(count - 1)])  7.93 us
    ppermute x4, waiting for transfers between devices, edges(): lax.ppermute(last, axis, [(i, i + 1) for i in range(count - 1)])  4.07 us
    pallas_call x1, Pallas kernels, prepare_call(): pl.pallas_call(prepare_kernel, name='prepare', grid=(layers // step,), in...  4.04 us
  transfers between devices with their start and end apart: 17, of which 8 were waited for; matrix products, arithmetic and copies ran while one was open for 2% of the time, Pallas kernels for 12%

profile of v5, /device:TPU:0, one launch (start us, length us, event | category | flops | bytes accessed | tf_op | source)
XLA Modules:
  0.0 188.6 jit_solution(4767829598765810984)
XLA Ops:
  0.6 0.8 reshape.165
  1.4 0.1 fusion
  1.5 0.2 reduce_window_sum.11
  1.7 0.2 select_reduce_fusion.1
  1.9 0.1 select_reduce_fusion
  2.0 0.7 all_to_all.24
  2.7 7.3 %all-to-all-start = ((s32[32,1,8]{2,1,0:T(1,128)}), s32[32,1,8]{2,1,0:T(1,128)S(1)}, u32[]{:S(2)}, u32[]{:S(2)}) async-start(s32[32,1,8]{2,1,0:T(1,128)} %bitcast.1), calls=%async_computation | async-start | bytes 32768 | tf_op jit(solution)/shard_map/all_to_all | solution.py:19
  10.0 4.0 %prepare.1 = (f32[16,32,8,128]{3,2,1,0:T(8,128)}, bf16[16,32,8,128]{3,2,1,0:T(8,128)(2,1)S(1)}, f32[32,8,128]{2,1,0:T(8,128)}, f32[32,8,128]{2,1,0:T(8,128)}, f3...) custom-call(f32[16,32,8,128]{3,2,1,0:T(8,128)} %start_ref.1, s32[16,32,128]{2,1,0:T(8,128)} %active_ref.1), custom_call_target="tpu_custom_call" | custom-call | tf_op jit(solution)/shard_map/prepare/pallas_call | solution.py:167
  14.1 3.1 %all-to-all-done = s32[32,1,8]{2,1,0:T(1,128)S(1)} async-done(((s32[32,1,8]{2,1,0:T(1,128)}), s32[32,1,8]{2,1,0:T(1,128)S(1)}, u32[]{:S(2)}, u32[]{:S(2)}) %all-to-all-start) | async-done | bytes 1056 | tf_op jit(solution)/shard_map/all_to_all | solution.py:19
  17.3 1.6 gather_fusion
  18.9 2.7 %all-to-all-start.1 = ((bf16[32,8,8,128]{3,2,1,0:T(8,128)(2,1)}), bf16[32,8,8,128]{3,2,1,0:T(8,128)(2,1)S(1)}, u32[]{:S(2)}, u32[]{:S(2)}) async-start(bf16[32,8,8,128]{3,2,1,0:T(8,128)(2,1)} %bitcast.4), calls=%async_computation.1 | async-start | bytes 1048576 | tf_op jit(solution)/shard_map/all_to_all | solution.py:19
  21.7 0.6 copy.22.refs_0_
  22.3 14.9 %all-to-all-done.1 = bf16[32,8,8,128]{3,2,1,0:T(8,128)(2,1)S(1)} async-done(((bf16[32,8,8,128]{3,2,1,0:T(8,128)(2,1)}), bf16[32,8,8,128]{3,2,1,0:T(8,128)(2,1)S(1)}, u32[]{:S(2)}, u32[]{:S(2)}) %all-to-all-start.1) | async-done | bytes 524320 | tf_op jit(solution)/shard_map/all_to_all | solution.py:19
  37.3 10.9 %shard_map.104 = (f32[4,8,512]{2,1,0:T(8,128)}, bf16[256,8,128]{2,1,0:T(8,128)(2,1)}) custom-call(s32[128]{0:T(128)S(1)} %multiply_add_fusion.slot_ref, bf16[256,8,128]{2,1,0:T(8,128)(2,1)S(1)} %bitcast.24, bf16[4,512,4096]{2,1,0:T(8,128)(2,1)} %sensor_ref.5, f32[4,1,512]{2,1,0:T(1,128)} %copy.22.refs_0_, f32[4,8,512]{2,1,0:T(8,128)} %refs_3_.1), custom_call_target="tpu_custom_call" | custom-call | tf_op jit(solution)/shard_map/pallas_call | solution.py:43
  48.2 3.0 %all-to-all-start.2 = ((bf16[32,8,8,128]{3,2,1,0:T(8,128)(2,1)}), bf16[32,8,8,128]{3,2,1,0:T(8,128)(2,1)S(1)}, u32[]{:S(2)}, u32[]{:S(2)}) async-start(bf16[32,8,8,128]{3,2,1,0:T(8,128)(2,1)} %bitcast.40), calls=%async_computation.2 | async-start | bytes 1048576 | tf_op jit(solution)/shard_map/all_to_all | solution.py:19
  51.2 1.3 collective-permute-start
  52.5 4.6 %collective-permute-start.2 = (f32[32,8,128]{2,1,0:T(8,128)S(1)}, f32[32,8,128]{2,1,0:T(8,128)S(1)}, u32[]{:S(2)}, u32[]{:S(2)}) collective-permute-start(f32[32,8,128]{2,1,0:T(8,128)S(1)} %copy-done.15), channel_id=1, source_target_pairs={{0,4},{4,8},{8,12},{12,16},{16,20},{20,24},{24,28},{1,5},{5,9},{9,... | collective-permute-start | bytes 393224 | tf_op jit(solution)/shard_map/ppermute | solution.py:28
  57.1 1.3 collective-permute-start.1
  58.4 3.0 %collective-permute-start.3 = (f32[16,8,128]{2,1,0:T(8,128)S(1)}, f32[16,8,128]{2,1,0:T(8,128)S(1)}, u32[]{:S(2)}, u32[]{:S(2)}) collective-permute-start(f32[16,8,128]{2,1,0:T(8,128)S(1)} %copy-done.17), channel_id=1, source_target_pairs={{0,1},{1,2},{2,3},{4,5},{5,6},{6,7},{8,9},{9,10},{10,11},{12,13},{... | collective-permute-start | bytes 196616 | tf_op jit(solution)/shard_map/ppermute | solution.py:28
  61.4 0.5 broadcast.134
  62.0 0.7 reduce.5
  62.6 0.1 reshape.166.ids_ref
  62.8 1.9 collective-permute-done.2.refs_5_
  64.7 0.7 broadcast_in_dim.16.refs_2_.refs_0_
  65.3 7.4 %shard_map.105 = (f32[32,8,128]{2,1,0:T(8,128)}, f32[16,8,128]{2,1,0:T(8,128)}, f32[16,32,8,128]{3,2,1,0:T(8,128)}) custom-call(s32[1]{0:T(128)} %bitcast.base_ref._, s32[512,128]{1,0:T(8,128)} %bitcast.35, s32[512,128]{1,0:T(8,128)} %bitcast.27, f32[8,128]{1,0:T(8,128)} %broadcast_in_dim.16.refs_2_.refs_0_, f32[32,8,128]{2,1,0:T(8,128)} %copy-done, ...), custom_call_target="tpu_custom_call" | custom-call | tf_op jit(solution)/shard_map/pallas_call | solution.py:43
  72.8 5.5 %shard_map.106 = (bf16[256,8,128]{2,1,0:T(8,128)(2,1)}, f32[8,128]{1,0:T(8,128)}, bf16[32,8,128]{2,1,0:T(8,128)(2,1)}, bf16[32,8,128]{2,1,0:T(8,128)(2,1)}, bf16...) custom-call(s32[256]{0:T(256)S(1)} %reshape.166.ids_ref, ...), custom_call_target="tpu_custom_call" | custom-call | tf_op jit(solution)/shard_map/pallas_call | solution.py:43
  78.2 7.1 %all-to-all-start.3 = ((bf16[32,8,8,128]{3,2,1,0:T(8,128)(2,1)}), bf16[32,8,8,128]{3,2,1,0:T(8,128)(2,1)S(1)}, u32[]{:S(2)}, u32[]{:S(2)}) async-start(bf16[32,8,8,128]{3,2,1,0:T(8,128)(2,1)} %bitcast.42), calls=%async_computation.3 | async-start | bytes 1048576 | tf_op jit(solution)/shard_map/all_to_all | solution.py:19
  85.3 1.3 collective-permute-start.4
  86.6 1.5 collective-permute-start.5
  88.1 5.9 %shard_map.107.refs_2_ = f32[8,128]{1,0:T(8,128)} custom-call(s32[1]{0:T(128)} %bitcast.base_ref._, s32[512,128]{1,0:T(8,128)} %bitcast.36, s32[512,128]{1,0:T(8,128)} %bitcast.29, f32[16,32,8,128]{3,2,1,0:T(8,128)} %get-tuple-element.41.refs_7_.field_ref.refs_11_, f32[16,32,8,128]{3,2,1,0:T(8,128)} %bitcast.33), custom_call_target="tpu_custom_call" | custom-call | tf_op jit(solution)/shard_map/pallas_call | solution.py:43
  94.0 6.9 %all-to-all-done.3 = bf16[32,8,8,128]{3,2,1,0:T(8,128)(2,1)S(1)} async-done(((bf16[32,8,8,128]{3,2,1,0:T(8,128)(2,1)}), bf16[32,8,8,128]{3,2,1,0:T(8,128)(2,1)S(1)}, u32[]{:S(2)}, u32[]{:S(2)}) %all-to-all-start.3) | async-done | bytes 524320 | tf_op jit(solution)/shard_map/all_to_all | solution.py:19
  101.0 11.3 %shard_map.108 = (f32[4,8,512]{2,1,0:T(8,128)}, bf16[288,8,128]{2,1,0:T(8,128)(2,1)}) custom-call(s32[128]{0:T(128)S(1)} %multiply_add_fusion.slot_ref, bf16[256,8,128]{2,1,0:T(8,128)(2,1)S(1)} %bitcast.23, bf16[4,512,4096]{2,1,0:T(8,128)(2,1)} %sensor_ref.5, f32[4,1,512]{2,1,0:T(1,128)} %copy.22.refs_0_, f32[8,128]{1,0:T(8,128)} %get-tuple-element.44.refs_1_, ...), custom_call_target="tpu_custom_call" | custom-call | tf_op jit(solution)/shard_map/pallas_call | solution.py:43
  112.3 4.1 %all-to-all-start.4 = ((bf16[32,9,8,128]{3,2,1,0:T(8,128)(2,1)}), bf16[32,9,8,128]{3,2,1,0:T(8,128)(2,1)S(1)}, u32[]{:S(2)}, u32[]{:S(2)}) async-start(bf16[32,9,8,128]{3,2,1,0:T(8,128)(2,1)} %bitcast.39), calls=%async_computation.4 | async-start | bytes 1179648 | tf_op jit(solution)/shard_map/all_to_all | solution.py:19
  116.4 2.2 %collective-permute-start.7 = (bf16[16,8,128]{2,1,0:T(8,128)(2,1)S(1)}, bf16[16,8,128]{2,1,0:T(8,128)(2,1)S(1)}, u32[]{:S(2)}, u32[]{:S(2)}) collective-permute-start(bf16[16,8,128]{2,1,0:T(8,128)(2,1)S(1)} %copy-done.9), channel_id=1, source_target_pairs={{0,1},{1,2},{2,3},{4,5},{5,6},{6,7},{8,9},{9,10},{10,11},{12,13},{... | collective-permute-start | bytes 98312 | tf_op jit(solution)/shard_map/ppermute | solution.py:28
  118.6 3.5 %collective-permute-start.6 = (bf16[32,8,128]{2,1,0:T(8,128)(2,1)S(1)}, bf16[32,8,128]{2,1,0:T(8,128)(2,1)S(1)}, u32[]{:S(2)}, u32[]{:S(2)}) collective-permute-start(bf16[32,8,128]{2,1,0:T(8,128)(2,1)S(1)} %copy-done.6), channel_id=1, source_target_pairs={{0,4},{4,8},{8,12},{12,16},{16,20},{20,24},{24,28},{1,5},{5,9},{9,... | collective-permute-start | bytes 196616 | tf_op jit(solution)/shard_map/ppermute | solution.py:28
  122.2 2.2 %collective-permute-done.6.refs_9_ = bf16[32,8,128]{2,1,0:T(8,128)(2,1)S(1)} collective-permute-done((bf16[32,8,128]{2,1,0:T(8,128)(2,1)S(1)}, bf16[32,8,128]{2,1,0:T(8,128)(2,1)S(1)}, u32[]{:S(2)}, u32[]{:S(2)}) %collective-permute-start.6) | collective-permute-done | bytes 65568 | tf_op jit(solution)/shard_map/ppermute | solution.py:28
  124.4 8.8 %all-to-all-done.4 = bf16[32,9,8,128]{3,2,1,0:T(8,128)(2,1)S(1)} async-done(((bf16[32,9,8,128]{3,2,1,0:T(8,128)(2,1)}), bf16[32,9,8,128]{3,2,1,0:T(8,128)(2,1)S(1)}, u32[]{:S(2)}, u32[]{:S(2)}) %all-to-all-start.4) | async-done | bytes 589856 | tf_op jit(solution)/shard_map/all_to_all | solution.py:19
  133.2 10.8 %shard_map.109 = (bf16[256,8,128]{2,1,0:T(8,128)(2,1)}, f32[8,128]{1,0:T(8,128)}, bf16[32,8,128]{2,1,0:T(8,128)(2,1)}, bf16[32,8,128]{2,1,0:T(8,128)(2,1)}, bf16...) custom-call(s32[257]{0:T(512)S(1)} %pad_add_fusion.ids_ref, ...), custom_call_target="tpu_custom_call" | custom-call | tf_op jit(solution)/shard_map/pallas_call | solution.py:43
  144.1 4.3 %all-to-all-start.5 = ((bf16[32,8,8,128]{3,2,1,0:T(8,128)(2,1)}), bf16[32,8,8,128]{3,2,1,0:T(8,128)(2,1)S(1)}, u32[]{:S(2)}, u32[]{:S(2)}) async-start(bf16[32,8,8,128]{3,2,1,0:T(8,128)(2,1)} %bitcast.41), calls=%async_computation.5 | async-start | bytes 1048576 | tf_op jit(solution)/shard_map/all_to_all | solution.py:19
  148.4 1.3 collective-permute-start.8
  149.7 1.3 collective-permute-start.9
  151.0 5.9 %shard_map.110.refs_2_ = f32[8,128]{1,0:T(8,128)} custom-call(s32[1]{0:T(128)} %bitcast.base_ref._, s32[512,128]{1,0:T(8,128)} %bitcast.38, s32[512,128]{1,0:T(8,128)} %bitcast.31, f32[16,32,8,128]{3,2,1,0:T(8,128)} %get-tuple-element.55.field_ref.refs_7_, f32[16,32,8,128]{3,2,1,0:T(8,128)} %get-tuple-element.56.grad_ref.refs_8_), custom_call_target="tpu_custom_call" | custom-call | tf_op jit(solution)/shard_map/pallas_call | solution.py:43
  156.9 7.1 %all-to-all-done.5 = bf16[32,8,8,128]{3,2,1,0:T(8,128)(2,1)S(1)} async-done(((bf16[32,8,8,128]{3,2,1,0:T(8,128)(2,1)}), bf16[32,8,8,128]{3,2,1,0:T(8,128)(2,1)S(1)}, u32[]{:S(2)}, u32[]{:S(2)}) %all-to-all-start.5) | async-done | bytes 524320 | tf_op jit(solution)/shard_map/all_to_all | solution.py:19
  164.0 8.2 %shard_map.111 = (f32[4,8,512]{2,1,0:T(8,128)}, f32[32,8,128]{2,1,0:T(8,128)}) custom-call(s32[128]{0:T(128)S(1)} %multiply_add_fusion.slot_ref, bf16[256,8,128]{2,1,0:T(8,128)(2,1)S(1)} %bitcast.22, bf16[4,512,4096]{2,1,0:T(8,128)(2,1)} %sensor_ref.5, f32[4,1,512]{2,1,0:T(1,128)} %copy.22.refs_0_, f32[8,128]{1,0:T(8,128)} %get-tuple-element.54.refs_1_, ...), custom_call_target="tpu_custom_call" | custom-call | tf_op jit(solution)/shard_map/pallas_call | solution.py:43
  172.2 4.1 %all-to-all-start.6 = ((f32[32,8,128]{2,1,0:T(8,128)}), f32[32,8,128]{2,1,0:T(8,128)S(1)}, u32[]{:S(2)}, u32[]{:S(2)}) async-start(f32[32,8,128]{2,1,0:T(8,128)} %get-tuple-element.63), calls=%async_computation.6 | async-start | bytes 262144 | tf_op jit(solution)/shard_map/all_to_all | solution.py:19
  176.3 0.6 mul.37.refs_2_
  176.9 7.6 %all-to-all-done.6.got_ref = f32[32,8,128]{2,1,0:T(8,128)S(1)} async-done(((f32[32,8,128]{2,1,0:T(8,128)}), f32[32,8,128]{2,1,0:T(8,128)S(1)}, u32[]{:S(2)}, u32[]{:S(2)}) %all-to-all-start.6) | async-done | bytes 131104 | tf_op jit(solution)/shard_map/all_to_all | solution.py:19
  184.5 3.9 %shard_map.112 = (f32[16,32,8,128]{3,2,1,0:T(8,128)}, f32[4,8,512]{2,1,0:T(8,128)}) custom-call(s32[1]{0:T(128)} %bitcast.base_ref._, f32[32,8,128]{2,1,0:T(8,128)S(1)} %all-to-all-done.6.got_ref, f32[8,128]{1,0:T(8,128)} %broadcast_in_dim.16.refs_2_.refs_0_, f32[8,128]{1,0:T(8,128)} %get-tuple-element.64.refs_1_, f32[4,1,512]{2,1,0:T(1,128)} %mul.37.refs_2_, ...), custom_call_target="tpu_custom_call" | custom-call | tf_op jit(solution)/shard_map/pallas_call | solution.py:43
  (54 shorter events, 0.3 us)
Async XLA Ops:
  2.7 14.5 %all-to-all-start = ((s32[32,1,8]{2,1,0:T(1,128)}), s32[32,1,8]{2,1,0:T(1,128)S(1)}, u32[]{:S(2)}, u32[]{:S(2)}) async-start(s32[32,1,8]{2,1,0:T(1,128)} %bitcast.1), calls=%async_computation | async-start | bytes 32768 | tf_op jit(solution)/shard_map/all_to_all | solution.py:19
  10.0 11.6 %copy-start.12 = (f32[4,512]{1,0:T(4,128)S(1)}, f32[4,512]{1,0:T(4,128)}, u32[]{:S(2)}) copy-start(f32[4,512]{1,0:T(4,128)} %param.11) | copy-start | bytes 24580
  10.0 11.6 %copy-start.13 = (s32[4]{0:T(128)S(1)}, s32[4]{0:T(128)}, u32[]{:S(2)}) copy-start(s32[4]{0:T(128)} %param.12) | copy-start | bytes 52
  18.9 18.4 %all-to-all-start.1 = ((bf16[32,8,8,128]{3,2,1,0:T(8,128)(2,1)}), bf16[32,8,8,128]{3,2,1,0:T(8,128)(2,1)S(1)}, u32[]{:S(2)}, u32[]{:S(2)}) async-start(bf16[32,8,8,128]{3,2,1,0:T(8,128)(2,1)} %bitcast.4), calls=%async_computation.1 | async-start | bytes 1048576 | tf_op jit(solution)/shard_map/all_to_all | solution.py:19
  37.2 14.0 %copy-start.16 = (f32[32,8,128]{2,1,0:T(8,128)S(1)}, f32[32,8,128]{2,1,0:T(8,128)}, u32[]{:S(2)}) copy-start(f32[32,8,128]{2,1,0:T(8,128)} %get-tuple-element.37) | copy-start | bytes 393220
  37.2 15.3 %copy-start.15 = (f32[32,8,128]{2,1,0:T(8,128)S(1)}, f32[32,8,128]{2,1,0:T(8,128)}, u32[]{:S(2)}) copy-start(f32[32,8,128]{2,1,0:T(8,128)} %get-tuple-element.39) | copy-start | bytes 393220
  37.2 19.8 %copy-start.18 = (f32[16,8,128]{2,1,0:T(8,128)S(1)}, f32[16,8,128]{2,1,0:T(8,128)}, u32[]{:S(2)}) copy-start(f32[16,8,128]{2,1,0:T(8,128)} %get-tuple-element.38) | copy-start | bytes 196612
  37.2 21.1 %copy-start.17 = (f32[16,8,128]{2,1,0:T(8,128)S(1)}, f32[16,8,128]{2,1,0:T(8,128)}, u32[]{:S(2)}) copy-start(f32[16,8,128]{2,1,0:T(8,128)} %get-tuple-element.40) | copy-start | bytes 196612
  37.3 27.4 %copy-start.14 = (f32[8]{0:T(128)S(1)}, f32[8]{0:T(128)}, u32[]{:S(2)}) copy-start(f32[8]{0:T(128)} %param.17) | copy-start | bytes 100
  48.2 24.6 %all-to-all-start.2 = ((bf16[32,8,8,128]{3,2,1,0:T(8,128)(2,1)}), bf16[32,8,8,128]{3,2,1,0:T(8,128)(2,1)S(1)}, u32[]{:S(2)}, u32[]{:S(2)}) async-start(bf16[32,8,8,128]{3,2,1,0:T(8,128)(2,1)} %bitcast.40), calls=%async_computation.2 | async-start | bytes 1048576 | tf_op jit(solution)/shard_map/all_to_all | solution.py:19
  51.2 11.6 %collective-permute-start = (f32[32,8,128]{2,1,0:T(8,128)S(1)}, f32[32,8,128]{2,1,0:T(8,128)S(1)}, u32[]{:S(2)}, u32[]{:S(2)}) collective-permute-start(f32[32,8,128]{2,1,0:T(8,128)S(1)} %copy-done.16), channel_id=1, source_target_pairs={{4,0},{8,4},{12,8},{16,12},{20,16},{24,20},{28,24},{5,1},{9,5},{13... | collective-permute-start | bytes 393224 | tf_op jit(solution)/shard_map/ppermute | solution.py:26
  52.5 12.1 %collective-permute-start.2 = (f32[32,8,128]{2,1,0:T(8,128)S(1)}, f32[32,8,128]{2,1,0:T(8,128)S(1)}, u32[]{:S(2)}, u32[]{:S(2)}) collective-permute-start(f32[32,8,128]{2,1,0:T(8,128)S(1)} %copy-done.15), channel_id=1, source_target_pairs={{0,4},{4,8},{8,12},{12,16},{16,20},{20,24},{24,28},{1,5},{5,9},{9,... | collective-permute-start | bytes 393224 | tf_op jit(solution)/shard_map/ppermute | solution.py:28
  57.1 5.7 %collective-permute-start.1 = (f32[16,8,128]{2,1,0:T(8,128)S(1)}, f32[16,8,128]{2,1,0:T(8,128)S(1)}, u32[]{:S(2)}, u32[]{:S(2)}) collective-permute-start(f32[16,8,128]{2,1,0:T(8,128)S(1)} %copy-done.18), channel_id=1, source_target_pairs={{1,0},{2,1},{3,2},{5,4},{6,5},{7,6},{9,8},{10,9},{11,10},{13,12},{... | collective-permute-start | bytes 196616 | tf_op jit(solution)/shard_map/ppermute | solution.py:26
  58.4 4.4 %collective-permute-start.3 = (f32[16,8,128]{2,1,0:T(8,128)S(1)}, f32[16,8,128]{2,1,0:T(8,128)S(1)}, u32[]{:S(2)}, u32[]{:S(2)}) collective-permute-start(f32[16,8,128]{2,1,0:T(8,128)S(1)} %copy-done.17), channel_id=1, source_target_pairs={{0,1},{1,2},{2,3},{4,5},{5,6},{6,7},{8,9},{9,10},{10,11},{12,13},{... | collective-permute-start | bytes 196616 | tf_op jit(solution)/shard_map/ppermute | solution.py:28
  62.7 2.6 %copy-start.3 = (f32[16,8,128]{2,1,0:T(8,128)}, f32[16,8,128]{2,1,0:T(8,128)S(1)}, u32[]{:S(2)}) copy-start(f32[16,8,128]{2,1,0:T(8,128)S(1)} %collective-permute-done.1.refs_4_) | copy-start | bytes 196612
  62.8 2.6 %copy-start.4 = (f32[16,8,128]{2,1,0:T(8,128)}, f32[16,8,128]{2,1,0:T(8,128)S(1)}, u32[]{:S(2)}) copy-start(f32[16,8,128]{2,1,0:T(8,128)S(1)} %collective-permute-done.3.refs_6_) | copy-start | bytes 196612
  62.8 2.5 %copy-start = (f32[32,8,128]{2,1,0:T(8,128)}, f32[32,8,128]{2,1,0:T(8,128)S(1)}, u32[]{:S(2)}) copy-start(f32[32,8,128]{2,1,0:T(8,128)S(1)} %collective-permute-done.refs_3_) | copy-start | bytes 393220
  64.7 0.7 copy-start.1
  78.2 22.7 %all-to-all-start.3 = ((bf16[32,8,8,128]{3,2,1,0:T(8,128)(2,1)}), bf16[32,8,8,128]{3,2,1,0:T(8,128)(2,1)S(1)}, u32[]{:S(2)}, u32[]{:S(2)}) async-start(bf16[32,8,8,128]{3,2,1,0:T(8,128)(2,1)} %bitcast.42), calls=%async_computation.3 | async-start | bytes 1048576 | tf_op jit(solution)/shard_map/all_to_all | solution.py:19
  85.3 8.7 %collective-permute-start.4 = (bf16[32,8,128]{2,1,0:T(8,128)(2,1)}, bf16[32,8,128]{2,1,0:T(8,128)(2,1)S(1)}, u32[]{:S(2)}, u32[]{:S(2)}) collective-permute-start(bf16[32,8,128]{2,1,0:T(8,128)(2,1)} %get-tuple-element.48), channel_id=1, source_target_pairs={{4,0},{8,4},{12,8},{16,12},{20,16},{24,20},{28,24},{5,1},{9,5},{13... | collective-permute-start | bytes 196616 | tf_op jit(solution)/shard_map/ppermute | solution.py:26
  86.6 7.4 %collective-permute-start.5 = (bf16[16,8,128]{2,1,0:T(8,128)(2,1)}, bf16[16,8,128]{2,1,0:T(8,128)(2,1)S(1)}, u32[]{:S(2)}, u32[]{:S(2)}) collective-permute-start(bf16[16,8,128]{2,1,0:T(8,128)(2,1)} %get-tuple-element.51), channel_id=1, source_target_pairs={{1,0},{2,1},{3,2},{5,4},{6,5},{7,6},{9,8},{10,9},{11,10},{13,12},{... | collective-permute-start | bytes 98312 | tf_op jit(solution)/shard_map/ppermute | solution.py:26
  94.0 7.0 %copy-start.5 = (bf16[16,8,128]{2,1,0:T(8,128)(2,1)}, bf16[16,8,128]{2,1,0:T(8,128)(2,1)S(1)}, u32[]{:S(2)}) copy-start(bf16[16,8,128]{2,1,0:T(8,128)(2,1)S(1)} %collective-permute-done.5.refs_8_) | copy-start | bytes 98308
  94.0 6.9 %copy-start.2 = (bf16[32,8,128]{2,1,0:T(8,128)(2,1)}, bf16[32,8,128]{2,1,0:T(8,128)(2,1)S(1)}, u32[]{:S(2)}) copy-start(bf16[32,8,128]{2,1,0:T(8,128)(2,1)S(1)} %collective-permute-done.4.refs_5_.refs_7_) | copy-start | bytes 196612
  101.0 15.5 %copy-start.9 = (bf16[16,8,128]{2,1,0:T(8,128)(2,1)S(1)}, bf16[16,8,128]{2,1,0:T(8,128)(2,1)}, u32[]{:S(2)}) copy-start(bf16[16,8,128]{2,1,0:T(8,128)(2,1)} %get-tuple-element.50.refs_7_) | copy-start | bytes 98308
  101.0 17.6 %copy-start.6 = (bf16[32,8,128]{2,1,0:T(8,128)(2,1)S(1)}, bf16[32,8,128]{2,1,0:T(8,128)(2,1)}, u32[]{:S(2)}) copy-start(bf16[32,8,128]{2,1,0:T(8,128)(2,1)} %get-tuple-element.47.refs_4_) | copy-start | bytes 196612
  112.3 20.9 %all-to-all-start.4 = ((bf16[32,9,8,128]{3,2,1,0:T(8,128)(2,1)}), bf16[32,9,8,128]{3,2,1,0:T(8,128)(2,1)S(1)}, u32[]{:S(2)}, u32[]{:S(2)}) async-start(bf16[32,9,8,128]{3,2,1,0:T(8,128)(2,1)} %bitcast.39), calls=%async_computation.4 | async-start | bytes 1179648 | tf_op jit(solution)/shard_map/all_to_all | solution.py:19
  116.4 5.7 %collective-permute-start.7 = (bf16[16,8,128]{2,1,0:T(8,128)(2,1)S(1)}, bf16[16,8,128]{2,1,0:T(8,128)(2,1)S(1)}, u32[]{:S(2)}, u32[]{:S(2)}) collective-permute-start(bf16[16,8,128]{2,1,0:T(8,128)(2,1)S(1)} %copy-done.9), channel_id=1, source_target_pairs={{0,1},{1,2},{2,3},{4,5},{5,6},{6,7},{8,9},{9,10},{10,11},{12,13},{... | collective-permute-start | bytes 98312 | tf_op jit(solution)/shard_map/ppermute | solution.py:28
  118.6 5.8 %collective-permute-start.6 = (bf16[32,8,128]{2,1,0:T(8,128)(2,1)S(1)}, bf16[32,8,128]{2,1,0:T(8,128)(2,1)S(1)}, u32[]{:S(2)}, u32[]{:S(2)}) collective-permute-start(bf16[32,8,128]{2,1,0:T(8,128)(2,1)S(1)} %copy-done.6), channel_id=1, source_target_pairs={{0,4},{4,8},{8,12},{12,16},{16,20},{20,24},{24,28},{1,5},{5,9},{9,... | collective-permute-start | bytes 196616 | tf_op jit(solution)/shard_map/ppermute | solution.py:28
  122.2 11.0 %copy-start.10 = (bf16[16,8,128]{2,1,0:T(8,128)(2,1)}, bf16[16,8,128]{2,1,0:T(8,128)(2,1)S(1)}, u32[]{:S(2)}) copy-start(bf16[16,8,128]{2,1,0:T(8,128)(2,1)S(1)} %collective-permute-done.7.refs_10_) | copy-start | bytes 98308
  124.4 8.8 %copy-start.7 = (bf16[32,8,128]{2,1,0:T(8,128)(2,1)}, bf16[32,8,128]{2,1,0:T(8,128)(2,1)S(1)}, u32[]{:S(2)}) copy-start(bf16[32,8,128]{2,1,0:T(8,128)(2,1)S(1)} %collective-permute-done.6.refs_9_) | copy-start | bytes 196612
  144.1 19.9 %all-to-all-start.5 = ((bf16[32,8,8,128]{3,2,1,0:T(8,128)(2,1)}), bf16[32,8,8,128]{3,2,1,0:T(8,128)(2,1)S(1)}, u32[]{:S(2)}, u32[]{:S(2)}) async-start(bf16[32,8,8,128]{3,2,1,0:T(8,128)(2,1)} %bitcast.41), calls=%async_computation.5 | async-start | bytes 1048576 | tf_op jit(solution)/shard_map/all_to_all | solution.py:19
  148.4 8.5 %collective-permute-start.8 = (bf16[32,8,128]{2,1,0:T(8,128)(2,1)}, bf16[32,8,128]{2,1,0:T(8,128)(2,1)S(1)}, u32[]{:S(2)}, u32[]{:S(2)}) collective-permute-start(bf16[32,8,128]{2,1,0:T(8,128)(2,1)} %get-tuple-element.59), channel_id=1, source_target_pairs={{4,0},{8,4},{12,8},{16,12},{20,16},{24,20},{28,24},{5,1},{9,5},{13... | collective-permute-start | bytes 196616 | tf_op jit(solution)/shard_map/ppermute | solution.py:26
  149.7 7.2 %collective-permute-start.9 = (bf16[16,8,128]{2,1,0:T(8,128)(2,1)}, bf16[16,8,128]{2,1,0:T(8,128)(2,1)S(1)}, u32[]{:S(2)}, u32[]{:S(2)}) collective-permute-start(bf16[16,8,128]{2,1,0:T(8,128)(2,1)} %get-tuple-element.62), channel_id=1, source_target_pairs={{1,0},{2,1},{3,2},{5,4},{6,5},{7,6},{9,8},{10,9},{11,10},{13,12},{... | collective-permute-start | bytes 98312 | tf_op jit(solution)/shard_map/ppermute | solution.py:26
  156.9 7.1 %copy-start.11 = (bf16[16,8,128]{2,1,0:T(8,128)(2,1)}, bf16[16,8,128]{2,1,0:T(8,128)(2,1)S(1)}, u32[]{:S(2)}) copy-start(bf16[16,8,128]{2,1,0:T(8,128)(2,1)S(1)} %collective-permute-done.9.refs_8_) | copy-start | bytes 98308
  156.9 7.1 %copy-start.8 = (bf16[32,8,128]{2,1,0:T(8,128)(2,1)}, bf16[32,8,128]{2,1,0:T(8,128)(2,1)S(1)}, u32[]{:S(2)}) copy-start(bf16[32,8,128]{2,1,0:T(8,128)(2,1)S(1)} %collective-permute-done.8.refs_5_) | copy-start | bytes 196612
  172.2 12.3 %all-to-all-start.6 = ((f32[32,8,128]{2,1,0:T(8,128)}), f32[32,8,128]{2,1,0:T(8,128)S(1)}, u32[]{:S(2)}, u32[]{:S(2)}) async-start(f32[32,8,128]{2,1,0:T(8,128)} %get-tuple-element.63), calls=%async_computation.6 | async-start | bytes 262144 | tf_op jit(solution)/shard_map/all_to_all | solution.py:19

commit v6 on v5

--- a/solution.py
+++ b/solution.py
@@ -33,8 +33,20 @@
 FAR = pl.BlockSpec(memory_space=pltpu.HBM)
 
 
+class Free:
+    def __init__(self, array):
+        self.array = array
+        self.shape, self.dtype = (array.shape, array.dtype)
+
+
 def far(array):
+    if isinstance(array, Free):
+        return array.array
     return pltpu.with_memory_space_constraint(array, pltpu.HBM)
+
+
+def far_spec(array):
+    return pl.BlockSpec(memory_space=pl.ANY) if isinstance(array, Free) else FAR
 
 
 def kernel_call(kernel, table, near, distant, outs, distant_outs, scratch):
@@ -46,7 +58,7 @@
         grid_spec=pltpu.PrefetchScalarGridSpec(
             num_scalar_prefetch=1,
             grid=(),
-            in_specs=near_specs + [FAR] * len(distant),
+            in_specs=near_specs + [far_spec(d) for d in distant],
             out_specs=[pl.BlockSpec(o.shape, functools.partial(origin, o.ndim)) for o in outs]
             + [FAR] * len(distant_outs),
             scratch_shapes=scratch,
@@ -366,7 +378,7 @@
 ):
     layers, rows, samples, cells = field.shape
     f32, bf16 = (jnp.float32, jnp.bfloat16)
-    small = [links, active, scale, *rims, *grad_rims]
+    small = [links, active, scale, *rims, *(Free(rim) for rim in grad_rims)]
     pad = pltpu.VMEM((layers + 1, rows + 1, samples, cells), f32)
     rim_z, rim_y = ((rows, samples, cells), (layers, samples, cells))
     outs = [
@@ -824,7 +836,8 @@
         )
 
     def sums_inputs(norm, faces, edge_z, edge_y, mine, theirs):
-        return [weight_sq, norm, faces, edge_z, mine[0], theirs[0], edge_y, mine[1], theirs[1]]
+        below, right = (Free(rim) for rim in theirs[:2])
+        return [weight_sq, norm, faces, edge_z, mine[0], below, edge_y, mine[1], right]
 
     grid = (depth_count, base, links, active_flat)
     model, bricks, *rims = prepare_call(start_model, active_cells)

time: 190 us -> 188 us (0.989)
  no operation moved by 1% of the time
where the time goes in v6:
time: 188 us; the launch traced here: 187 us
  Pallas kernels  73.7 us (39%)
  waiting for transfers between devices  52.6 us (28%)
  starting transfers between devices  52.1 us (28%)
  local copies, waits for them, and re-layouts  5.65 us (3%)
    pallas_call x9, Pallas kernels, kernel_call(): pl.pallas_call(kernel, out_shape=out_shapes, grid_spec=pltpu.PrefetchScal...  69.7 us
    all_to_all x7, waiting for transfers between devices, swap(): return lax.all_to_all(field, AXES, split_axis=0, concat_axis=0, tiled=True)  48.5 us
    all_to_all x7, starting transfers between devices, swap(): return lax.all_to_all(field, AXES, split_axis=0, concat_axis=0, tiled=True)  30.9 us
    ppermute x4, starting transfers between devices, edges(): lax.ppermute(last, axis, [(i, i + 1) for i in range(count - 1)])  13.3 us
    ppermute x6, starting transfers between devices, edges(): lax.ppermute(first, axis, [(i + 1, i) for i in range(count - 1)])  7.93 us
    ppermute x4, waiting for transfers between devices, edges(): lax.ppermute(last, axis, [(i, i + 1) for i in range(count - 1)])  4.08 us
    pallas_call x1, Pallas kernels, prepare_call(): pl.pallas_call(prepare_kernel, name='prepare', grid=(layers // step,), in...  4.04 us
  transfers between devices with their start and end apart: 17, of which 8 were waited for; matrix products, arithmetic and copies ran while one was open for 2% of the time, Pallas kernels for 12%

profile of v6, /device:TPU:0, one launch (start us, length us, event | category | flops | bytes accessed | tf_op | source)
XLA Modules:
  0.0 186.7 jit_solution(10356864258084395845)
XLA Ops:
  0.6 0.8 reshape.165
  1.4 0.1 fusion
  1.5 0.2 reduce_window_sum.11
  1.7 0.2 select_reduce_fusion.1
  1.9 0.1 select_reduce_fusion
  2.0 0.7 all_to_all.24
  2.7 7.3 %all-to-all-start = ((s32[32,1,8]{2,1,0:T(1,128)}), s32[32,1,8]{2,1,0:T(1,128)S(1)}, u32[]{:S(2)}, u32[]{:S(2)}) async-start(s32[32,1,8]{2,1,0:T(1,128)} %bitcast.1), calls=%async_computation | async-start | bytes 32768 | tf_op jit(solution)/shard_map/all_to_all | solution.py:19
  10.0 4.0 %prepare.1 = (f32[16,32,8,128]{3,2,1,0:T(8,128)}, bf16[16,32,8,128]{3,2,1,0:T(8,128)(2,1)S(1)}, f32[32,8,128]{2,1,0:T(8,128)}, f32[32,8,128]{2,1,0:T(8,128)}, f3...) custom-call(f32[16,32,8,128]{3,2,1,0:T(8,128)} %start_ref.1, s32[16,32,128]{2,1,0:T(8,128)} %active_ref.1), custom_call_target="tpu_custom_call" | custom-call | tf_op jit(solution)/shard_map/prepare/pallas_call | solution.py:179
  14.1 3.1 %all-to-all-done = s32[32,1,8]{2,1,0:T(1,128)S(1)} async-done(((s32[32,1,8]{2,1,0:T(1,128)}), s32[32,1,8]{2,1,0:T(1,128)S(1)}, u32[]{:S(2)}, u32[]{:S(2)}) %all-to-all-start) | async-done | bytes 1056 | tf_op jit(solution)/shard_map/all_to_all | solution.py:19
  17.3 1.6 gather_fusion
  18.9 2.7 %all-to-all-start.1 = ((bf16[32,8,8,128]{3,2,1,0:T(8,128)(2,1)}), bf16[32,8,8,128]{3,2,1,0:T(8,128)(2,1)S(1)}, u32[]{:S(2)}, u32[]{:S(2)}) async-start(bf16[32,8,8,128]{3,2,1,0:T(8,128)(2,1)} %bitcast.4), calls=%async_computation.1 | async-start | bytes 1048576 | tf_op jit(solution)/shard_map/all_to_all | solution.py:19
  21.7 0.6 copy.22.refs_0_
  22.3 14.9 %all-to-all-done.1 = bf16[32,8,8,128]{3,2,1,0:T(8,128)(2,1)S(1)} async-done(((bf16[32,8,8,128]{3,2,1,0:T(8,128)(2,1)}), bf16[32,8,8,128]{3,2,1,0:T(8,128)(2,1)S(1)}, u32[]{:S(2)}, u32[]{:S(2)}) %all-to-all-start.1) | async-done | bytes 524320 | tf_op jit(solution)/shard_map/all_to_all | solution.py:19
  37.3 10.9 %shard_map.104 = (f32[4,8,512]{2,1,0:T(8,128)}, bf16[256,8,128]{2,1,0:T(8,128)(2,1)}) custom-call(s32[128]{0:T(128)S(1)} %multiply_add_fusion.slot_ref, bf16[256,8,128]{2,1,0:T(8,128)(2,1)S(1)} %bitcast.24, bf16[4,512,4096]{2,1,0:T(8,128)(2,1)} %sensor_ref.5, f32[4,1,512]{2,1,0:T(1,128)} %copy.22.refs_0_, f32[4,8,512]{2,1,0:T(8,128)} %refs_3_.1), custom_call_target="tpu_custom_call" | custom-call | tf_op jit(solution)/shard_map/pallas_call | solution.py:55
  48.2 3.0 %all-to-all-start.2 = ((bf16[32,8,8,128]{3,2,1,0:T(8,128)(2,1)}), bf16[32,8,8,128]{3,2,1,0:T(8,128)(2,1)S(1)}, u32[]{:S(2)}, u32[]{:S(2)}) async-start(bf16[32,8,8,128]{3,2,1,0:T(8,128)(2,1)} %bitcast.40), calls=%async_computation.2 | async-start | bytes 1048576 | tf_op jit(solution)/shard_map/all_to_all | solution.py:19
  51.2 1.3 collective-permute-start
  52.5 4.6 %collective-permute-start.2 = (f32[32,8,128]{2,1,0:T(8,128)S(1)}, f32[32,8,128]{2,1,0:T(8,128)S(1)}, u32[]{:S(2)}, u32[]{:S(2)}) collective-permute-start(f32[32,8,128]{2,1,0:T(8,128)S(1)} %copy-done.9), channel_id=1, source_target_pairs={{0,4},{4,8},{8,12},{12,16},{16,20},{20,24},{24,28},{1,5},{5,9},{9,... | collective-permute-start | bytes 393224 | tf_op jit(solution)/shard_map/ppermute | solution.py:28
  57.1 1.3 collective-permute-start.1
  58.4 3.0 %collective-permute-start.3 = (f32[16,8,128]{2,1,0:T(8,128)S(1)}, f32[16,8,128]{2,1,0:T(8,128)S(1)}, u32[]{:S(2)}, u32[]{:S(2)}) collective-permute-start(f32[16,8,128]{2,1,0:T(8,128)S(1)} %copy-done.11), channel_id=1, source_target_pairs={{0,1},{1,2},{2,3},{4,5},{5,6},{6,7},{8,9},{9,10},{10,11},{12,13},{... | collective-permute-start | bytes 196616 | tf_op jit(solution)/shard_map/ppermute | solution.py:28
  61.4 0.5 broadcast.134
  62.0 0.7 reduce.5
  62.6 0.1 reshape.166.ids_ref
  62.8 1.9 collective-permute-done.2.refs_5_
  64.7 0.7 broadcast_in_dim.16.refs_2_.refs_0_
  65.3 7.4 %shard_map.105 = (f32[32,8,128]{2,1,0:T(8,128)}, f32[16,8,128]{2,1,0:T(8,128)}, f32[16,32,8,128]{3,2,1,0:T(8,128)}) custom-call(s32[1]{0:T(128)} %bitcast.base_ref._, s32[512,128]{1,0:T(8,128)} %bitcast.35, s32[512,128]{1,0:T(8,128)} %bitcast.27, f32[8,128]{1,0:T(8,128)} %broadcast_in_dim.16.refs_2_.refs_0_, f32[32,8,128]{2,1,0:T(8,128)} %copy-done, ...), custom_call_target="tpu_custom_call" | custom-call | tf_op jit(solution)/shard_map/pallas_call | solution.py:55
  72.8 5.4 %shard_map.106 = (bf16[256,8,128]{2,1,0:T(8,128)(2,1)}, f32[8,128]{1,0:T(8,128)}, bf16[32,8,128]{2,1,0:T(8,128)(2,1)}, bf16[32,8,128]{2,1,0:T(8,128)(2,1)}, bf16...) custom-call(s32[256]{0:T(256)S(1)} %reshape.166.ids_ref, ...), custom_call_target="tpu_custom_call" | custom-call | tf_op jit(solution)/shard_map/pallas_call | solution.py:55
  78.2 7.1 %all-to-all-start.3 = ((bf16[32,8,8,128]{3,2,1,0:T(8,128)(2,1)}), bf16[32,8,8,128]{3,2,1,0:T(8,128)(2,1)S(1)}, u32[]{:S(2)}, u32[]{:S(2)}) async-start(bf16[32,8,8,128]{3,2,1,0:T(8,128)(2,1)} %bitcast.42), calls=%async_computation.3 | async-start | bytes 1048576 | tf_op jit(solution)/shard_map/all_to_all | solution.py:19
  85.3 1.3 collective-permute-start.4
  86.6 1.5 collective-permute-start.5
  88.1 5.9 %shard_map.107.refs_2_ = f32[8,128]{1,0:T(8,128)} custom-call(s32[1]{0:T(128)} %bitcast.base_ref._, s32[512,128]{1,0:T(8,128)} %bitcast.36, s32[512,128]{1,0:T(8,128)} %bitcast.29, f32[16,32,8,128]{3,2,1,0:T(8,128)} %get-tuple-element.41.refs_7_.field_ref.refs_11_, f32[16,32,8,128]{3,2,1,0:T(8,128)} %bitcast.33), custom_call_target="tpu_custom_call" | custom-call | tf_op jit(solution)/shard_map/pallas_call | solution.py:55
  94.0 6.9 %all-to-all-done.3 = bf16[32,8,8,128]{3,2,1,0:T(8,128)(2,1)S(1)} async-done(((bf16[32,8,8,128]{3,2,1,0:T(8,128)(2,1)}), bf16[32,8,8,128]{3,2,1,0:T(8,128)(2,1)S(1)}, u32[]{:S(2)}, u32[]{:S(2)}) %all-to-all-start.3) | async-done | bytes 524320 | tf_op jit(solution)/shard_map/all_to_all | solution.py:19
  100.9 11.3 %shard_map.108 = (f32[4,8,512]{2,1,0:T(8,128)}, bf16[288,8,128]{2,1,0:T(8,128)(2,1)}) custom-call(s32[128]{0:T(128)S(1)} %multiply_add_fusion.slot_ref, bf16[256,8,128]{2,1,0:T(8,128)(2,1)S(1)} %bitcast.23, bf16[4,512,4096]{2,1,0:T(8,128)(2,1)} %sensor_ref.5, f32[4,1,512]{2,1,0:T(1,128)} %copy.22.refs_0_, f32[8,128]{1,0:T(8,128)} %get-tuple-element.44.refs_1_, ...), custom_call_target="tpu_custom_call" | custom-call | tf_op jit(solution)/shard_map/pallas_call | solution.py:55
  112.2 3.5 %all-to-all-start.4 = ((bf16[32,9,8,128]{3,2,1,0:T(8,128)(2,1)}), bf16[32,9,8,128]{3,2,1,0:T(8,128)(2,1)S(1)}, u32[]{:S(2)}, u32[]{:S(2)}) async-start(bf16[32,9,8,128]{3,2,1,0:T(8,128)(2,1)} %bitcast.39), calls=%async_computation.4 | async-start | bytes 1179648 | tf_op jit(solution)/shard_map/all_to_all | solution.py:19
  115.7 2.2 %collective-permute-start.7 = (bf16[16,8,128]{2,1,0:T(8,128)(2,1)S(1)}, bf16[16,8,128]{2,1,0:T(8,128)(2,1)S(1)}, u32[]{:S(2)}, u32[]{:S(2)}) collective-permute-start(bf16[16,8,128]{2,1,0:T(8,128)(2,1)S(1)} %copy-done.5), channel_id=1, source_target_pairs={{0,1},{1,2},{2,3},{4,5},{5,6},{6,7},{8,9},{9,10},{10,11},{12,13},{... | collective-permute-start | bytes 98312 | tf_op jit(solution)/shard_map/ppermute | solution.py:28
  117.9 3.5 %collective-permute-start.6 = (bf16[32,8,128]{2,1,0:T(8,128)(2,1)S(1)}, bf16[32,8,128]{2,1,0:T(8,128)(2,1)S(1)}, u32[]{:S(2)}, u32[]{:S(2)}) collective-permute-start(bf16[32,8,128]{2,1,0:T(8,128)(2,1)S(1)} %copy-done.4), channel_id=1, source_target_pairs={{0,4},{4,8},{8,12},{12,16},{16,20},{20,24},{24,28},{1,5},{5,9},{9,... | collective-permute-start | bytes 196616 | tf_op jit(solution)/shard_map/ppermute | solution.py:28
  121.5 2.2 %collective-permute-done.6.refs_9_ = bf16[32,8,128]{2,1,0:T(8,128)(2,1)S(1)} collective-permute-done((bf16[32,8,128]{2,1,0:T(8,128)(2,1)S(1)}, bf16[32,8,128]{2,1,0:T(8,128)(2,1)S(1)}, u32[]{:S(2)}, u32[]{:S(2)}) %collective-permute-start.6) | collective-permute-done | bytes 65568 | tf_op jit(solution)/shard_map/ppermute | solution.py:28
  123.7 8.8 %all-to-all-done.4 = bf16[32,9,8,128]{3,2,1,0:T(8,128)(2,1)S(1)} async-done(((bf16[32,9,8,128]{3,2,1,0:T(8,128)(2,1)}), bf16[32,9,8,128]{3,2,1,0:T(8,128)(2,1)S(1)}, u32[]{:S(2)}, u32[]{:S(2)}) %all-to-all-start.4) | async-done | bytes 589856 | tf_op jit(solution)/shard_map/all_to_all | solution.py:19
  132.5 10.9 %shard_map.109 = (bf16[256,8,128]{2,1,0:T(8,128)(2,1)}, f32[8,128]{1,0:T(8,128)}, bf16[32,8,128]{2,1,0:T(8,128)(2,1)}, bf16[32,8,128]{2,1,0:T(8,128)(2,1)}, bf16...) custom-call(s32[257]{0:T(512)S(1)} %pad_add_fusion.ids_ref, ...), custom_call_target="tpu_custom_call" | custom-call | tf_op jit(solution)/shard_map/pallas_call | solution.py:55
  143.4 3.7 %all-to-all-start.5 = ((bf16[32,8,8,128]{3,2,1,0:T(8,128)(2,1)}), bf16[32,8,8,128]{3,2,1,0:T(8,128)(2,1)S(1)}, u32[]{:S(2)}, u32[]{:S(2)}) async-start(bf16[32,8,8,128]{3,2,1,0:T(8,128)(2,1)} %bitcast.41), calls=%async_computation.5 | async-start | bytes 1048576 | tf_op jit(solution)/shard_map/all_to_all | solution.py:19
  147.1 1.3 collective-permute-start.8
  148.4 1.3 collective-permute-start.9
  149.7 5.9 %shard_map.110.refs_2_ = f32[8,128]{1,0:T(8,128)} custom-call(s32[1]{0:T(128)} %bitcast.base_ref._, s32[512,128]{1,0:T(8,128)} %bitcast.38, s32[512,128]{1,0:T(8,128)} %bitcast.31, f32[16,32,8,128]{3,2,1,0:T(8,128)} %get-tuple-element.55.field_ref.refs_7_, f32[16,32,8,128]{3,2,1,0:T(8,128)} %get-tuple-element.56.grad_ref.refs_8_), custom_call_target="tpu_custom_call" | custom-call | tf_op jit(solution)/shard_map/pallas_call | solution.py:55
  155.6 7.1 %all-to-all-done.5 = bf16[32,8,8,128]{3,2,1,0:T(8,128)(2,1)S(1)} async-done(((bf16[32,8,8,128]{3,2,1,0:T(8,128)(2,1)}), bf16[32,8,8,128]{3,2,1,0:T(8,128)(2,1)S(1)}, u32[]{:S(2)}, u32[]{:S(2)}) %all-to-all-start.5) | async-done | bytes 524320 | tf_op jit(solution)/shard_map/all_to_all | solution.py:19
  162.7 8.2 %shard_map.111 = (f32[4,8,512]{2,1,0:T(8,128)}, f32[32,8,128]{2,1,0:T(8,128)}) custom-call(s32[128]{0:T(128)S(1)} %multiply_add_fusion.slot_ref, bf16[256,8,128]{2,1,0:T(8,128)(2,1)S(1)} %bitcast.22, bf16[4,512,4096]{2,1,0:T(8,128)(2,1)} %sensor_ref.5, f32[4,1,512]{2,1,0:T(1,128)} %copy.22.refs_0_, f32[8,128]{1,0:T(8,128)} %get-tuple-element.54.refs_1_, ...), custom_call_target="tpu_custom_call" | custom-call | tf_op jit(solution)/shard_map/pallas_call | solution.py:55
  170.9 3.5 %all-to-all-start.6 = ((f32[32,8,128]{2,1,0:T(8,128)}), f32[32,8,128]{2,1,0:T(8,128)S(1)}, u32[]{:S(2)}, u32[]{:S(2)}) async-start(f32[32,8,128]{2,1,0:T(8,128)} %get-tuple-element.63), calls=%async_computation.6 | async-start | bytes 262144 | tf_op jit(solution)/shard_map/all_to_all | solution.py:19
  174.4 0.6 mul.37.refs_2_
  175.0 7.6 %all-to-all-done.6.got_ref = f32[32,8,128]{2,1,0:T(8,128)S(1)} async-done(((f32[32,8,128]{2,1,0:T(8,128)}), f32[32,8,128]{2,1,0:T(8,128)S(1)}, u32[]{:S(2)}, u32[]{:S(2)}) %all-to-all-start.6) | async-done | bytes 131104 | tf_op jit(solution)/shard_map/all_to_all | solution.py:19
  182.6 3.9 %shard_map.112 = (f32[16,32,8,128]{3,2,1,0:T(8,128)}, f32[4,8,512]{2,1,0:T(8,128)}) custom-call(s32[1]{0:T(128)} %bitcast.base_ref._, f32[32,8,128]{2,1,0:T(8,128)S(1)} %all-to-all-done.6.got_ref, f32[8,128]{1,0:T(8,128)} %broadcast_in_dim.16.refs_2_.refs_0_, f32[8,128]{1,0:T(8,128)} %get-tuple-element.64.refs_1_, f32[4,1,512]{2,1,0:T(1,128)} %mul.37.refs_2_, ...), custom_call_target="tpu_custom_call" | custom-call | tf_op jit(solution)/shard_map/pallas_call | solution.py:55
  (42 shorter events, 0.3 us)
Async XLA Ops:
  2.7 14.5 %all-to-all-start = ((s32[32,1,8]{2,1,0:T(1,128)}), s32[32,1,8]{2,1,0:T(1,128)S(1)}, u32[]{:S(2)}, u32[]{:S(2)}) async-start(s32[32,1,8]{2,1,0:T(1,128)} %bitcast.1), calls=%async_computation | async-start | bytes 32768 | tf_op jit(solution)/shard_map/all_to_all | solution.py:19
  10.0 11.6 %copy-start.6 = (f32[4,512]{1,0:T(4,128)S(1)}, f32[4,512]{1,0:T(4,128)}, u32[]{:S(2)}) copy-start(f32[4,512]{1,0:T(4,128)} %param.11) | copy-start | bytes 24580
  10.0 11.6 %copy-start.7 = (s32[4]{0:T(128)S(1)}, s32[4]{0:T(128)}, u32[]{:S(2)}) copy-start(s32[4]{0:T(128)} %param.12) | copy-start | bytes 52
  18.9 18.4 %all-to-all-start.1 = ((bf16[32,8,8,128]{3,2,1,0:T(8,128)(2,1)}), bf16[32,8,8,128]{3,2,1,0:T(8,128)(2,1)S(1)}, u32[]{:S(2)}, u32[]{:S(2)}) async-start(bf16[32,8,8,128]{3,2,1,0:T(8,128)(2,1)} %bitcast.4), calls=%async_computation.1 | async-start | bytes 1048576 | tf_op jit(solution)/shard_map/all_to_all | solution.py:19
  37.2 14.0 %copy-start.10 = (f32[32,8,128]{2,1,0:T(8,128)S(1)}, f32[32,8,128]{2,1,0:T(8,128)}, u32[]{:S(2)}) copy-start(f32[32,8,128]{2,1,0:T(8,128)} %get-tuple-element.37) | copy-start | bytes 393220
  37.2 15.3 %copy-start.9 = (f32[32,8,128]{2,1,0:T(8,128)S(1)}, f32[32,8,128]{2,1,0:T(8,128)}, u32[]{:S(2)}) copy-start(f32[32,8,128]{2,1,0:T(8,128)} %get-tuple-element.39) | copy-start | bytes 393220
  37.2 19.8 %copy-start.12 = (f32[16,8,128]{2,1,0:T(8,128)S(1)}, f32[16,8,128]{2,1,0:T(8,128)}, u32[]{:S(2)}) copy-start(f32[16,8,128]{2,1,0:T(8,128)} %get-tuple-element.38) | copy-start | bytes 196612
  37.2 21.1 %copy-start.11 = (f32[16,8,128]{2,1,0:T(8,128)S(1)}, f32[16,8,128]{2,1,0:T(8,128)}, u32[]{:S(2)}) copy-start(f32[16,8,128]{2,1,0:T(8,128)} %get-tuple-element.40) | copy-start | bytes 196612
  37.2 27.4 %copy-start.8 = (f32[8]{0:T(128)S(1)}, f32[8]{0:T(128)}, u32[]{:S(2)}) copy-start(f32[8]{0:T(128)} %param.17) | copy-start | bytes 100
  48.2 24.6 %all-to-all-start.2 = ((bf16[32,8,8,128]{3,2,1,0:T(8,128)(2,1)}), bf16[32,8,8,128]{3,2,1,0:T(8,128)(2,1)S(1)}, u32[]{:S(2)}, u32[]{:S(2)}) async-start(bf16[32,8,8,128]{3,2,1,0:T(8,128)(2,1)} %bitcast.40), calls=%async_computation.2 | async-start | bytes 1048576 | tf_op jit(solution)/shard_map/all_to_all | solution.py:19
  51.2 11.6 %collective-permute-start = (f32[32,8,128]{2,1,0:T(8,128)S(1)}, f32[32,8,128]{2,1,0:T(8,128)S(1)}, u32[]{:S(2)}, u32[]{:S(2)}) collective-permute-start(f32[32,8,128]{2,1,0:T(8,128)S(1)} %copy-done.10), channel_id=1, source_target_pairs={{4,0},{8,4},{12,8},{16,12},{20,16},{24,20},{28,24},{5,1},{9,5},{13... | collective-permute-start | bytes 393224 | tf_op jit(solution)/shard_map/ppermute | solution.py:26
  52.5 12.1 %collective-permute-start.2 = (f32[32,8,128]{2,1,0:T(8,128)S(1)}, f32[32,8,128]{2,1,0:T(8,128)S(1)}, u32[]{:S(2)}, u32[]{:S(2)}) collective-permute-start(f32[32,8,128]{2,1,0:T(8,128)S(1)} %copy-done.9), channel_id=1, source_target_pairs={{0,4},{4,8},{8,12},{12,16},{16,20},{20,24},{24,28},{1,5},{5,9},{9,... | collective-permute-start | bytes 393224 | tf_op jit(solution)/shard_map/ppermute | solution.py:28
  57.1 5.7 %collective-permute-start.1 = (f32[16,8,128]{2,1,0:T(8,128)S(1)}, f32[16,8,128]{2,1,0:T(8,128)S(1)}, u32[]{:S(2)}, u32[]{:S(2)}) collective-permute-start(f32[16,8,128]{2,1,0:T(8,128)S(1)} %copy-done.12), channel_id=1, source_target_pairs={{1,0},{2,1},{3,2},{5,4},{6,5},{7,6},{9,8},{10,9},{11,10},{13,12},{... | collective-permute-start | bytes 196616 | tf_op jit(solution)/shard_map/ppermute | solution.py:26
  58.4 4.4 %collective-permute-start.3 = (f32[16,8,128]{2,1,0:T(8,128)S(1)}, f32[16,8,128]{2,1,0:T(8,128)S(1)}, u32[]{:S(2)}, u32[]{:S(2)}) collective-permute-start(f32[16,8,128]{2,1,0:T(8,128)S(1)} %copy-done.11), channel_id=1, source_target_pairs={{0,1},{1,2},{2,3},{4,5},{5,6},{6,7},{8,9},{9,10},{10,11},{12,13},{... | collective-permute-start | bytes 196616 | tf_op jit(solution)/shard_map/ppermute | solution.py:28
  62.7 2.6 %copy-start.2 = (f32[16,8,128]{2,1,0:T(8,128)}, f32[16,8,128]{2,1,0:T(8,128)S(1)}, u32[]{:S(2)}) copy-start(f32[16,8,128]{2,1,0:T(8,128)S(1)} %collective-permute-done.1.refs_4_) | copy-start | bytes 196612
  62.8 2.6 %copy-start.3 = (f32[16,8,128]{2,1,0:T(8,128)}, f32[16,8,128]{2,1,0:T(8,128)S(1)}, u32[]{:S(2)}) copy-start(f32[16,8,128]{2,1,0:T(8,128)S(1)} %collective-permute-done.3.refs_6_) | copy-start | bytes 196612
  62.8 2.5 %copy-start = (f32[32,8,128]{2,1,0:T(8,128)}, f32[32,8,128]{2,1,0:T(8,128)S(1)}, u32[]{:S(2)}) copy-start(f32[32,8,128]{2,1,0:T(8,128)S(1)} %collective-permute-done.refs_3_) | copy-start | bytes 393220
  64.6 0.7 copy-start.1
  78.2 22.7 %all-to-all-start.3 = ((bf16[32,8,8,128]{3,2,1,0:T(8,128)(2,1)}), bf16[32,8,8,128]{3,2,1,0:T(8,128)(2,1)S(1)}, u32[]{:S(2)}, u32[]{:S(2)}) async-start(bf16[32,8,8,128]{3,2,1,0:T(8,128)(2,1)} %bitcast.42), calls=%async_computation.3 | async-start | bytes 1048576 | tf_op jit(solution)/shard_map/all_to_all | solution.py:19
  85.3 8.7 %collective-permute-start.4 = (bf16[32,8,128]{2,1,0:T(8,128)(2,1)}, bf16[32,8,128]{2,1,0:T(8,128)(2,1)S(1)}, u32[]{:S(2)}, u32[]{:S(2)}) collective-permute-start(bf16[32,8,128]{2,1,0:T(8,128)(2,1)} %get-tuple-element.48), channel_id=1, source_target_pairs={{4,0},{8,4},{12,8},{16,12},{20,16},{24,20},{28,24},{5,1},{9,5},{13... | collective-permute-start | bytes 196616 | tf_op jit(solution)/shard_map/ppermute | solution.py:26
  86.6 7.4 %collective-permute-start.5 = (bf16[16,8,128]{2,1,0:T(8,128)(2,1)}, bf16[16,8,128]{2,1,0:T(8,128)(2,1)S(1)}, u32[]{:S(2)}, u32[]{:S(2)}) collective-permute-start(bf16[16,8,128]{2,1,0:T(8,128)(2,1)} %get-tuple-element.51), channel_id=1, source_target_pairs={{1,0},{2,1},{3,2},{5,4},{6,5},{7,6},{9,8},{10,9},{11,10},{13,12},{... | collective-permute-start | bytes 98312 | tf_op jit(solution)/shard_map/ppermute | solution.py:26
  100.9 14.8 %copy-start.5 = (bf16[16,8,128]{2,1,0:T(8,128)(2,1)S(1)}, bf16[16,8,128]{2,1,0:T(8,128)(2,1)}, u32[]{:S(2)}) copy-start(bf16[16,8,128]{2,1,0:T(8,128)(2,1)} %get-tuple-element.50.refs_7_) | copy-start | bytes 98308
  100.9 17.0 %copy-start.4 = (bf16[32,8,128]{2,1,0:T(8,128)(2,1)S(1)}, bf16[32,8,128]{2,1,0:T(8,128)(2,1)}, u32[]{:S(2)}) copy-start(bf16[32,8,128]{2,1,0:T(8,128)(2,1)} %get-tuple-element.47.refs_4_) | copy-start | bytes 196612
  112.2 20.3 %all-to-all-start.4 = ((bf16[32,9,8,128]{3,2,1,0:T(8,128)(2,1)}), bf16[32,9,8,128]{3,2,1,0:T(8,128)(2,1)S(1)}, u32[]{:S(2)}, u32[]{:S(2)}) async-start(bf16[32,9,8,128]{3,2,1,0:T(8,128)(2,1)} %bitcast.39), calls=%async_computation.4 | async-start | bytes 1179648 | tf_op jit(solution)/shard_map/all_to_all | solution.py:19
  115.7 5.7 %collective-permute-start.7 = (bf16[16,8,128]{2,1,0:T(8,128)(2,1)S(1)}, bf16[16,8,128]{2,1,0:T(8,128)(2,1)S(1)}, u32[]{:S(2)}, u32[]{:S(2)}) collective-permute-start(bf16[16,8,128]{2,1,0:T(8,128)(2,1)S(1)} %copy-done.5), channel_id=1, source_target_pairs={{0,1},{1,2},{2,3},{4,5},{5,6},{6,7},{8,9},{9,10},{10,11},{12,13},{... | collective-permute-start | bytes 98312 | tf_op jit(solution)/shard_map/ppermute | solution.py:28
  117.9 5.8 %collective-permute-start.6 = (bf16[32,8,128]{2,1,0:T(8,128)(2,1)S(1)}, bf16[32,8,128]{2,1,0:T(8,128)(2,1)S(1)}, u32[]{:S(2)}, u32[]{:S(2)}) collective-permute-start(bf16[32,8,128]{2,1,0:T(8,128)(2,1)S(1)} %copy-done.4), channel_id=1, source_target_pairs={{0,4},{4,8},{8,12},{12,16},{16,20},{20,24},{24,28},{1,5},{5,9},{9,... | collective-permute-start | bytes 196616 | tf_op jit(solution)/shard_map/ppermute | solution.py:28
  143.4 19.3 %all-to-all-start.5 = ((bf16[32,8,8,128]{3,2,1,0:T(8,128)(2,1)}), bf16[32,8,8,128]{3,2,1,0:T(8,128)(2,1)S(1)}, u32[]{:S(2)}, u32[]{:S(2)}) async-start(bf16[32,8,8,128]{3,2,1,0:T(8,128)(2,1)} %bitcast.41), calls=%async_computation.5 | async-start | bytes 1048576 | tf_op jit(solution)/shard_map/all_to_all | solution.py:19
  147.1 8.5 %collective-permute-start.8 = (bf16[32,8,128]{2,1,0:T(8,128)(2,1)}, bf16[32,8,128]{2,1,0:T(8,128)(2,1)S(1)}, u32[]{:S(2)}, u32[]{:S(2)}) collective-permute-start(bf16[32,8,128]{2,1,0:T(8,128)(2,1)} %get-tuple-element.59), channel_id=1, source_target_pairs={{4,0},{8,4},{12,8},{16,12},{20,16},{24,20},{28,24},{5,1},{9,5},{13... | collective-permute-start | bytes 196616 | tf_op jit(solution)/shard_map/ppermute | solution.py:26
  148.4 7.2 %collective-permute-start.9 = (bf16[16,8,128]{2,1,0:T(8,128)(2,1)}, bf16[16,8,128]{2,1,0:T(8,128)(2,1)S(1)}, u32[]{:S(2)}, u32[]{:S(2)}) collective-permute-start(bf16[16,8,128]{2,1,0:T(8,128)(2,1)} %get-tuple-element.62), channel_id=1, source_target_pairs={{1,0},{2,1},{3,2},{5,4},{6,5},{7,6},{9,8},{10,9},{11,10},{13,12},{... | collective-permute-start | bytes 98312 | tf_op jit(solution)/shard_map/ppermute | solution.py:26
  170.9 11.7 %all-to-all-start.6 = ((f32[32,8,128]{2,1,0:T(8,128)}), f32[32,8,128]{2,1,0:T(8,128)S(1)}, u32[]{:S(2)}, u32[]{:S(2)}) async-start(f32[32,8,128]{2,1,0:T(8,128)} %get-tuple-element.63), calls=%async_computation.6 | async-start | bytes 262144 | tf_op jit(solution)/shard_map/all_to_all | solution.py:19
